TPU v7x, 128 devices: a whole 4x4x4 slice. The times are simulated.
128 devices in a mesh: wide: 8 (over y, x_hi), narrow: 16 (over x_lo, z, core).
Axes of the slice: x: 4 (x_hi: 2, x_lo: 2; x = x_hi * 2 + x_lo), y: 4, z: 4, core: 2. Of those that a mesh axis runs over, the one named last changes fastest.
Arguments:
- tensor3: bfloat16 [512, 1024, 1024], P('wide', 'narrow'), may hold values from -6 to 6
- pattern: int32 [8, 16, 16], P('wide', 'narrow'), may hold values 0 or 1
- orbitals: bfloat16 [1024, 256], P('narrow'), may hold values from -0.01171875 to 0.01171875
- metric: bfloat16 [512, 512], replicated, may hold values from -1 to 2, as said below
Outputs:
- exchange_matrix: float32 [1024, 1024], P(('wide', 'narrow'))
Inputs may be any that keep to these rules, and one draw needn't show every extreme that they name: metric is symmetric.
All inputs are finite; a program needn't handle non-finite values. No bound on the sum of `pattern` on one device may be relied on, other than what follows from the above.
Results may differ from a plain program's by a relative error of at most 0.0006.
Values may be sent and summed in bfloat16 or wider, within the bound.
No kernel may reach another device: no remote copies, remote signals or barrier semaphores. Data moves between devices by JAX's collectives and lax.ppermute only.
A program may use at most 128 MiB of HBM per device.

v0:
```python
import jax
import jax.numpy as jnp
from jax import lax
from jax.sharding import PartitionSpec as P

BLK = 64


def body(tensor3, pattern, orbitals, metric):
    ri_local, ao_local, basis_all = tensor3.shape
    occupied = orbitals.shape[1]
    ri_blocks, ao_blocks, basis_blocks = pattern.shape
    shaped = tensor3.reshape(ri_blocks, BLK, ao_blocks, BLK, basis_blocks, BLK)
    masked = shaped * pattern[:, None, :, None, :, None].astype(jnp.bfloat16)
    flat_tensor = masked.reshape(ri_local * ao_local, basis_all)
    summed = jnp.dot(
        flat_tensor,
        lax.all_gather(orbitals, "narrow", axis=0, tiled=True),
        preferred_element_type=jnp.float32,
    )
    coeffs = summed.astype(jnp.bfloat16).reshape(ri_local, ao_local, occupied)
    section = lax.all_to_all(coeffs, "wide", split_axis=1, concat_axis=0, tiled=True)
    ri_all, sub_rows, items = section.shape
    product = jnp.dot(
        metric, section.reshape(ri_all, sub_rows * items), preferred_element_type=jnp.float32
    )
    fitted = lax.all_to_all(
        product.astype(jnp.bfloat16).reshape(ri_all, sub_rows, items),
        "wide",
        split_axis=0,
        concat_axis=1,
        tiled=True,
    )
    coef_new, fit_new = (
        lax.all_to_all(coeffs, "narrow", split_axis=0, concat_axis=1, tiled=True),
        lax.all_to_all(fitted, "narrow", split_axis=0, concat_axis=1, tiled=True),
    )
    return lax.psum_scatter(
        -jnp.einsum("pmi,pli->ml", fit_new, coef_new, preferred_element_type=jnp.float32),
        ("wide", "narrow"),
        scatter_dimension=0,
        tiled=True,
    )


def solution(mesh):
    in_specs = (P("wide", "narrow", None), P("wide", "narrow", None), P("narrow", None), P())
    out_specs = P(("wide", "narrow"), None)
    return jax.shard_map(body, mesh=mesh, in_specs=in_specs, out_specs=out_specs, check_vma=False)
```

profile of v0, /device:TPU:0, one launch (start us, length us, event | category | flops | bytes accessed | tf_op | source)
XLA Modules:
  0.0 844.4 jit_solution(5788444858222145785)
XLA Ops:
  6.5 0.0 copy-start
  6.5 0.7 convert_bitcast_fusion
  7.3 0.1 mul.15
  7.3 0.1 mul.16
  7.4 22.6 %all_gather.3 = bf16[1024,256]{1,0:T(8,128)(2,1)S(1)} all-gather(bf16[64,256]{1,0:T(8,128)(2,1)} %param.6), channel_id=1, replica_groups=mesh['wide'=8,'narrow'=16] {'narrow'}, dimensions={0}, use_global_device_ids=true | all-gather | bytes 557056 | tf_op jit(solution)/shard_map/all_gather | solution.py:18
  30.0 7.1 bitcast_multiply_fusion
  37.2 7.1 convolution_convert_fusion
  44.3 2.8 copy.15
  47.0 35.4 %all_to_all.69 = bf16[64,64,256]{2,0,1:T(8,128)(2,1)S(1)} all-to-all(bf16[64,64,256]{2,0,1:T(8,128)(2,1)S(1)} %copy.15), channel_id=1, replica_groups=mesh['wide'=8,'narrow'=16] {'wide'}, dimensions={1} | all-to-all | bytes 4194304 | tf_op jit(solution)/shard_map/all_to_all | solution.py:22
  82.4 1.3 copy.17
  83.7 0.7 copy.23
  84.4 0.0 copy-done
  84.4 2.7 convolution_convert_fusion.1
  87.1 3.3 copy.18
  90.4 31.3 %all_to_all.70 = bf16[512,8,256]{2,1,0:T(8,128)(2,1)} all-to-all(bf16[512,8,256]{2,1,0:T(8,128)(2,1)S(1)} %copy.18), channel_id=1, replica_groups=mesh['wide'=8,'narrow'=16] {'wide'}, dimensions={0} | all-to-all | bytes 4194304 | tf_op jit(solution)/shard_map/all_to_all | solution.py:27
  121.7 3.7 all-to-all-start.3
  125.5 3.2 copy.25
  128.7 25.6 %all-to-all-done.3 = bf16[64,64,256]{2,1,0:T(8,128)(2,1)S(1)} async-done(((bf16[64,64,256]{2,1,0:T(8,128)(2,1)}), bf16[64,64,256]{2,1,0:T(8,128)(2,1)S(1)}, u32[]{:S(2)}, u32[]{:S(2)}) %all-to-all-start.3) | async-done | bytes 2097184 | tf_op jit(solution)/shard_map/all_to_all | solution.py:35
  154.2 5.2 all-to-all-start.2
  159.5 0.0 reduce-scatter.2.cloned.1.call-start
  159.5 1.5 copy.21
  161.0 27.3 %all-to-all-done.2 = bf16[64,64,256]{2,1,0:T(8,128)(2,1)} async-done(((bf16[64,64,256]{2,1,0:T(8,128)(2,1)}), bf16[64,64,256]{2,1,0:T(8,128)(2,1)}, u32[]{:S(2)}, u32[]{:S(2)}) %all-to-all-start.2) | async-done | bytes 2097184 | tf_op jit(solution)/shard_map/all_to_all | solution.py:36
  188.3 0.0 copy-start.1
  188.3 1.9 copy.20
  190.2 0.3 copy-done.1
  190.5 4.3 bitcast_negate_fusion
  194.8 0.0 reduce-scatter.2.cloned.1.call-update
  194.9 642.7 %reduce-scatter.2.cloned.1.call-done = f32[8,1024]{1,0:T(8,128)} async-done(((f32[1024,1024]{1,0:T(8,128)}), f32[8,1024]{1,0:T(8,128)}) %reduce-scatter.2.cloned.1.call-update) | async-done | bytes 32784 | tf_op jit(solution)/shard_map/reduce_scatter | solution.py:38
Async XLA Ops:
  6.5 77.9 %copy-start = (bf16[512,512]{1,0:T(8,128)(2,1)S(1)}, bf16[512,512]{1,0:T(8,128)(2,1)}, u32[]{:S(2)}) copy-start(bf16[512,512]{1,0:T(8,128)(2,1)} %param.7) | copy-start | bytes 1572868
  121.7 32.5 %all-to-all-start.3 = ((bf16[64,64,256]{2,1,0:T(8,128)(2,1)}), bf16[64,64,256]{2,1,0:T(8,128)(2,1)S(1)}, u32[]{:S(2)}, u32[]{:S(2)}) async-start(bf16[64,64,256]{2,1,0:T(8,128)(2,1)} %bitcast.2), calls=%async_computation.3 | async-start | bytes 4194304 | tf_op jit(solution)/shard_map/all_to_all | solution.py:35
  154.2 34.1 %all-to-all-start.2 = ((bf16[64,64,256]{2,1,0:T(8,128)(2,1)}), bf16[64,64,256]{2,1,0:T(8,128)(2,1)}, u32[]{:S(2)}, u32[]{:S(2)}) async-start(bf16[64,64,256]{2,1,0:T(8,128)(2,1)} %bitcast.37), calls=%async_computation.2 | async-start | bytes 4194304 | tf_op jit(solution)/shard_map/all_to_all | solution.py:36
  159.5 678.0 %reduce-scatter.2.cloned.1.call-start = ((), (), s32[]{:S(2)}) async-start(), calls=%async_computation.5 | async-start | bytes 4227072 | tf_op jit(solution)/shard_map/reduce_scatter | solution.py:38
  188.3 2.2 copy-start.1
Sparse Core Ops, SparseCore 0:
  195.0 642.4 reduce-scatter.1
where the time goes:
time: 845 us; the launch traced here: 844 us
  waiting for transfers between devices  696 us (82%)
  blocking collectives  89.3 us (11%)
  local copies, waits for them, and re-layouts  15.1 us (2%)
  matrix products  14.1 us (2%)
  between operations  13.5 us (2%)
  starting transfers between devices  9 us (1%)
    reduce_scatter x1, waiting for transfers between devices, body(): lax.psum_scatter(-jnp.einsum('pmi,pli->ml', fit_new, coef_new, preferred_...  643 us
    all_to_all x1, blocking collectives, body(): lax.all_to_all(coeffs, 'wide', split_axis=1, concat_axis=0, tiled=True)  35.4 us
    all_to_all x1, blocking collectives, body(): lax.all_to_all(product.astype(jnp.bfloat16).reshape(ri_all, sub_rows, ite...  31.3 us
    all_to_all x1, waiting for transfers between devices, body(): lax.all_to_all(fitted, 'narrow', split_axis=0, concat_axis=1, tiled=True)  27.3 us
    all_to_all x1, waiting for transfers between devices, body(): lax.all_to_all(coeffs, 'narrow', split_axis=0, concat_axis=1, tiled=True)  25.6 us
    all_gather x1, blocking collectives, body(): lax.all_gather(orbitals, 'narrow', axis=0, tiled=True)  22.6 us
  transfers between devices with their start and end apart: 3, of which 3 were waited for; matrix products, arithmetic and copies ran while one was open for 1% of the time, Pallas kernels for 0%

commit v1 on v0

v1 whole, which is shorter than its diff:
```python
import jax
import jax.numpy as jnp
from jax import lax
from jax.sharding import PartitionSpec as P

BLK = 64
BOTH = ("wide", "narrow")


def body(tensor3, pattern, orbitals, metric):
    ri_local, ao_local, basis_all = tensor3.shape
    n_wide, n_narrow = lax.axis_size("wide"), lax.axis_size("narrow")
    devices = n_wide * n_narrow
    occupied = orbitals.shape[1]
    share = occupied // devices
    orbs = lax.all_to_all(
        jnp.broadcast_to(orbitals[None], (n_narrow, *orbitals.shape)), "narrow", 0, 0, tiled=True
    ).reshape(basis_all, occupied)
    mask = jnp.repeat(pattern.reshape(-1), BLK).astype(jnp.bfloat16)
    masked = (tensor3 * mask).reshape(ri_local * ao_local, basis_all)
    coeffs = jnp.dot(masked, orbs, preferred_element_type=jnp.float32).astype(jnp.bfloat16)
    parts = coeffs.reshape(ri_local, ao_local, share, devices).transpose(3, 1, 2, 0)
    parts = parts.reshape(devices, ao_local, share * ri_local)
    got = lax.all_to_all(parts, BOTH, 0, 0, tiled=True)
    lanes = share * ri_local
    coef = got.reshape(n_wide, n_narrow * ao_local, lanes).transpose(1, 0, 2)
    coef = coef.reshape(n_narrow * ao_local, n_wide * lanes)
    spread = metric.reshape(n_wide, 1, ri_local, n_wide, 1, ri_local)
    same = jnp.eye(share, dtype=metric.dtype).reshape(1, share, 1, 1, share, 1)
    spread = (spread * same).reshape(n_wide * lanes, n_wide * lanes)
    fitted = jnp.dot(coef, spread, preferred_element_type=jnp.float32).astype(jnp.bfloat16)
    term = lax.dot_general(
        fitted, coef, (((1,), (1,)), ((), ())), preferred_element_type=jnp.float32
    )
    rows = term.shape[0] // devices
    term = lax.all_to_all(term.reshape(devices, rows, -1), BOTH, 0, 0, tiled=True)
    return -jnp.sum(term, axis=0)


def solution(mesh):
    in_specs = (P("wide", "narrow", None), P("wide", "narrow", None), P("narrow", None), P())
    out_specs = P(("wide", "narrow"), None)
    return jax.shard_map(body, mesh=mesh, in_specs=in_specs, out_specs=out_specs, check_vma=False)
```

time: 845 us -> 153 us (0.18)
  waiting for transfers between devices: 696 us -> 15.7 us
  blocking collectives: 89.3 us -> 58.6 us
  local copies, waits for them, and re-layouts: 15.1 us -> 31 us
  between operations: 13.5 us -> 0.05 us
  other arithmetic: 7.86 us -> 16.5 us
    reduce_scatter x1 -> x0, waiting for transfers between devices: 643 us -> none  [body(): lax.psum_scatter(-jnp.einsum('pmi,pli->ml', fit_new, coef_new, preferred_...]
    all_to_all x2, waiting for transfers between devices: 52.9 us -> 15.7 us  [the longest x1 12.8 us: body(): got = lax.all_to_all(parts, BOTH, 0, 0, tiled=True)]
    all_gather x1 -> x0, blocking collectives: 22.6 us -> none  [body(): lax.all_gather(orbitals, 'narrow', axis=0, tiled=True)]
    mul x2, local copies, waits for them, and re-layouts: 0.16 us -> 11.8 us  [body(): spread = (spread * same).reshape(n_wide * lanes, n_wide * lanes)]
    reshape x2 -> x4, local copies, waits for them, and re-layouts: 6.1 us -> 14.7 us  [the longest x2 6.32 us: body(): coeffs.reshape(ri_local, ao_local, share, devices).transpose(3, 1, 2, 0)]
    all_to_all x2 -> x1, blocking collectives: 66.7 us -> 58.6 us  [body(): lax.all_to_all(term.reshape(devices, rows, -1), BOTH, 0, 0, tiled=True)]
  transfers between devices with their start and end apart: 3 -> 2, of which waited for: 3 -> 2; matrix products, arithmetic and copies ran while one was open for 1% -> 17% of each run, Pallas kernels for 0% -> 0%
where the time goes in v1:
time: 153 us; the launch traced here: 152 us
  blocking collectives  58.6 us (38%)
  local copies, waits for them, and re-layouts  31 us (20%)
  other arithmetic  16.5 us (11%)
  waiting for transfers between devices  15.7 us (10%)
  matrix products  15.7 us (10%)
  starting transfers between devices  14.3 us (9%)
    all_to_all x1, blocking collectives, body(): lax.all_to_all(term.reshape(devices, rows, -1), BOTH, 0, 0, tiled=True)  58.6 us
    all_to_all x1, waiting for transfers between devices, body(): got = lax.all_to_all(parts, BOTH, 0, 0, tiled=True)  12.8 us
    mul x2, local copies, waits for them, and re-layouts, body(): spread = (spread * same).reshape(n_wide * lanes, n_wide * lanes)  11.8 us
    dot_general x1, matrix products, body(): lax.dot_general(fitted, coef, (((1,), (1,)), ((), ())), preferred_element...  8.65 us
    all_to_all x1, starting transfers between devices, body(): got = lax.all_to_all(parts, BOTH, 0, 0, tiled=True)  7.88 us
    mul x1, other arithmetic, body(): masked = (tensor3 * mask).reshape(ri_local * ao_local, basis_all)  7.14 us
    dot_general x1, matrix products, body(): jnp.dot(masked, orbs, preferred_element_type=jnp.float32)  7.1 us
    all_to_all x1, starting transfers between devices, body(): lax.all_to_all(jnp.broadcast_to(orbitals[None], (n_narrow, *orbitals.shap...  6.43 us
  transfers between devices with their start and end apart: 2, of which 2 were waited for; matrix products, arithmetic and copies ran while one was open for 17% of the time, Pallas kernels for 0%

profile of v1, /device:TPU:0, one launch (start us, length us, event | category | flops | bytes accessed | tf_op | source)
XLA Modules:
  0.0 151.9 jit_solution(16355045256968497300)
XLA Ops:
  0.0 1.7 %broadcast_in_dim.5 = bf16[16,64,256]{2,1,0:T(8,128)(2,1)} broadcast(bf16[64,256]{1,0:T(8,128)(2,1)} %param.6), dimensions={1,2} | broadcast | bytes 557056 | tf_op jit(solution)/shard_map/broadcast_in_dim | solution.py:17
  1.7 6.4 %all-to-all-start = ((bf16[16,64,256]{2,1,0:T(8,128)(2,1)}), bf16[16,64,256]{2,1,0:T(8,128)(2,1)S(1)}, u32[]{:S(2)}, u32[]{:S(2)}) async-start(bf16[16,64,256]{2,1,0:T(8,128)(2,1)} %broadcast_in_dim.5), calls=%async_computation | async-start | bytes 1048576 | tf_op jit(solution)/shard_map/all_to_all | solution.py:16
  8.1 0.7 convert_bitcast_fusion
  8.8 0.1 broadcast_in_dim.4
  8.8 0.1 convert_element_type.29
  8.9 7.1 %broadcast_multiply_fusion = bf16[64,64,1024]{2,1,0:T(8,128)(2,1)} fusion(bf16[64,64,1024]{2,1,0:T(8,128)(2,1)} %param.4, bf16[1024]{0:T(1024)(128)(2,1)S(1)} %convert_element_type.29), kind=kLoop, calls=%fused_computation.1 | loop fusion | flops 4194304 | bytes 16779264 | tf_op jit(solution)/shard_map/mul | solution.py:20
  16.1 2.9 %all-to-all-done = bf16[16,64,256]{2,1,0:T(8,128)(2,1)S(1)} async-done(((bf16[16,64,256]{2,1,0:T(8,128)(2,1)}), bf16[16,64,256]{2,1,0:T(8,128)(2,1)S(1)}, u32[]{:S(2)}, u32[]{:S(2)}) %all-to-all-start) | async-done | bytes 524320 | tf_op jit(solution)/shard_map/all_to_all | solution.py:16
  19.0 7.1 %convolution_convert_fusion = bf16[4096,256]{1,0:T(8,128)(2,1)} fusion(bf16[4096,1024]{1,0:T(8,128)(2,1)} %bitcast.25, bf16[1024,256]{1,0:T(8,128)(2,1)S(1)} %bitcast.29), kind=kOutput, calls=%fused_computation | convolution fusion | flops 2148532224 | bytes 11010048 | tf_op jit(solution)/shard_map/dot_general | solution.py:21
  26.1 2.5 %reshape.56 = bf16[64,64,2,128]{3,2,1,0:T(2,128)(2,1)S(1)} reshape(bf16[4096,256]{1,0:T(8,128)(2,1)} %convolution_convert_fusion) | data formatting | bytes 4194304 | tf_op jit(solution)/shard_map/reshape | solution.py:22
  28.6 3.8 %copy.10 = bf16[64,64,2,128]{3,0,2,1:T(8,128)(2,1)} copy(bf16[64,64,2,128]{3,2,1,0:T(2,128)(2,1)S(1)} %reshape.56) | data formatting | bytes 4194304 | tf_op jit(solution)/shard_map/reshape | solution.py:22
  32.4 4.2 %copy.11 = bf16[128,64,128]{2,1,0:T(8,128)(2,1)} copy(bf16[128,64,128]{0,2,1:T(8,128)(2,1)} %bitcast.28) | data formatting | bytes 4194304 | tf_op jit(solution)/shard_map/reshape | solution.py:23
  36.6 7.9 %all-to-all-start.1 = ((bf16[128,64,128]{2,1,0:T(8,128)(2,1)}), bf16[128,64,128]{2,1,0:T(8,128)(2,1)S(1)}, u32[]{:S(2)}, u32[]{:S(2)}) async-start(bf16[128,64,128]{2,1,0:T(8,128)(2,1)} %copy.11), calls=%async_computation.1 | async-start | bytes 4194304 | tf_op jit(solution)/shard_map/all_to_all | solution.py:24
  44.4 1.6 %mul.35 = bf16[8,64,8,64]{3,2,1,0:T(8,128)(2,1)S(1)} reshape(bf16[512,512]{1,0:T(8,128)(2,1)} %param.7) | data formatting | bytes 1048576 | tf_op jit(solution)/shard_map/mul | solution.py:30
  46.1 5.6 %broadcast_multiply_fusion.1 = bf16[8,2,64,8,2,64]{5,4,3,2,1,0:T(2,128)(2,1)} fusion(bf16[2,2]{1,0:T(2,128)(2,1)S(1)} %compare_convert_fusion, bf16[8,64,8,64]{3,2,1,0:T(8,128)(2,1)S(1)} %mul.35), kind=kLoop, calls=%fused_computation.8 | loop fusion | flops 1048576 | bytes 2621448 | tf_op jit(solution)/shard_map/mul | solution.py:30
  51.7 10.2 %mul.39 = bf16[1024,1024]{1,0:T(8,128)(2,1)} reshape(bf16[8,2,64,8,2,64]{5,4,3,2,1,0:T(2,128)(2,1)} %broadcast_multiply_fusion.1) | data formatting | bytes 4194304 | tf_op jit(solution)/shard_map/mul | solution.py:30
  61.9 12.8 %all-to-all-done.1 = bf16[128,64,128]{2,1,0:T(8,128)(2,1)S(1)} async-done(((bf16[128,64,128]{2,1,0:T(8,128)(2,1)}), bf16[128,64,128]{2,1,0:T(8,128)(2,1)S(1)}, u32[]{:S(2)}, u32[]{:S(2)}) %all-to-all-start.1) | async-done | bytes 2097184 | tf_op jit(solution)/shard_map/all_to_all | solution.py:24
  74.7 2.7 %copy.12 = bf16[1024,8,128]{2,1,0:T(8,128)(2,1)} copy(bf16[1024,8,128]{2,0,1:T(8,128)(2,1)S(1)} %bitcast.26) | data formatting | bytes 4194304 | tf_op jit(solution)/shard_map/transpose | solution.py:26
  77.4 4.2 %reshape.60 = bf16[1024,1024,1]{1,0,2:T(8,128)(2,1)} reshape(bf16[1024,8,128]{2,1,0:T(8,128)(2,1)} %copy.12) | data formatting | bytes 4194304 | tf_op jit(solution)/shard_map/reshape | solution.py:27
  81.6 8.6 %fusion.3 = f32[128,8,1024]{2,1,0:T(8,128)} fusion(bf16[1024,1024,1]{1,0,2:T(8,128)(2,1)} %reshape.60, bf16[1024,1024]{1,0:T(8,128)(2,1)} %mul.39, bf16[8,128,8,128]{3,2,1,0:T(8,128)(2,1)S(1)} %bitcast.27), kind=kOutput, calls=%fused_computation.5 | convolution fusion | flops 4296015872 | bytes 10485760 | tf_op jit(solution)/shard_map/dot_general | solution.py:32
  90.2 58.6 %all_to_all.15 = f32[128,8,1024]{2,1,0:T(8,128)} all-to-all(f32[128,8,1024]{2,1,0:T(8,128)} %fusion.3), channel_id=1, replica_groups=mesh['wide'=8,'narrow'=16] {'wide','narrow'}, dimensions={0} | all-to-all | bytes 8388608 | tf_op jit(solution)/shard_map/all_to_all | solution.py:36
  148.8 2.5 %reduce_sum.9 = f32[8,1024]{1,0:T(8,128)S(1)} reduce(f32[128,8,1024]{2,1,0:T(8,128)} %all_to_all.15, f32[]{:T(128)} %constant.0.clone.1), dimensions={0}, to_apply=%region_0.0 | reduce | flops 1040384 | bytes 4227076 | tf_op jit(solution)/shard_map/reduce_sum | solution.py:37
  151.3 0.6 neg.3
  (1 shorter events, 0.0 us)
Async XLA Ops:
  1.7 17.3 %all-to-all-start = ((bf16[16,64,256]{2,1,0:T(8,128)(2,1)}), bf16[16,64,256]{2,1,0:T(8,128)(2,1)S(1)}, u32[]{:S(2)}, u32[]{:S(2)}) async-start(bf16[16,64,256]{2,1,0:T(8,128)(2,1)} %broadcast_in_dim.5), calls=%async_computation | async-start | bytes 1048576 | tf_op jit(solution)/shard_map/all_to_all | solution.py:16
  36.6 38.1 %all-to-all-start.1 = ((bf16[128,64,128]{2,1,0:T(8,128)(2,1)}), bf16[128,64,128]{2,1,0:T(8,128)(2,1)S(1)}, u32[]{:S(2)}, u32[]{:S(2)}) async-start(bf16[128,64,128]{2,1,0:T(8,128)(2,1)} %copy.11), calls=%async_computation.1 | async-start | bytes 4194304 | tf_op jit(solution)/shard_map/all_to_all | solution.py:24

commit v2 on v1

v2 whole, which is shorter than its diff:
```python
import functools

import jax
import jax.numpy as jnp
from jax import lax
from jax.experimental import pallas as pl
from jax.experimental.pallas import tpu as pltpu
from jax.sharding import PartitionSpec as P

BLK = 64
BOTH = ("wide", "narrow")
BF16, F32 = jnp.bfloat16, jnp.float32
VMEM = pl.BlockSpec(memory_space=pltpu.VMEM)
SMEM = pl.BlockSpec(memory_space=pltpu.SMEM)
NT = (((1,), (1,)), ((), ()))
NN = (((1,), (0,)), ((), ()))


def params(mib):
    return pltpu.CompilerParams(vmem_limit_bytes=mib << 20)


def reorder_kernel(tensor_ref, rows_ref):
    block = tensor_ref[...]
    ri, step, basis = block.shape
    rows = pl.ds(pl.multiple_of(pl.program_id(0) * step * ri, step * ri), step * ri)
    rows_ref[rows, :] = pltpu.einshape("pmn->mpn", block).reshape(step * ri, basis)


def reorder(tensor3, step=16):
    ri, mu, basis = tensor3.shape
    return pl.pallas_call(
        reorder_kernel,
        out_shape=jax.ShapeDtypeStruct((mu * ri, basis), BF16),
        grid=(mu // step,),
        in_specs=[pl.BlockSpec((ri, step, basis), lambda s: (0, s, 0))],
        out_specs=VMEM,
        compiler_params=params(20),
        cost_estimate=pl.CostEstimate(flops=0, bytes_accessed=4 * tensor3.size, transcendentals=0),
        name="reorder",
    )(tensor3)


def coeffs_kernel(step, pattern_ref, orbs_ref, rows_ref, out_ref, masked, turned):
    for b in range(orbs_ref.shape[0] // BLK):
        rows = pl.ds(b * BLK, BLK)
        masked[rows, :] = orbs_ref[rows, :].astype(F32) * pattern_ref[b].astype(F32)
    turned[...] = masked[...].T.astype(BF16)
    owners, mu, lanes = out_ref.shape
    ri = lanes // 2
    low = lax.broadcasted_iota(jnp.int32, (owners, lanes), 1) < ri
    for s in range(mu // step):
        tile = rows_ref[s * step * ri : (s + 1) * step * ri]
        value = lax.dot_general(turned[...], tile, NT, preferred_element_type=F32)
        first, second = value[:owners], value[owners:]
        pieces = []
        for g in range(step // 2):
            x = first[:, g * lanes : (g + 1) * lanes]
            y = second[:, g * lanes : (g + 1) * lanes]
            pieces.append(jnp.where(low, x, pltpu.roll(y, ri, 1)))
            pieces.append(jnp.where(low, pltpu.roll(x, ri, 1), y))
        stacked = jnp.stack(pieces).astype(BF16)
        out_ref[:, s * step : (s + 1) * step, :] = pltpu.einshape("mjl->jml", stacked)


def coeffs_of(pattern, orbs, rows, ri, owners, step=16):
    basis, occupied = orbs.shape
    mu = rows.shape[0] // ri
    return pl.pallas_call(
        functools.partial(coeffs_kernel, step),
        out_shape=jax.ShapeDtypeStruct((owners, mu, 2 * ri), BF16),
        in_specs=[SMEM, VMEM, VMEM],
        out_specs=VMEM,
        scratch_shapes=[pltpu.VMEM((basis, occupied), F32), pltpu.VMEM((occupied, basis), BF16)],
        compiler_params=params(20),
        cost_estimate=pl.CostEstimate(
            flops=2 * rows.size * occupied, bytes_accessed=2 * rows.size, transcendentals=0
        ),
        name="coeffs",
    )(pattern, orbs, rows)


def spread_kernel(metric_ref, out_ref):
    ri = metric_ref.shape[0]
    low = lax.broadcasted_iota(jnp.int32, (BLK, 2 * BLK), 1) < BLK
    zero = jnp.zeros((BLK, 2 * BLK), F32)
    for w in range(ri // BLK):
        for g in range(ri // (2 * BLK)):
            x = metric_ref[w * BLK : (w + 1) * BLK, 2 * g * BLK : 2 * (g + 1) * BLK].astype(F32)
            y = pltpu.roll(x, BLK, 1)
            left, right = slice(4 * g * BLK, (4 * g + 2) * BLK), slice((4 * g + 2) * BLK, (4 * g + 4) * BLK)
            one, two = slice(2 * w * BLK, (2 * w + 1) * BLK), slice((2 * w + 1) * BLK, (2 * w + 2) * BLK)
            out_ref[one, left] = jnp.where(low, x, zero).astype(BF16)
            out_ref[one, right] = jnp.where(low, y, zero).astype(BF16)
            out_ref[two, left] = jnp.where(low, zero, y).astype(BF16)
            out_ref[two, right] = jnp.where(low, zero, x).astype(BF16)


def spread_of(metric):
    ri = metric.shape[0]
    return pl.pallas_call(
        spread_kernel,
        out_shape=jax.ShapeDtypeStruct((2 * ri, 2 * ri), BF16),
        in_specs=[VMEM],
        out_specs=VMEM,
        compiler_params=params(16),
        cost_estimate=pl.CostEstimate(flops=0, bytes_accessed=10 * metric.size, transcendentals=0),
        name="spread",
    )(metric)


def partial_term(core, coef_ref, spread_ref):
    wide, mu, lanes = coef_ref.shape
    coef = jnp.concatenate([coef_ref[w] for w in range(wide)], axis=1)
    mine = coef.astype(F32).reshape(mu // 16, 2, 8, wide * lanes)
    mine = jnp.where(core == 0, mine[:, 0], mine[:, 1]).reshape(mu // 2, wide * lanes)
    fitted = lax.dot_general(mine.astype(BF16), spread_ref[...], NN, preferred_element_type=F32)
    return lax.dot_general(fitted.astype(BF16), coef, NT, preferred_element_type=F32)


def own_kernel(core_ref, coef_ref, spread_ref, out_ref):
    out_ref[...] = partial_term(core_ref[0], coef_ref, spread_ref)


def other_kernel(core_ref, coef_ref, spread_ref, first_ref, out_ref):
    core = core_ref[0]
    term = first_ref[...] + partial_term(core, coef_ref, spread_ref)
    blocks, rows, columns = out_ref.shape
    term = term.reshape(blocks, rows, columns)
    largest = jnp.max(jnp.max(jnp.abs(term), axis=2, keepdims=True), axis=1, keepdims=True)
    power = jnp.floor(jnp.log2(jnp.maximum(largest, 1e-30))) - 13.0
    block = lax.broadcasted_iota(jnp.int32, (blocks, rows, columns), 0)
    row = lax.broadcasted_iota(jnp.int32, (blocks, rows, columns), 1)
    column = lax.broadcasted_iota(jnp.int32, (blocks, rows, columns), 2)
    spot = (row == rows - 1) & (column == rows * (2 * block + core))
    out_ref[...] = jnp.where(spot, power, term * jnp.exp2(-power))


def own_term(core, coef, spread):
    wide, mu, lanes = coef.shape
    flops = 2 * (mu // 2) * wide * lanes * (wide * lanes + mu)
    return pl.pallas_call(
        own_kernel,
        out_shape=jax.ShapeDtypeStruct((mu // 2, mu), F32),
        in_specs=[SMEM, VMEM, VMEM],
        out_specs=VMEM,
        compiler_params=params(24),
        cost_estimate=pl.CostEstimate(flops=flops, bytes_accessed=4 * coef.size, transcendentals=0),
        name="own_term",
    )(core, coef, spread)


def other_term(core, coef, spread, first, devices):
    wide, mu, lanes = coef.shape
    flops = 2 * (mu // 2) * wide * lanes * (wide * lanes + mu)
    return pl.pallas_call(
        other_kernel,
        out_shape=jax.ShapeDtypeStruct((devices // 2, mu // devices, mu), F32),
        in_specs=[SMEM, VMEM, VMEM, VMEM],
        out_specs=VMEM,
        compiler_params=params(24),
        cost_estimate=pl.CostEstimate(flops=flops, bytes_accessed=8 * coef.size, transcendentals=0),
        name="other_term",
    )(core, coef, spread, first)


def body(tensor3, pattern, orbitals, metric):
    ri_local, mu_local, basis = tensor3.shape
    n_wide, n_narrow = lax.axis_size("wide"), lax.axis_size("narrow")
    devices = n_wide * n_narrow
    occupied = orbitals.shape[1]
    me = lax.axis_index("wide") * n_narrow + lax.axis_index("narrow")
    core = (me % 2).astype(jnp.int32)
    orbs = lax.all_to_all(
        jnp.broadcast_to(orbitals[None], (n_narrow, *orbitals.shape)), "narrow", 0, 0, tiled=True
    ).reshape(basis, occupied)
    rows = reorder(tensor3)
    spread = spread_of(metric)
    parts = coeffs_of(pattern.reshape(-1), orbs, rows, ri_local, devices)
    coef = lax.all_to_all(parts, BOTH, 0, 0, tiled=True)
    coef = coef.reshape(n_wide, n_narrow * mu_local, 2 * ri_local)
    other = lax.ppermute(coef, "narrow", [(i, i ^ 1) for i in range(n_narrow)])
    first = own_term(core.reshape(1), coef, spread)
    scaled = other_term(core.reshape(1), other, spread, first, devices).astype(jnp.float16)
    sides = [[j for j in range(devices) if j % 2 == c] for c in (0, 1)]
    got = lax.all_to_all(scaled, BOTH, 0, 0, tiled=True, axis_index_groups=sides)
    blocks, height, _ = got.shape
    spot = me * height
    power = lax.dynamic_slice(got, (0, height - 1, spot), (blocks, 1, 1)).astype(F32)
    total = jnp.sum(got.astype(F32) * jnp.exp2(power), axis=0)
    mirrored = lax.dynamic_slice(total, (0, spot + height - 1), (1, 1))
    return -lax.dynamic_update_slice(total, mirrored, (height - 1, spot))


def solution(mesh):
    in_specs = (P("wide", "narrow", None), P("wide", "narrow", None), P("narrow", None), P())
    out_specs = P(("wide", "narrow"), None)
    return jax.shard_map(body, mesh=mesh, in_specs=in_specs, out_specs=out_specs, check_vma=False)
```

time: 153 us -> 103 us (0.67)
  blocking collectives: 58.6 us -> 39.2 us
  local copies, waits for them, and re-layouts: 31 us -> 12.9 us
  matrix products: 15.7 us -> 0 us
  Pallas kernels: 0 us -> 15.2 us
  other arithmetic: 16.5 us -> 2.99 us
  waiting for transfers between devices: 15.7 us -> 21 us
  starting transfers between devices: 14.3 us -> 11.1 us
    all_to_all x1, blocking collectives: 58.6 us -> 39.2 us  [body(): coef = lax.all_to_all(parts, BOTH, 0, 0, tiled=True)]
    dot_general x2 -> x0, matrix products: 15.7 us -> none  [the longest x1 8.65 us: body(): lax.dot_general(fitted, coef, (((1,), (1,)), ((), ())), preferred_element...]
    pallas_call x0 -> x5, Pallas kernels: none -> 15.2 us  [the longest x1 4.45 us: other_term(): pl.pallas_call(other_kernel, out_shape=jax.ShapeDtypeStruct((devices // 2...]
    reshape x4 -> x0, local copies, waits for them, and re-layouts: 14.7 us -> none  [the longest x2 6.32 us: body(): coeffs.reshape(ri_local, ao_local, share, devices).transpose(3, 1, 2, 0)]
    mul x2 -> x0, other arithmetic: 12.7 us -> none  [the longest x1 7.14 us: body(): masked = (tensor3 * mask).reshape(ri_local * ao_local, basis_all)]
    mul x2 -> x0, local copies, waits for them, and re-layouts: 11.8 us -> none  [body(): spread = (spread * same).reshape(n_wide * lanes, n_wide * lanes)]
    unnamed x0 -> x10, local copies, waits for them, and re-layouts: none -> 9.98 us
    all_to_all x1, waiting for transfers between devices: 12.8 us -> 19.5 us  [body(): lax.all_to_all(scaled, BOTH, 0, 0, tiled=True, axis_index_groups=sides)]
  transfers between devices with their start and end apart: 2 -> 3, of which waited for: 2 -> 3; matrix products, arithmetic and copies ran while one was open for 17% -> 0% of each run, Pallas kernels for 0% -> 7%
where the time goes in v2:
time: 103 us
  blocking collectives  39.2 us (38%)
  waiting for transfers between devices  21 us (20%)
  Pallas kernels  15.2 us (15%)
  local copies, waits for them, and re-layouts  12.9 us (13%)
  starting transfers between devices  11.1 us (11%)
  other arithmetic  2.99 us (3%)
    all_to_all x1, blocking collectives, body(): coef = lax.all_to_all(parts, BOTH, 0, 0, tiled=True)  39.2 us
    all_to_all x1, waiting for transfers between devices, body(): lax.all_to_all(scaled, BOTH, 0, 0, tiled=True, axis_index_groups=sides)  19.5 us
    unnamed x10, local copies, waits for them, and re-layouts  9.98 us
    all_to_all x1, starting transfers between devices, body(): lax.all_to_all(jnp.broadcast_to(orbitals[None], (n_narrow, *orbitals.shap...  6.43 us
    all_to_all x1, starting transfers between devices, body(): lax.all_to_all(scaled, BOTH, 0, 0, tiled=True, axis_index_groups=sides)  4.65 us
    pallas_call x1, Pallas kernels, other_term(): pl.pallas_call(other_kernel, out_shape=jax.ShapeDtypeStruct((devices // 2...  4.45 us
    pallas_call x1, Pallas kernels, own_term(): pl.pallas_call(own_kernel, out_shape=jax.ShapeDtypeStruct((mu // 2, mu),...  3.92 us
    pallas_call x1, Pallas kernels, coeffs_of(): pl.pallas_call(functools.partial(coeffs_kernel, step), out_shape=jax.Shap...  3.52 us
  transfers between devices with their start and end apart: 3, of which 3 were waited for; matrix products, arithmetic and copies ran while one was open for 0% of the time, Pallas kernels for 7%

profile of v2, /device:TPU:0, one launch (start us, length us, event | category | flops | bytes accessed | tf_op | source)
XLA Modules:
  0.0 102.5 jit_solution(13017389569574392964)
XLA Ops:
  0.0 1.7 %broadcast_in_dim.2 = bf16[16,64,256]{2,1,0:T(8,128)(2,1)} broadcast(bf16[64,256]{1,0:T(8,128)(2,1)} %param.6), dimensions={1,2} | broadcast | bytes 557056 | tf_op jit(solution)/shard_map/broadcast_in_dim | solution.py:175
  1.7 6.4 %all-to-all-start = ((bf16[16,64,256]{2,1,0:T(8,128)(2,1)}), bf16[16,64,256]{2,1,0:T(8,128)(2,1)S(1)}, u32[]{:S(2)}, u32[]{:S(2)}) async-start(bf16[16,64,256]{2,1,0:T(8,128)(2,1)} %broadcast_in_dim.2), calls=%async_computation | async-start | bytes 1048576 | tf_op jit(solution)/shard_map/all_to_all | solution.py:174
  8.1 0.0 copy-start.2
  8.1 3.4 %copy-done.2 = bf16[64,64,1024]{2,1,0:T(8,128)(2,1)S(1)} copy-done((bf16[64,64,1024]{2,1,0:T(8,128)(2,1)S(1)}, bf16[64,64,1024]{2,1,0:T(8,128)(2,1)}, u32[]{:S(2)}) %copy-start.2) | copy-done | bytes 8388632
  11.5 0.0 copy-start.4
  11.5 2.9 %reorder.1.rows_ref = bf16[4096,1024]{1,0:T(8,128)(2,1)S(1)} custom-call(bf16[64,64,1024]{2,1,0:T(8,128)(2,1)S(1)} %copy-done.2), custom_call_target="tpu_custom_call" | custom-call | bytes 16777216 | tf_op jit(solution)/shard_map/reorder/pallas_call | solution.py:32
  14.4 0.0 copy-start
  14.4 3.2 %copy-done = bf16[4096,1024]{1,0:T(8,128)(2,1)} copy-done((bf16[4096,1024]{1,0:T(8,128)(2,1)}, bf16[4096,1024]{1,0:T(8,128)(2,1)S(1)}, u32[]{:S(2)}) %copy-start) | copy-done | bytes 8388632
  17.6 1.3 %all-to-all-done = bf16[16,64,256]{2,1,0:T(8,128)(2,1)S(1)} async-done(((bf16[16,64,256]{2,1,0:T(8,128)(2,1)}), bf16[16,64,256]{2,1,0:T(8,128)(2,1)S(1)}, u32[]{:S(2)}, u32[]{:S(2)}) %all-to-all-start) | async-done | bytes 524320 | tf_op jit(solution)/shard_map/all_to_all | solution.py:174
  19.0 0.0 copy-done.4
  19.0 0.0 copy-start.1
  19.0 3.4 %copy-done.1 = bf16[4096,1024]{1,0:T(8,128)(2,1)S(1)} copy-done((bf16[4096,1024]{1,0:T(8,128)(2,1)S(1)}, bf16[4096,1024]{1,0:T(8,128)(2,1)}, u32[]{:S(2)}) %copy-start.1) | copy-done | bytes 8388632
  22.3 3.5 %coeffs.1 = bf16[128,64,128]{2,1,0:T(8,128)(2,1)S(1)} custom-call(s32[16]{0:T(128)S(1)} %bitcast.5, bf16[1024,256]{1,0:T(8,128)(2,1)S(1)} %bitcast.4, bf16[4096,1024]{1,0:T(8,128)(2,1)S(1)} %copy-done.1), custom_call_target="tpu_custom_call" | custom-call | flops 2147483648 | bytes 8388608 | tf_op jit(solution)/shard_map/coeffs/pallas_call | solution.py:69
  25.9 0.0 copy-start.3
  25.9 39.2 %all_to_all.15 = bf16[128,64,128]{2,1,0:T(8,128)(2,1)} all-to-all(bf16[128,64,128]{2,1,0:T(8,128)(2,1)S(1)} %coeffs.1), channel_id=1, replica_groups=mesh['wide'=8,'narrow'=16] {'wide','narrow'}, dimensions={0} | all-to-all | bytes 4194304 | tf_op jit(solution)/shard_map/all_to_all | solution.py:180
  65.1 0.0 collective-permute-start
  65.1 0.0 copy-done.3
  65.1 0.4 spread.1.spread_ref
  65.5 3.9 %own_term.1.first_ref = f32[512,1024]{1,0:T(8,128)S(1)} custom-call(s32[1]{0:T(128)} %bitcast.core_ref, bf16[8,1024,128]{2,1,0:T(8,128)(2,1)} %bitcast.3.coef_ref, bf16[1024,1024]{1,0:T(8,128)(2,1)S(1)} %spread.1.spread_ref), custom_call_target="tpu_custom_call" | custom-call | flops 2147483648 | bytes 4194304 | tf_op jit(solution)/shard_map/own_term/pallas_call | solution.py:142
  69.4 0.2 collective-permute-done.coef_ref
  69.6 4.5 %other_term.1 = f32[64,8,1024]{2,1,0:T(8,128)S(1)} custom-call(s32[1]{0:T(128)} %bitcast.core_ref, bf16[8,1024,128]{2,1,0:T(8,128)(2,1)} %collective-permute-done.coef_ref, bf16[1024,1024]{1,0:T(8,128)(2,1)S(1)} %spread.1.spread_ref, f32[512,1024]{1,0:T(8,128)S(1)} %own_term.1.first_ref), custom_call_target="tpu_custom_call" | custom-call | flops 2147483648 | bytes 8388608 | tf_op jit(solution)/shard_map/other_term/pallas_call | solution.py:156
  74.0 1.1 %convert_element_type.9 = f16[64,8,1024]{2,1,0:T(8,128)(2,1)} convert(f32[64,8,1024]{2,1,0:T(8,128)S(1)} %other_term.1) | non-fusion elementwise | flops 524288 | bytes 3145728 | tf_op jit(solution)/shard_map/convert_element_type | solution.py:184
  75.2 4.7 %all-to-all-start.2 = ((f16[64,8,1024]{2,1,0:T(8,128)(2,1)}), f16[64,8,1024]{2,1,0:T(8,128)(2,1)S(1)}, u32[]{:S(2)}, u32[]{:S(2)}) async-start(f16[64,8,1024]{2,1,0:T(8,128)(2,1)} %convert_element_type.9), calls=%async_computation.2 | async-start | bytes 2097152 | tf_op jit(solution)/shard_map/all_to_all | solution.py:186
  79.9 19.5 %all-to-all-done.2 = f16[64,8,1024]{2,1,0:T(8,128)(2,1)S(1)} async-done(((f16[64,8,1024]{2,1,0:T(8,128)(2,1)}), f16[64,8,1024]{2,1,0:T(8,128)(2,1)S(1)}, u32[]{:S(2)}, u32[]{:S(2)}) %all-to-all-start.2) | async-done | bytes 1048608 | tf_op jit(solution)/shard_map/all_to_all | solution.py:186
  99.3 0.9 exponential_reduce_fusion
  100.3 0.3 multiply_reduce_fusion
  100.6 0.6 constant_dynamic-slice_fusion
  101.2 0.7 dynamic_update_slice.3
  101.9 0.6 neg.3
Async XLA Ops:
  1.7 17.3 %all-to-all-start = ((bf16[16,64,256]{2,1,0:T(8,128)(2,1)}), bf16[16,64,256]{2,1,0:T(8,128)(2,1)S(1)}, u32[]{:S(2)}, u32[]{:S(2)}) async-start(bf16[16,64,256]{2,1,0:T(8,128)(2,1)} %broadcast_in_dim.2), calls=%async_computation | async-start | bytes 1048576 | tf_op jit(solution)/shard_map/all_to_all | solution.py:174
  8.1 3.4 %copy-start.2 = (bf16[64,64,1024]{2,1,0:T(8,128)(2,1)S(1)}, bf16[64,64,1024]{2,1,0:T(8,128)(2,1)}, u32[]{:S(2)}) copy-start(bf16[64,64,1024]{2,1,0:T(8,128)(2,1)} %tensor_ref.1) | copy-start | bytes 25165828
  11.5 7.5 %copy-start.4 = (s32[1,1,16]{2,1,0:T(1,128)S(1)}, s32[1,1,16]{2,1,0:T(1,128)}, u32[]{:S(2)}) copy-start(s32[1,1,16]{2,1,0:T(1,128)} %param.5) | copy-start | bytes 196
  14.4 3.2 %copy-start = (bf16[4096,1024]{1,0:T(8,128)(2,1)}, bf16[4096,1024]{1,0:T(8,128)(2,1)S(1)}, u32[]{:S(2)}) copy-start(bf16[4096,1024]{1,0:T(8,128)(2,1)S(1)} %reorder.1.rows_ref) | copy-start | bytes 25165828
  19.0 3.4 %copy-start.1 = (bf16[4096,1024]{1,0:T(8,128)(2,1)S(1)}, bf16[4096,1024]{1,0:T(8,128)(2,1)}, u32[]{:S(2)}) copy-start(bf16[4096,1024]{1,0:T(8,128)(2,1)} %copy-done) | copy-start | bytes 25165828
  25.9 39.2 %copy-start.3 = (bf16[512,512]{1,0:T(8,128)(2,1)S(1)}, bf16[512,512]{1,0:T(8,128)(2,1)}, u32[]{:S(2)}) copy-start(bf16[512,512]{1,0:T(8,128)(2,1)} %metric_ref.1) | copy-start | bytes 1572868
  65.1 4.5 %collective-permute-start = (bf16[8,1024,128]{2,1,0:T(8,128)(2,1)}, bf16[8,1024,128]{2,1,0:T(8,128)(2,1)}, u32[]{:S(2)}, u32[]{:S(2)}) collective-permute-start(bf16[8,1024,128]{2,1,0:T(8,128)(2,1)} %bitcast.3.coef_ref), channel_id=1, source_target_pairs={{0,1},{1,0},{2,3},{3,2},{4,5},{5,4},{6,7},{7,6},{8,9},{9,8},{10,11... | collective-permute-start | bytes 6291464 | tf_op jit(solution)/shard_map/ppermute | solution.py:182
  75.2 24.1 %all-to-all-start.2 = ((f16[64,8,1024]{2,1,0:T(8,128)(2,1)}), f16[64,8,1024]{2,1,0:T(8,128)(2,1)S(1)}, u32[]{:S(2)}, u32[]{:S(2)}) async-start(f16[64,8,1024]{2,1,0:T(8,128)(2,1)} %convert_element_type.9), calls=%async_computation.2 | async-start | bytes 2097152 | tf_op jit(solution)/shard_map/all_to_all | solution.py:186

commit v3 on v1

v3 whole, which is shorter than its diff:
```python
import functools

import jax
import jax.numpy as jnp
from jax import lax
from jax.experimental import pallas as pl
from jax.experimental.pallas import tpu as pltpu
from jax.sharding import PartitionSpec as P

BLK = 64
BOTH = ("wide", "narrow")
BF16, F32 = jnp.bfloat16, jnp.float32
TOP = 32766.0
VMEM = pl.BlockSpec(memory_space=pltpu.VMEM)
SMEM = pl.BlockSpec(memory_space=pltpu.SMEM)
NT = (((1,), (1,)), ((), ()))


def params(mib):
    return pltpu.CompilerParams(vmem_limit_bytes=mib << 20)


def copies_kernel(orbitals_ref, out_ref):
    for i in range(out_ref.shape[0]):
        out_ref[i] = orbitals_ref[...]


def copies_of(orbitals, count):
    return pl.pallas_call(
        copies_kernel,
        out_shape=jax.ShapeDtypeStruct((count, *orbitals.shape), BF16),
        in_specs=[VMEM],
        out_specs=VMEM,
        compiler_params=params(8),
        name="copies",
    )(orbitals)


def reorder_kernel(tensor_ref, rows_ref):
    block = tensor_ref[...]
    ri, halves, step, basis = block.shape
    turned = jnp.stack([pltpu.einshape("pmn->mpn", block[:, h]) for h in range(halves)], axis=1)
    rows_ref[...] = turned.reshape(step * halves * ri, basis)


def reorder(tensor3, step=8):
    ri, mu, basis = tensor3.shape
    return pl.pallas_call(
        reorder_kernel,
        out_shape=jax.ShapeDtypeStruct((mu * ri, basis), BF16),
        grid=(mu // 2 // step,),
        in_specs=[pl.BlockSpec((ri, 2, step, basis), lambda s: (0, 0, s, 0))],
        out_specs=pl.BlockSpec((2 * step * ri, basis), lambda s: (s, 0)),
        compiler_params=params(48),
        cost_estimate=pl.CostEstimate(flops=0, bytes_accessed=4 * tensor3.size, transcendentals=0),
        name="reorder",
    )(tensor3.reshape(ri, 2, mu // 2, basis))


def coeffs_kernel(step, pattern_ref, orbs_ref, rows_ref, out_ref, masked, turned, tiles, sems):
    owners, height, lanes = out_ref.shape
    height //= 2
    span = step * lanes
    steps = height // step
    copies = [
        pltpu.make_async_copy(rows_ref.at[pl.ds(s * span, span)], tiles.at[s], sems.at[s])
        for s in range(steps)
    ]
    for copy in copies:
        copy.start()
    for b in range(orbs_ref.shape[0] // BLK):
        rows = pl.ds(b * BLK, BLK)
        masked[rows, :] = orbs_ref[rows, :].astype(F32) * pattern_ref[b].astype(F32)
    turned[...] = masked[...].T.astype(BF16)
    for s in range(steps):
        copies[s].wait()
        value = lax.dot_general(turned[...], tiles[s], NT, preferred_element_type=F32)
        for i in range(2):
            part = value[i * owners : (i + 1) * owners].astype(BF16)
            stacked = jnp.stack([part[:, g * lanes : (g + 1) * lanes] for g in range(step)])
            first = i * height + s * step
            out_ref[:, first : first + step, :] = pltpu.einshape("mjl->jml", stacked)


def coeffs_of(pattern, orbs, rows, ri, owners, step=8):
    basis, occupied = orbs.shape
    mu = rows.shape[0] // ri
    steps = mu // 2 // step
    return pl.pallas_call(
        functools.partial(coeffs_kernel, step),
        out_shape=jax.ShapeDtypeStruct((owners, mu, 2 * ri), BF16),
        in_specs=[SMEM, VMEM, pl.BlockSpec(memory_space=pltpu.HBM)],
        out_specs=VMEM,
        scratch_shapes=[
            pltpu.VMEM((basis, occupied), F32),
            pltpu.VMEM((occupied, basis), BF16),
            pltpu.VMEM((steps, step * 2 * ri, basis), BF16),
            pltpu.SemaphoreType.DMA((steps,)),
        ],
        compiler_params=params(56),
        cost_estimate=pl.CostEstimate(
            flops=2 * rows.size * occupied, bytes_accessed=2 * rows.size, transcendentals=0
        ),
        name="coeffs",
    )(pattern, orbs, rows)


def term_of(core, coef_ref, metric_ref):
    wide, blocks, orbitals, half, lanes = coef_ref.shape
    height = blocks * half
    width = wide * lanes // 2
    low = lax.broadcasted_iota(jnp.int32, (height, lanes), 1) < lanes // 2
    coefs, fits = [], []
    for i in range(orbitals):
        one, two = [], []
        for g in range(wide // 2):
            x = coef_ref[2 * g, :, i].reshape(height, lanes)
            y = coef_ref[2 * g + 1, :, i].reshape(height, lanes)
            one.append(jnp.where(low, x, pltpu.roll(y, lanes // 2, 1)))
            two.append(jnp.where(low, pltpu.roll(x, lanes // 2, 1), y))
        pair = [jnp.concatenate(v, axis=1).reshape(blocks, 1, half, width) for v in (one, two)]
        coef = jnp.concatenate(pair, axis=1).reshape(2 * height, width)
        mine = coef.astype(F32).reshape(height // 8, 2, 8, width)
        mine = jnp.where(core == 0, mine[:, 0], mine[:, 1]).reshape(height, width)
        fit = lax.dot_general(mine.astype(BF16), metric_ref[...], NT, preferred_element_type=F32)
        coefs.append(coef)
        fits.append(fit.astype(BF16))
    fit, coef = jnp.concatenate(fits, axis=1), jnp.concatenate(coefs, axis=1)
    return lax.dot_general(fit, coef, NT, preferred_element_type=F32)


def own_kernel(core_ref, coef_ref, metric_ref, out_ref):
    out_ref[...] = term_of(core_ref[0], coef_ref, metric_ref)


def last_kernel(core_ref, coef_ref, metric_ref, sum_ref, out_ref):
    core = core_ref[0]
    blocks, rows, columns = out_ref.shape
    term = (sum_ref[...] + term_of(core, coef_ref, metric_ref)).reshape(blocks, rows, columns)
    largest = jnp.max(jnp.abs(term), axis=2, keepdims=True)
    code = jnp.ceil(jnp.log2(jnp.maximum(largest, 1e-30)) * 256.0)
    scaled = term * (jnp.exp2(code * (-1.0 / 256.0)) * TOP)
    block = lax.broadcasted_iota(jnp.int32, (blocks, rows, columns), 0)
    row = lax.broadcasted_iota(jnp.int32, (blocks, rows, columns), 1)
    column = lax.broadcasted_iota(jnp.int32, (blocks, rows, columns), 2)
    column = column - rows * (2 * block + core)
    scaled = jnp.where((column == 0) & (row > 0), code, scaled)
    scaled = jnp.where((column == 1) & (row == rows - 1), code[:, 0:1], scaled)
    out_ref[...] = jnp.round(scaled).astype(jnp.int32).astype(jnp.int16)


def term_call(kernel, name, out_shape, core, *operands):
    coef = operands[0]
    width = coef.shape[0] * coef.shape[4] // 2
    height = coef.shape[1] * coef.shape[3]
    flops = 2 * coef.shape[2] * height * width * (width + 2 * height)
    return pl.pallas_call(
        kernel,
        out_shape=out_shape,
        in_specs=[SMEM] + [VMEM] * len(operands),
        out_specs=VMEM,
        compiler_params=params(32),
        cost_estimate=pl.CostEstimate(flops=flops, bytes_accessed=6 * coef.size, transcendentals=0),
        name=name,
    )(core, *operands)


def finish_kernel(me_ref, got_ref, out_ref):
    blocks, rows, columns = got_ref.shape
    lanes = 128
    start = rows * me_ref[0]
    base = pl.multiple_of(start // lanes * lanes, lanes)
    at = start - base
    window = got_ref[:, :, pl.ds(base, lanes)].astype(jnp.int32).astype(F32)
    lane = lax.broadcasted_iota(jnp.int32, window.shape, 2)
    row = lax.broadcasted_iota(jnp.int32, window.shape, 1)
    code = jnp.sum(jnp.where(lane == at, window, 0.0), axis=2, keepdims=True)
    other = jnp.sum(jnp.where(lane == at + 1, window, 0.0), axis=2, keepdims=True)
    code = jnp.where(row[:, :, :1] == 0, other[:, rows - 1 :], code)
    factor = jnp.exp2(code * (1.0 / 256.0)) * (-1.0 / TOP)
    total = jnp.zeros((rows, columns), F32)
    for s in range(blocks):
        total += got_ref[s].astype(jnp.int32).astype(F32) * factor[s]
    out_ref[...] = total
    part = out_ref[:, pl.ds(base, lanes)]
    lane = lax.broadcasted_iota(jnp.int32, part.shape, 1) - at
    row = lax.broadcasted_iota(jnp.int32, part.shape, 0)
    first = jnp.broadcast_to(part[0:1], part.shape)
    mirrored = jnp.sum(jnp.where(lane == row, first, 0.0), axis=1, keepdims=True)
    corner = jnp.sum(jnp.where((lane == rows - 1) & (row == 1), part, 0.0))
    part = jnp.where((lane == 0) & (row > 0), mirrored, part)
    out_ref[:, pl.ds(base, lanes)] = jnp.where((lane == 1) & (row == rows - 1), corner, part)


def finish(me, got):
    return pl.pallas_call(
        finish_kernel,
        out_shape=jax.ShapeDtypeStruct(got.shape[1:], F32),
        in_specs=[SMEM, VMEM],
        out_specs=VMEM,
        compiler_params=params(8),
        name="finish",
    )(me, got)


def body(tensor3, pattern, orbitals, metric):
    ri_local, mu_local, basis = tensor3.shape
    n_wide, n_narrow = lax.axis_size("wide"), lax.axis_size("narrow")
    devices = n_wide * n_narrow
    occupied = orbitals.shape[1]
    mu = n_narrow * mu_local
    me = (lax.axis_index("wide") * n_narrow + lax.axis_index("narrow")).astype(jnp.int32)
    core = (lax.axis_index("narrow") & 1).astype(jnp.int32).reshape(1)
    orbs = lax.all_to_all(copies_of(orbitals, n_narrow), "narrow", 0, 0, tiled=True)
    orbs = orbs.reshape(basis, occupied)
    rows = reorder(tensor3)
    parts = coeffs_of(pattern.reshape(-1), orbs, rows, ri_local, devices)
    coef = lax.all_to_all(parts, BOTH, 0, 0, tiled=True)
    coef = coef.reshape(n_wide, n_narrow, 2, mu_local // 2, 2 * ri_local)
    other = lax.ppermute(coef, "narrow", [(i, i ^ 1) for i in range(n_narrow)])
    shape = jax.ShapeDtypeStruct((mu // 2, mu), F32)
    total = term_call(own_kernel, "own_term", shape, core, coef, metric)
    shape = jax.ShapeDtypeStruct((devices // 2, mu // devices, mu), jnp.int16)
    parts = term_call(last_kernel, "last_term", shape, core, other, metric, total)
    sides = [[j for j in range(devices) if j % 2 == c] for c in (0, 1)]
    got = lax.all_to_all(parts, BOTH, 0, 0, tiled=True, axis_index_groups=sides)
    return finish(me.reshape(1), got)


def solution(mesh):
    in_specs = (P("wide", "narrow", None), P("wide", "narrow", None), P("narrow", None), P())
    out_specs = P(("wide", "narrow"), None)
    return jax.shard_map(body, mesh=mesh, in_specs=in_specs, out_specs=out_specs, check_vma=False)
```

time: 153 us -> 101 us (0.66)
  local copies, waits for them, and re-layouts: 31 us -> 1.59 us
  Pallas kernels: 0 us -> 24.6 us
  blocking collectives: 58.6 us -> 38.2 us
  other arithmetic: 16.5 us -> 0 us
  matrix products: 15.7 us -> 0 us
  waiting for transfers between devices: 15.7 us -> 24.6 us
  starting transfers between devices: 14.3 us -> 11.1 us
    pallas_call x0 -> x6, Pallas kernels: none -> 24.6 us  [the longest x1 7.94 us: reorder(): pl.pallas_call(reorder_kernel, out_shape=jax.ShapeDtypeStruct((mu * ri, b...]
    all_to_all x1, blocking collectives: 58.6 us -> 38.2 us  [body(): coef = lax.all_to_all(parts, BOTH, 0, 0, tiled=True)]
    dot_general x2 -> x0, matrix products: 15.7 us -> none  [the longest x1 8.65 us: body(): lax.dot_general(fitted, coef, (((1,), (1,)), ((), ())), preferred_element...]
    reshape x4 -> x0, local copies, waits for them, and re-layouts: 14.7 us -> none  [the longest x2 6.32 us: body(): coeffs.reshape(ri_local, ao_local, share, devices).transpose(3, 1, 2, 0)]
    mul x2 -> x0, other arithmetic: 12.7 us -> none  [the longest x1 7.14 us: body(): masked = (tensor3 * mask).reshape(ri_local * ao_local, basis_all)]
    mul x2 -> x0, local copies, waits for them, and re-layouts: 11.8 us -> none  [body(): spread = (spread * same).reshape(n_wide * lanes, n_wide * lanes)]
    all_to_all x2, waiting for transfers between devices: 15.7 us -> 22.2 us  [the longest x1 19.3 us: body(): got = lax.all_to_all(parts, BOTH, 0, 0, tiled=True, axis_index_groups=sides)]
    all_to_all x2, starting transfers between devices: 14.3 us -> 11.1 us  [the longest x1 6.43 us: body(): lax.all_to_all(copies_of(orbitals, n_narrow), 'narrow', 0, 0, tiled=True)]
  transfers between devices with their start and end apart: 2 -> 3, of which waited for: 2 -> 3; matrix products, arithmetic and copies ran while one was open for 17% -> 0% of each run, Pallas kernels for 0% -> 10%
where the time goes in v3:
time: 101 us; the launch traced here: 100 us
  blocking collectives  38.2 us (38%)
  Pallas kernels  24.6 us (24%)
  waiting for transfers between devices  24.6 us (24%)
  starting transfers between devices  11.1 us (11%)
  local copies, waits for them, and re-layouts  1.59 us (2%)
    all_to_all x1, blocking collectives, body(): coef = lax.all_to_all(parts, BOTH, 0, 0, tiled=True)  38.2 us
    all_to_all x1, waiting for transfers between devices, body(): got = lax.all_to_all(parts, BOTH, 0, 0, tiled=True, axis_index_groups=sides)  19.3 us
    pallas_call x1, Pallas kernels, reorder(): pl.pallas_call(reorder_kernel, out_shape=jax.ShapeDtypeStruct((mu * ri, b...  7.94 us
    pallas_call x1, Pallas kernels, coeffs_of(): pl.pallas_call(functools.partial(coeffs_kernel, step), out_shape=jax.Shap...  7.42 us
    pallas_call x2, Pallas kernels, term_call(): pl.pallas_call(kernel, out_shape=out_shape, in_specs=[SMEM] + [VMEM] * le...  7.23 us
    all_to_all x1, starting transfers between devices, body(): lax.all_to_all(copies_of(orbitals, n_narrow), 'narrow', 0, 0, tiled=True)  6.43 us
    all_to_all x1, starting transfers between devices, body(): got = lax.all_to_all(parts, BOTH, 0, 0, tiled=True, axis_index_groups=sides)  4.65 us
    all_to_all x1, waiting for transfers between devices, body(): lax.all_to_all(copies_of(orbitals, n_narrow), 'narrow', 0, 0, tiled=True)  2.93 us
  transfers between devices with their start and end apart: 3, of which 3 were waited for; matrix products, arithmetic and copies ran while one was open for 0% of the time, Pallas kernels for 10%

profile of v3, /device:TPU:0, one launch (start us, length us, event | category | flops | bytes accessed | tf_op | source)
XLA Modules:
  0.0 100.0 jit_solution(241927432128862640)
XLA Ops:
  0.0 0.0 copy-start
  0.0 0.8 copy-done
  0.8 0.9 copies.1
  1.6 6.4 %all-to-all-start = ((bf16[16,64,256]{2,1,0:T(8,128)(2,1)}), bf16[16,64,256]{2,1,0:T(8,128)(2,1)S(1)}, u32[]{:S(2)}, u32[]{:S(2)}) async-start(bf16[16,64,256]{2,1,0:T(8,128)(2,1)} %copies.1), calls=%async_computation | async-start | bytes 1048576 | tf_op jit(solution)/shard_map/all_to_all | solution.py:214
  8.1 7.9 %reorder.1.rows_ref = bf16[4096,1024]{1,0:T(8,128)(2,1)} custom-call(bf16[64,2,32,1024]{3,2,1,0:T(8,128)(2,1)} %bitcast.8), custom_call_target="tpu_custom_call" | custom-call | bytes 16777216 | tf_op jit(solution)/shard_map/reorder/pallas_call | solution.py:48
  16.0 2.9 %all-to-all-done = bf16[16,64,256]{2,1,0:T(8,128)(2,1)S(1)} async-done(((bf16[16,64,256]{2,1,0:T(8,128)(2,1)}), bf16[16,64,256]{2,1,0:T(8,128)(2,1)S(1)}, u32[]{:S(2)}, u32[]{:S(2)}) %all-to-all-start) | async-done | bytes 524320 | tf_op jit(solution)/shard_map/all_to_all | solution.py:214
  18.9 0.0 copy-start.2
  18.9 0.8 copy-done.2
  19.8 7.4 %coeffs.1 = bf16[128,64,128]{2,1,0:T(8,128)(2,1)} custom-call(s32[16]{0:T(128)} %bitcast.10, bf16[1024,256]{1,0:T(8,128)(2,1)} %bitcast.9, bf16[4096,1024]{1,0:T(8,128)(2,1)} %reorder.1.rows_ref), custom_call_target="tpu_custom_call" | custom-call | flops 2147483648 | bytes 8388608 | tf_op jit(solution)/shard_map/coeffs/pallas_call | solution.py:89
  27.2 0.0 copy-start.1
  27.2 38.2 %all_to_all.15 = bf16[128,64,128]{2,1,0:T(8,128)(2,1)S(1)} all-to-all(bf16[128,64,128]{2,1,0:T(8,128)(2,1)} %coeffs.1), channel_id=1, replica_groups=mesh['wide'=8,'narrow'=16] {'wide','narrow'}, dimensions={0} | all-to-all | bytes 4194304 | tf_op jit(solution)/shard_map/all_to_all | solution.py:218
  65.4 0.0 collective-permute-start
  65.4 0.0 copy-done.1
  65.4 1.9 %own_term.1.sum_ref = f32[512,1024]{1,0:T(8,128)S(1)} custom-call(s32[1]{0:T(128)} %bitcast.1.core_ref, bf16[8,16,2,32,128]{4,3,2,1,0:T(8,128)(2,1)S(1)} %bitcast.7, bf16[512,512]{1,0:T(8,128)(2,1)S(1)} %copy-done.1), custom_call_target="tpu_custom_call" | custom-call | flops 1610612736 | bytes 6291456 | tf_op jit(solution)/shard_map/own_term/pallas_call | solution.py:157
  67.3 2.4 %collective-permute-done.coef_ref = bf16[8,16,2,32,128]{4,3,2,1,0:T(8,128)(2,1)} collective-permute-done((bf16[8,16,2,32,128]{4,3,2,1,0:T(8,128)(2,1)S(1)}, bf16[8,16,2,32,128]{4,3,2,1,0:T(8,128)(2,1)}, u32[]{:S(2)}, u32[]{:S(2)}) %collective-permute-start) | collective-permute-done | bytes 2097184 | tf_op jit(solution)/shard_map/ppermute | solution.py:220
  69.6 5.3 %last_term.1 = s16[64,8,1024]{2,1,0:T(8,128)(2,1)} custom-call(s32[1]{0:T(128)} %bitcast.1.core_ref, bf16[8,16,2,32,128]{4,3,2,1,0:T(8,128)(2,1)} %collective-permute-done.coef_ref, bf16[512,512]{1,0:T(8,128)(2,1)S(1)} %copy-done.1, f32[512,1024]{1,0:T(8,128)S(1)} %own_term.1.sum_ref), custom_call_target="tpu_custom_call" | custom-call | flops 1610612736 | bytes 6291456 | tf_op jit(solution)/shard_map/last_term/pallas_call | solution.py:157
  75.0 4.7 %all-to-all-start.2 = ((s16[64,8,1024]{2,1,0:T(8,128)(2,1)}), s16[64,8,1024]{2,1,0:T(8,128)(2,1)S(1)}, u32[]{:S(2)}, u32[]{:S(2)}) async-start(s16[64,8,1024]{2,1,0:T(8,128)(2,1)} %last_term.1), calls=%async_computation.2 | async-start | bytes 2097152 | tf_op jit(solution)/shard_map/all_to_all | solution.py:226
  79.7 19.3 %all-to-all-done.2.got_ref = s16[64,8,1024]{2,1,0:T(8,128)(2,1)S(1)} async-done(((s16[64,8,1024]{2,1,0:T(8,128)(2,1)}), s16[64,8,1024]{2,1,0:T(8,128)(2,1)S(1)}, u32[]{:S(2)}, u32[]{:S(2)}) %all-to-all-start.2) | async-done | bytes 1048608 | tf_op jit(solution)/shard_map/all_to_all | solution.py:226
  98.9 1.1 %finish.1 = f32[8,1024]{1,0:T(8,128)} custom-call(s32[1]{0:T(128)} %bitcast.me_ref, s16[64,8,1024]{2,1,0:T(8,128)(2,1)S(1)} %all-to-all-done.2.got_ref), custom_call_target="tpu_custom_call" | custom-call | tf_op jit(solution)/shard_map/finish/pallas_call | solution.py:196
Async XLA Ops:
  0.0 0.8 copy-start
  1.6 17.3 %all-to-all-start = ((bf16[16,64,256]{2,1,0:T(8,128)(2,1)}), bf16[16,64,256]{2,1,0:T(8,128)(2,1)S(1)}, u32[]{:S(2)}, u32[]{:S(2)}) async-start(bf16[16,64,256]{2,1,0:T(8,128)(2,1)} %copies.1), calls=%async_computation | async-start | bytes 1048576 | tf_op jit(solution)/shard_map/all_to_all | solution.py:214
  18.9 0.8 copy-start.2
  27.2 38.2 %copy-start.1 = (bf16[512,512]{1,0:T(8,128)(2,1)S(1)}, bf16[512,512]{1,0:T(8,128)(2,1)}, u32[]{:S(2)}) copy-start(bf16[512,512]{1,0:T(8,128)(2,1)} %metric_ref.3) | copy-start | bytes 1572868
  65.4 4.3 %collective-permute-start = (bf16[8,16,2,32,128]{4,3,2,1,0:T(8,128)(2,1)S(1)}, bf16[8,16,2,32,128]{4,3,2,1,0:T(8,128)(2,1)}, u32[]{:S(2)}, u32[]{:S(2)}) collective-permute-start(bf16[8,16,2,32,128]{4,3,2,1,0:T(8,128)(2,1)S(1)} %bitcast.6), channel_id=1, source_target_pairs={{0,1},{1,0},{2,3},{3,2},{4,5},{5,4},{6,7},{7,6},{8,9},{9,8},{10,11... | collective-permute-start | bytes 6291464 | tf_op jit(solution)/shard_map/ppermute | solution.py:220
  75.0 24.0 %all-to-all-start.2 = ((s16[64,8,1024]{2,1,0:T(8,128)(2,1)}), s16[64,8,1024]{2,1,0:T(8,128)(2,1)S(1)}, u32[]{:S(2)}, u32[]{:S(2)}) async-start(s16[64,8,1024]{2,1,0:T(8,128)(2,1)} %last_term.1), calls=%async_computation.2 | async-start | bytes 2097152 | tf_op jit(solution)/shard_map/all_to_all | solution.py:226

commit v4 on v3

--- a/solution.py
+++ b/solution.py
@@ -20,61 +20,52 @@
     return pltpu.CompilerParams(vmem_limit_bytes=mib << 20)
 
 
-def copies_kernel(orbitals_ref, out_ref):
-    for i in range(out_ref.shape[0]):
-        out_ref[i] = orbitals_ref[...]
-
-
-def copies_of(orbitals, count):
-    return pl.pallas_call(
-        copies_kernel,
-        out_shape=jax.ShapeDtypeStruct((count, *orbitals.shape), BF16),
-        in_specs=[VMEM],
-        out_specs=VMEM,
-        compiler_params=params(8),
-        name="copies",
-    )(orbitals)
-
-
-def reorder_kernel(tensor_ref, rows_ref):
-    block = tensor_ref[...]
-    ri, halves, step, basis = block.shape
-    turned = jnp.stack([pltpu.einshape("pmn->mpn", block[:, h]) for h in range(halves)], axis=1)
-    rows_ref[...] = turned.reshape(step * halves * ri, basis)
-
-
-def reorder(tensor3, step=8):
-    ri, mu, basis = tensor3.shape
-    return pl.pallas_call(
-        reorder_kernel,
-        out_shape=jax.ShapeDtypeStruct((mu * ri, basis), BF16),
-        grid=(mu // 2 // step,),
-        in_specs=[pl.BlockSpec((ri, 2, step, basis), lambda s: (0, 0, s, 0))],
-        out_specs=pl.BlockSpec((2 * step * ri, basis), lambda s: (s, 0)),
-        compiler_params=params(48),
-        cost_estimate=pl.CostEstimate(flops=0, bytes_accessed=4 * tensor3.size, transcendentals=0),
-        name="reorder",
-    )(tensor3.reshape(ri, 2, mu // 2, basis))
-
-
-def coeffs_kernel(step, pattern_ref, orbs_ref, rows_ref, out_ref, masked, turned, tiles, sems):
-    owners, height, lanes = out_ref.shape
-    height //= 2
-    span = step * lanes
-    steps = height // step
+def copies_kernel(orbitals_ref, out_ref, sems):
     copies = [
-        pltpu.make_async_copy(rows_ref.at[pl.ds(s * span, span)], tiles.at[s], sems.at[s])
-        for s in range(steps)
+        pltpu.make_async_copy(orbitals_ref, out_ref.at[i], sems.at[i])
+        for i in range(out_ref.shape[0])
     ]
     for copy in copies:
         copy.start()
+    for copy in copies:
+        copy.wait()
+
+
+def copies_of(orbitals, count):
+    return pl.pallas_call(
+        copies_kernel,
+        out_shape=jax.ShapeDtypeStruct((count, *orbitals.shape), BF16),
+        in_specs=[pl.BlockSpec(memory_space=pl.ANY)],
+        out_specs=pl.BlockSpec(memory_space=pl.ANY),
+        scratch_shapes=[pltpu.SemaphoreType.DMA((count,))],
+        compiler_params=params(8),
+        cost_estimate=pl.CostEstimate(flops=10**10, bytes_accessed=40 << 20, transcendentals=0),
+        name="copies",
+    )(orbitals)
+
+
+def coeffs_kernel(step, pattern_ref, orbs_ref, tensor_ref, out_ref, masked, turned, tiles):
+    owners, height, lanes = out_ref.shape
+    height, ri = height // 2, lanes // 2
+    steps = height // step
+
+    def gather(s):
+        for h in range(2):
+            block = tensor_ref[:, h * height + s * step : h * height + (s + 1) * step, :]
+            block = pltpu.einshape("pmn->mpn", block)
+            for m in range(step):
+                first = m * lanes + h * ri
+                tiles[s % 2, first : first + ri, :] = block[m]
+
+    gather(0)
     for b in range(orbs_ref.shape[0] // BLK):
         rows = pl.ds(b * BLK, BLK)
         masked[rows, :] = orbs_ref[rows, :].astype(F32) * pattern_ref[b].astype(F32)
     turned[...] = masked[...].T.astype(BF16)
     for s in range(steps):
-        copies[s].wait()
-        value = lax.dot_general(turned[...], tiles[s], NT, preferred_element_type=F32)
+        if s + 1 < steps:
+            gather(s + 1)
+        value = lax.dot_general(turned[...], tiles[s % 2], NT, preferred_element_type=F32)
         for i in range(2):
             part = value[i * owners : (i + 1) * owners].astype(BF16)
             stacked = jnp.stack([part[:, g * lanes : (g + 1) * lanes] for g in range(step)])
@@ -82,27 +73,25 @@
             out_ref[:, first : first + step, :] = pltpu.einshape("mjl->jml", stacked)
 
 
-def coeffs_of(pattern, orbs, rows, ri, owners, step=8):
+def coeffs_of(pattern, orbs, tensor3, owners, step=8):
     basis, occupied = orbs.shape
-    mu = rows.shape[0] // ri
-    steps = mu // 2 // step
+    ri, mu, _ = tensor3.shape
     return pl.pallas_call(
         functools.partial(coeffs_kernel, step),
         out_shape=jax.ShapeDtypeStruct((owners, mu, 2 * ri), BF16),
-        in_specs=[SMEM, VMEM, pl.BlockSpec(memory_space=pltpu.HBM)],
+        in_specs=[SMEM, VMEM, VMEM],
         out_specs=VMEM,
         scratch_shapes=[
             pltpu.VMEM((basis, occupied), F32),
             pltpu.VMEM((occupied, basis), BF16),
-            pltpu.VMEM((steps, step * 2 * ri, basis), BF16),
-            pltpu.SemaphoreType.DMA((steps,)),
+            pltpu.VMEM((2, step * 2 * ri, basis), BF16),
         ],
-        compiler_params=params(56),
+        compiler_params=params(20),
         cost_estimate=pl.CostEstimate(
-            flops=2 * rows.size * occupied, bytes_accessed=2 * rows.size, transcendentals=0
+            flops=2 * tensor3.size * occupied, bytes_accessed=2 * tensor3.size, transcendentals=0
         ),
         name="coeffs",
-    )(pattern, orbs, rows)
+    )(pattern, orbs, tensor3)
 
 
 def term_of(core, coef_ref, metric_ref):
@@ -139,14 +128,24 @@
     term = (sum_ref[...] + term_of(core, coef_ref, metric_ref)).reshape(blocks, rows, columns)
     largest = jnp.max(jnp.abs(term), axis=2, keepdims=True)
     code = jnp.ceil(jnp.log2(jnp.maximum(largest, 1e-30)) * 256.0)
-    scaled = term * (jnp.exp2(code * (-1.0 / 256.0)) * TOP)
-    block = lax.broadcasted_iota(jnp.int32, (blocks, rows, columns), 0)
-    row = lax.broadcasted_iota(jnp.int32, (blocks, rows, columns), 1)
-    column = lax.broadcasted_iota(jnp.int32, (blocks, rows, columns), 2)
-    column = column - rows * (2 * block + core)
-    scaled = jnp.where((column == 0) & (row > 0), code, scaled)
-    scaled = jnp.where((column == 1) & (row == rows - 1), code[:, 0:1], scaled)
-    out_ref[...] = jnp.round(scaled).astype(jnp.int32).astype(jnp.int16)
+    factor = jnp.exp2(code * (-1.0 / 256.0)) * TOP
+    lanes = 128
+    group = lanes // (2 * rows)
+    shape = (group, rows, lanes)
+    block = lax.broadcasted_iota(jnp.int32, shape, 0)
+    row = lax.broadcasted_iota(jnp.int32, shape, 1)
+    column = lax.broadcasted_iota(jnp.int32, shape, 2) - rows * (2 * block + core)
+    first = (column == 0) & (row > 0)
+    second = (column == 1) & (row == rows - 1)
+    for g in range(blocks // group):
+        some = slice(g * group, (g + 1) * group)
+        codes = code[some]
+        scaled = term[some] * factor[some]
+        part = scaled[:, :, g * lanes : (g + 1) * lanes]
+        part = jnp.where(first, codes, jnp.where(second, codes[:, 0:1], part))
+        scaled = [scaled[:, :, : g * lanes], part, scaled[:, :, (g + 1) * lanes :]]
+        scaled = jnp.concatenate([piece for piece in scaled if piece.size], axis=2)
+        out_ref[some] = jnp.round(scaled).astype(jnp.int32).astype(jnp.int16)
 
 
 def term_call(kernel, name, out_shape, core, *operands):
@@ -213,8 +212,7 @@
     core = (lax.axis_index("narrow") & 1).astype(jnp.int32).reshape(1)
     orbs = lax.all_to_all(copies_of(orbitals, n_narrow), "narrow", 0, 0, tiled=True)
     orbs = orbs.reshape(basis, occupied)
-    rows = reorder(tensor3)
-    parts = coeffs_of(pattern.reshape(-1), orbs, rows, ri_local, devices)
+    parts = coeffs_of(pattern.reshape(-1), orbs, tensor3, devices)
     coef = lax.all_to_all(parts, BOTH, 0, 0, tiled=True)
     coef = coef.reshape(n_wide, n_narrow, 2, mu_local // 2, 2 * ri_local)
     other = lax.ppermute(coef, "narrow", [(i, i ^ 1) for i in range(n_narrow)])

time: 101 us -> 95.9 us (0.950)
  blocking collectives: 38.2 us -> 55.3 us
  Pallas kernels: 24.6 us -> 13.1 us
  starting transfers between devices: 11.1 us -> 4.66 us
  waiting for transfers between devices: 24.6 us -> 21.7 us
    all_to_all x0 -> x1, blocking collectives: none -> 17.4 us  [body(): lax.all_to_all(copies_of(orbitals, n_narrow), 'narrow', 0, 0, tiled=True)]
    pallas_call x1 -> x0, Pallas kernels: 7.94 us -> none  [reorder(): pl.pallas_call(reorder_kernel, out_shape=jax.ShapeDtypeStruct((mu * ri, b...]
    all_to_all x1 -> x0, starting transfers between devices: 6.43 us -> none  [body(): lax.all_to_all(copies_of(orbitals, n_narrow), 'narrow', 0, 0, tiled=True)]
    pallas_call x1, Pallas kernels: 7.42 us -> 4.43 us  [coeffs_of(): pl.pallas_call(functools.partial(coeffs_kernel, step), out_shape=jax.Shap...]
    all_to_all x1 -> x0, waiting for transfers between devices: 2.93 us -> none  [body(): lax.all_to_all(copies_of(orbitals, n_narrow), 'narrow', 0, 0, tiled=True)]
  transfers between devices with their start and end apart: 3 -> 2, of which waited for: 3 -> 2; matrix products, arithmetic and copies ran while one was open for 0% -> 0% of each run, Pallas kernels for 10% -> 2%
where the time goes in v4:
time: 95.9 us; the launch traced here: 95.6 us
  blocking collectives  55.3 us (58%)
  waiting for transfers between devices  21.7 us (23%)
  Pallas kernels  13.1 us (14%)
  starting transfers between devices  4.66 us (5%)
    all_to_all x1, blocking collectives, body(): coef = lax.all_to_all(parts, BOTH, 0, 0, tiled=True)  37.9 us
    all_to_all x1, waiting for transfers between devices, body(): got = lax.all_to_all(parts, BOTH, 0, 0, tiled=True, axis_index_groups=sides)  19.3 us
    all_to_all x1, blocking collectives, body(): lax.all_to_all(copies_of(orbitals, n_narrow), 'narrow', 0, 0, tiled=True)  17.4 us
    pallas_call x2, Pallas kernels, term_call(): pl.pallas_call(kernel, out_shape=out_shape, in_specs=[SMEM] + [VMEM] * le...  6.75 us
    all_to_all x1, starting transfers between devices, body(): got = lax.all_to_all(parts, BOTH, 0, 0, tiled=True, axis_index_groups=sides)  4.65 us
    pallas_call x1, Pallas kernels, coeffs_of(): pl.pallas_call(functools.partial(coeffs_kernel, step), out_shape=jax.Shap...  4.43 us
    ppermute x1, waiting for transfers between devices, body(): other = lax.ppermute(coef, 'narrow', [(i, i ^ 1) for i in range(n_narrow)])  2.39 us
  transfers between devices with their start and end apart: 2, of which 2 were waited for; matrix products, arithmetic and copies ran while one was open for 0% of the time, Pallas kernels for 2%

profile of v4, /device:TPU:0, one launch (start us, length us, event | category | flops | bytes accessed | tf_op | source)
XLA Modules:
  0.0 95.6 jit_solution(14132720824714819868)
XLA Ops:
  0.0 0.0 copy-start.1
  0.0 0.0 copy-start.3
  0.0 0.8 copy-done.3
  0.8 0.0 copy-start
  0.8 0.8 copies.1
  1.6 17.4 %all_to_all.15 = bf16[16,64,256]{2,1,0:T(8,128)(2,1)S(1)} all-to-all(bf16[16,64,256]{2,1,0:T(8,128)(2,1)S(1)} %copies.1), channel_id=1, replica_groups=mesh['wide'=8,'narrow'=16] {'narrow'}, dimensions={0} | all-to-all | bytes 1048576 | tf_op jit(solution)/shard_map/all_to_all | solution.py:213
  19.0 0.0 copy-done.1
  19.0 0.0 copy-done
  19.0 4.4 %coeffs.1 = bf16[128,64,128]{2,1,0:T(8,128)(2,1)S(1)} custom-call(s32[16]{0:T(128)S(1)} %bitcast.8, bf16[1024,256]{1,0:T(8,128)(2,1)S(1)} %bitcast.5, bf16[64,64,1024]{2,1,0:T(8,128)(2,1)S(1)} %copy-done), custom_call_target="tpu_custom_call" | custom-call | flops 2147483648 | bytes 8388608 | tf_op jit(solution)/shard_map/coeffs/pallas_call | solution.py:79
  23.4 0.0 copy-start.2
  23.4 37.9 %all_to_all.16 = bf16[128,64,128]{2,1,0:T(8,128)(2,1)S(1)} all-to-all(bf16[128,64,128]{2,1,0:T(8,128)(2,1)S(1)} %coeffs.1), channel_id=1, replica_groups=mesh['wide'=8,'narrow'=16] {'wide','narrow'}, dimensions={0} | all-to-all | bytes 4194304 | tf_op jit(solution)/shard_map/all_to_all | solution.py:216
  61.4 0.0 collective-permute-start
  61.4 0.0 copy-done.2
  61.4 1.9 %own_term.1.sum_ref = f32[512,1024]{1,0:T(8,128)S(1)} custom-call(s32[1]{0:T(128)} %bitcast.1.core_ref, bf16[8,16,2,32,128]{4,3,2,1,0:T(8,128)(2,1)S(1)} %bitcast.7, bf16[512,512]{1,0:T(8,128)(2,1)S(1)} %copy-done.2), custom_call_target="tpu_custom_call" | custom-call | flops 1610612736 | bytes 6291456 | tf_op jit(solution)/shard_map/own_term/pallas_call | solution.py:156
  63.3 2.4 %collective-permute-done.coef_ref = bf16[8,16,2,32,128]{4,3,2,1,0:T(8,128)(2,1)} collective-permute-done((bf16[8,16,2,32,128]{4,3,2,1,0:T(8,128)(2,1)S(1)}, bf16[8,16,2,32,128]{4,3,2,1,0:T(8,128)(2,1)}, u32[]{:S(2)}, u32[]{:S(2)}) %collective-permute-start) | collective-permute-done | bytes 2097184 | tf_op jit(solution)/shard_map/ppermute | solution.py:218
  65.7 4.9 %last_term.1 = s16[64,8,1024]{2,1,0:T(8,128)(2,1)} custom-call(s32[1]{0:T(128)} %bitcast.1.core_ref, bf16[8,16,2,32,128]{4,3,2,1,0:T(8,128)(2,1)} %collective-permute-done.coef_ref, bf16[512,512]{1,0:T(8,128)(2,1)S(1)} %copy-done.2, f32[512,1024]{1,0:T(8,128)S(1)} %own_term.1.sum_ref), custom_call_target="tpu_custom_call" | custom-call | flops 1610612736 | bytes 6291456 | tf_op jit(solution)/shard_map/last_term/pallas_call | solution.py:156
  70.5 4.7 %all-to-all-start.2 = ((s16[64,8,1024]{2,1,0:T(8,128)(2,1)}), s16[64,8,1024]{2,1,0:T(8,128)(2,1)S(1)}, u32[]{:S(2)}, u32[]{:S(2)}) async-start(s16[64,8,1024]{2,1,0:T(8,128)(2,1)} %last_term.1), calls=%async_computation.2 | async-start | bytes 2097152 | tf_op jit(solution)/shard_map/all_to_all | solution.py:224
  75.2 19.3 %all-to-all-done.2.got_ref = s16[64,8,1024]{2,1,0:T(8,128)(2,1)S(1)} async-done(((s16[64,8,1024]{2,1,0:T(8,128)(2,1)}), s16[64,8,1024]{2,1,0:T(8,128)(2,1)S(1)}, u32[]{:S(2)}, u32[]{:S(2)}) %all-to-all-start.2) | async-done | bytes 1048608 | tf_op jit(solution)/shard_map/all_to_all | solution.py:224
  94.5 1.1 %finish.1 = f32[8,1024]{1,0:T(8,128)} custom-call(s32[1]{0:T(128)} %bitcast.me_ref, s16[64,8,1024]{2,1,0:T(8,128)(2,1)S(1)} %all-to-all-done.2.got_ref), custom_call_target="tpu_custom_call" | custom-call | tf_op jit(solution)/shard_map/finish/pallas_call | solution.py:195
Async XLA Ops:
  0.0 19.0 %copy-start.1 = (s32[1,1,16]{2,1,0:T(1,128)S(1)}, s32[1,1,16]{2,1,0:T(1,128)}, u32[]{:S(2)}) copy-start(s32[1,1,16]{2,1,0:T(1,128)} %param.5) | copy-start | bytes 196
  0.0 0.8 copy-start.3
  0.8 18.2 %copy-start = (bf16[64,64,1024]{2,1,0:T(8,128)(2,1)S(1)}, bf16[64,64,1024]{2,1,0:T(8,128)(2,1)}, u32[]{:S(2)}) copy-start(bf16[64,64,1024]{2,1,0:T(8,128)(2,1)} %tensor_ref.1) | copy-start | bytes 25165828
  23.4 38.0 %copy-start.2 = (bf16[512,512]{1,0:T(8,128)(2,1)S(1)}, bf16[512,512]{1,0:T(8,128)(2,1)}, u32[]{:S(2)}) copy-start(bf16[512,512]{1,0:T(8,128)(2,1)} %metric_ref.3) | copy-start | bytes 1572868
  61.4 4.3 %collective-permute-start = (bf16[8,16,2,32,128]{4,3,2,1,0:T(8,128)(2,1)S(1)}, bf16[8,16,2,32,128]{4,3,2,1,0:T(8,128)(2,1)}, u32[]{:S(2)}, u32[]{:S(2)}) collective-permute-start(bf16[8,16,2,32,128]{4,3,2,1,0:T(8,128)(2,1)S(1)} %bitcast.6), channel_id=1, source_target_pairs={{0,1},{1,0},{2,3},{3,2},{4,5},{5,4},{6,7},{7,6},{8,9},{9,8},{10,11... | collective-permute-start | bytes 6291464 | tf_op jit(solution)/shard_map/ppermute | solution.py:218
  70.5 24.0 %all-to-all-start.2 = ((s16[64,8,1024]{2,1,0:T(8,128)(2,1)}), s16[64,8,1024]{2,1,0:T(8,128)(2,1)S(1)}, u32[]{:S(2)}, u32[]{:S(2)}) async-start(s16[64,8,1024]{2,1,0:T(8,128)(2,1)} %last_term.1), calls=%async_computation.2 | async-start | bytes 2097152 | tf_op jit(solution)/shard_map/all_to_all | solution.py:224

commit v5 on v4

v5 whole, which is shorter than its diff:
```python
import functools

import jax
import jax.numpy as jnp
from jax import lax
from jax.experimental import pallas as pl
from jax.experimental.pallas import tpu as pltpu
from jax.sharding import PartitionSpec as P

BLK = 64
BOTH = ("wide", "narrow")
BF16, F32 = jnp.bfloat16, jnp.float32
TOP = 32766.0
VMEM = pl.BlockSpec(memory_space=pltpu.VMEM)
SMEM = pl.BlockSpec(memory_space=pltpu.SMEM)
NT = (((1,), (1,)), ((), ()))


def params(mib):
    return pltpu.CompilerParams(vmem_limit_bytes=mib << 20)


def copies_kernel(orbitals_ref, out_ref, sems):
    copies = [
        pltpu.make_async_copy(orbitals_ref, out_ref.at[i], sems.at[i])
        for i in range(out_ref.shape[0])
    ]
    for copy in copies:
        copy.start()
    for copy in copies:
        copy.wait()


def copies_of(orbitals, count):
    return pl.pallas_call(
        copies_kernel,
        out_shape=jax.ShapeDtypeStruct((count, *orbitals.shape), BF16),
        in_specs=[pl.BlockSpec(memory_space=pl.ANY)],
        out_specs=pl.BlockSpec(memory_space=pl.ANY),
        scratch_shapes=[pltpu.SemaphoreType.DMA((count,))],
        compiler_params=params(8),
        cost_estimate=pl.CostEstimate(flops=10**10, bytes_accessed=40 << 20, transcendentals=0),
        name="copies",
    )(orbitals)


def coeffs_kernel(step, pattern_ref, orbs_ref, tensor_ref, out_ref, masked):
    owners, height, lanes = out_ref.shape
    height, ri = height // 2, lanes // 2
    basis, occupied = orbs_ref.shape
    for b in range(basis // BLK):
        rows = pl.ds(b * BLK, BLK)
        masked[rows, :] = (orbs_ref[rows, :].astype(F32) * pattern_ref[b].astype(F32)).astype(BF16)
    for s in range(0, height, step):
        halves = []
        for h in range(2):
            block = tensor_ref[:, h * height + s : h * height + s + step, :]
            value = jnp.dot(
                block.reshape(ri * step, basis), masked[...], preferred_element_type=F32
            )
            halves.append(pltpu.einshape("pmi->mpi", value.reshape(ri, step, occupied)))
        value = jnp.concatenate(halves, axis=1)
        turned = jnp.stack([value[m].T for m in range(step)]).astype(BF16)
        turned = pltpu.einshape("mjl->jml", turned)
        for i in range(2):
            first = i * height + s
            out_ref[:, first : first + step, :] = turned[i * owners : (i + 1) * owners]


def coeffs_of(pattern, orbs, tensor3, owners, step=8):
    basis, occupied = orbs.shape
    ri, mu, _ = tensor3.shape
    return pl.pallas_call(
        functools.partial(coeffs_kernel, step),
        out_shape=jax.ShapeDtypeStruct((owners, mu, 2 * ri), BF16),
        in_specs=[SMEM, VMEM, VMEM],
        out_specs=VMEM,
        scratch_shapes=[pltpu.VMEM((basis, occupied), BF16)],
        compiler_params=params(20),
        cost_estimate=pl.CostEstimate(
            flops=2 * tensor3.size * occupied, bytes_accessed=2 * tensor3.size, transcendentals=0
        ),
        name="coeffs",
    )(pattern, orbs, tensor3)


def pack(coef_ref, out_ref):
    wide, blocks, orbitals, half, lanes = coef_ref.shape
    height, width = blocks * half, wide * lanes // 2
    low = lax.broadcasted_iota(jnp.int32, (height, lanes), 1) < lanes // 2
    for i in range(orbitals):
        for g in range(wide // 2):
            x = coef_ref[2 * g, :, i].reshape(height, lanes)
            y = coef_ref[2 * g + 1, :, i].reshape(height, lanes)
            one = jnp.where(low, x, pltpu.roll(y, lanes // 2, 1)).reshape(blocks, 1, half, lanes)
            two = jnp.where(low, pltpu.roll(x, lanes // 2, 1), y).reshape(blocks, 1, half, lanes)
            at = i * width + g * lanes
            both = jnp.concatenate([one, two], axis=1).reshape(2 * height, lanes)
            out_ref[:, at : at + lanes] = both


def term_of(core, first, count, packed_ref, metric_ref):
    width = metric_ref.shape[0]
    orbitals = packed_ref.shape[1] // width
    mine = packed_ref[first : first + count, :].astype(F32)
    mine = mine.reshape(count // 16, 2, 8, orbitals * width)
    mine = jnp.where(core == 0, mine[:, 0], mine[:, 1]).reshape(count // 2, orbitals * width)
    mine = mine.astype(BF16)
    fits = [
        lax.dot_general(
            mine[:, i * width : (i + 1) * width], metric_ref[...], NT, preferred_element_type=F32
        ).astype(BF16)
        for i in range(orbitals)
    ]
    fit = jnp.concatenate(fits, axis=1)
    return lax.dot_general(fit, packed_ref[...], NT, preferred_element_type=F32)


def first_kernel(core_ref, coef_ref, metric_ref, packed_ref, out_ref):
    pack(coef_ref, packed_ref)
    count = packed_ref.shape[0] // 2
    out_ref[...] = term_of(1 - core_ref[0], 0, count, packed_ref, metric_ref)


def second_kernel(core_ref, packed_ref, metric_ref, out_ref):
    count = packed_ref.shape[0] // 2
    out_ref[...] = term_of(1 - core_ref[0], count, count, packed_ref, metric_ref)


def own_kernel(core_ref, packed_ref, metric_ref, out_ref):
    out_ref[...] = term_of(core_ref[0], 0, packed_ref.shape[0], packed_ref, metric_ref)


def term_call(kernel, name, out_shape, core, *operands):
    rows = jax.tree.leaves(out_shape)[-1].shape[0]
    coef, metric = operands
    width = metric.shape[0]
    flops = 4 * rows * width * (width + coef.size // (2 * width))
    return pl.pallas_call(
        kernel,
        out_shape=out_shape,
        in_specs=[SMEM, VMEM, VMEM],
        out_specs=jax.tree.map(lambda _: VMEM, out_shape),
        compiler_params=params(20),
        cost_estimate=pl.CostEstimate(flops=flops, bytes_accessed=6 << 20, transcendentals=0),
        name=name,
    )(core, coef, metric)


def code_kernel(core_ref, sum_ref, one_ref, two_ref, out_ref, held, sems):
    copies = [
        pltpu.make_async_copy(ref, held.at[k], sems.at[k]) for k, ref in enumerate((one_ref, two_ref))
    ]
    for copy in copies:
        copy.start()
    core = core_ref[0]
    blocks, rows, columns = out_ref.shape
    lanes = 128
    group = lanes // (2 * rows)
    shape = (group, rows, lanes)
    block = lax.broadcasted_iota(jnp.int32, shape, 0)
    row = lax.broadcasted_iota(jnp.int32, shape, 1)
    column = lax.broadcasted_iota(jnp.int32, shape, 2) - rows * (2 * block + core)
    first = (column == 0) & (row > 0)
    second = (column == 1) & (row == rows - 1)
    groups = blocks // group
    for g in range(groups):
        k, at = divmod(g, groups // 2)
        if at == 0:
            copies[k].wait()
        term = sum_ref[g * group * rows : (g + 1) * group * rows, :]
        term += held[k, at * group * rows : (at + 1) * group * rows, :]
        term = term.reshape(group, rows, columns)
        largest = jnp.max(jnp.abs(term), axis=2, keepdims=True)
        code = jnp.ceil(jnp.log2(jnp.maximum(largest, 1e-30)) * 256.0)
        scaled = term * (jnp.exp2(code * (-1.0 / 256.0)) * TOP)
        part = scaled[:, :, g * lanes : (g + 1) * lanes]
        part = jnp.where(first, code, jnp.where(second, code[:, 0:1], part))
        scaled = [scaled[:, :, : g * lanes], part, scaled[:, :, (g + 1) * lanes :]]
        scaled = jnp.concatenate([piece for piece in scaled if piece.size], axis=2)
        out_ref[g * group : (g + 1) * group] = jnp.round(scaled).astype(jnp.int32).astype(jnp.int16)


def code_of(core, total, one, two, blocks):
    rows, columns = total.shape
    anywhere = pl.BlockSpec(memory_space=pl.ANY)
    return pl.pallas_call(
        code_kernel,
        out_shape=jax.ShapeDtypeStruct((blocks, rows // blocks, columns), jnp.int16),
        in_specs=[SMEM, VMEM, anywhere, anywhere],
        out_specs=VMEM,
        scratch_shapes=[pltpu.VMEM((2, *one.shape), F32), pltpu.SemaphoreType.DMA((2,))],
        compiler_params=params(16),
        cost_estimate=pl.CostEstimate(flops=0, bytes_accessed=6 << 20, transcendentals=0),
        name="code",
    )(core, total, one, two)


def finish_kernel(me_ref, got_ref, out_ref):
    blocks, rows, columns = got_ref.shape
    lanes = 128
    start = rows * me_ref[0]
    base = pl.multiple_of(start // lanes * lanes, lanes)
    at = start - base
    window = got_ref[:, :, pl.ds(base, lanes)].astype(jnp.int32).astype(F32)
    lane = lax.broadcasted_iota(jnp.int32, window.shape, 2)
    row = lax.broadcasted_iota(jnp.int32, window.shape, 1)
    code = jnp.sum(jnp.where(lane == at, window, 0.0), axis=2, keepdims=True)
    other = jnp.sum(jnp.where(lane == at + 1, window, 0.0), axis=2, keepdims=True)
    code = jnp.where(row[:, :, :1] == 0, other[:, rows - 1 :], code)
    factor = jnp.exp2(code * (1.0 / 256.0)) * (-1.0 / TOP)
    total = jnp.zeros((rows, columns), F32)
    for s in range(blocks):
        total += got_ref[s].astype(jnp.int32).astype(F32) * factor[s]
    out_ref[...] = total
    part = out_ref[:, pl.ds(base, lanes)]
    lane = lax.broadcasted_iota(jnp.int32, part.shape, 1) - at
    row = lax.broadcasted_iota(jnp.int32, part.shape, 0)
    first = jnp.broadcast_to(part[0:1], part.shape)
    mirrored = jnp.sum(jnp.where(lane == row, first, 0.0), axis=1, keepdims=True)
    corner = jnp.sum(jnp.where((lane == rows - 1) & (row == 1), part, 0.0))
    part = jnp.where((lane == 0) & (row > 0), mirrored, part)
    out_ref[:, pl.ds(base, lanes)] = jnp.where((lane == 1) & (row == rows - 1), corner, part)


def finish(me, got):
    return pl.pallas_call(
        finish_kernel,
        out_shape=jax.ShapeDtypeStruct(got.shape[1:], F32),
        in_specs=[SMEM, VMEM],
        out_specs=VMEM,
        compiler_params=params(8),
        name="finish",
    )(me, got)


def body(tensor3, pattern, orbitals, metric):
    ri_local, mu_local, basis = tensor3.shape
    n_wide, n_narrow = lax.axis_size("wide"), lax.axis_size("narrow")
    devices = n_wide * n_narrow
    me = (lax.axis_index("wide") * n_narrow + lax.axis_index("narrow")).astype(jnp.int32)
    core = (lax.axis_index("narrow") & 1).astype(jnp.int32).reshape(1)
    me, core, orbitals = lax.optimization_barrier((me.reshape(1), core, orbitals))
    swap = [(i, i ^ 1) for i in range(n_narrow)]
    orbs = lax.all_to_all(copies_of(orbitals, n_narrow), "narrow", 0, 0, tiled=True)
    orbs = orbs.reshape(basis, orbitals.shape[1])
    parts = coeffs_of(pattern.reshape(-1), orbs, tensor3, devices)
    coef = lax.all_to_all(parts, BOTH, 0, 0, tiled=True)
    coef = coef.reshape(n_wide, n_narrow, 2, mu_local // 2, 2 * ri_local)
    mu = n_narrow * mu_local
    quarter = jax.ShapeDtypeStruct((mu // 4, mu), F32)
    packed = jax.ShapeDtypeStruct((mu, 2 * metric.shape[0]), BF16)
    packed, one = term_call(first_kernel, "first", (packed, quarter), core, coef, metric)
    one = lax.ppermute(one, "narrow", swap)
    two = term_call(second_kernel, "second", quarter, core, packed, metric)
    two = lax.ppermute(two, "narrow", swap)
    total = jax.ShapeDtypeStruct((mu // 2, mu), F32)
    total = term_call(own_kernel, "own", total, core, packed, metric)
    parts = code_of(core, total, one, two, devices // 2)
    sides = [[j for j in range(devices) if j % 2 == c] for c in (0, 1)]
    got = lax.all_to_all(parts, BOTH, 0, 0, tiled=True, axis_index_groups=sides)
    return finish(me, got)


def solution(mesh):
    in_specs = (P("wide", "narrow", None), P("wide", "narrow", None), P("narrow", None), P())
    out_specs = P(("wide", "narrow"), None)
    return jax.shard_map(body, mesh=mesh, in_specs=in_specs, out_specs=out_specs, check_vma=False)
```

time: 95.9 us -> 92.6 us (0.966)
  blocking collectives: 55.3 us -> 78.4 us
  waiting for transfers between devices: 21.7 us -> 1.81 us
  starting transfers between devices: 4.66 us -> 0.58 us
  Pallas kernels: 13.1 us -> 10.7 us
    all_to_all x0 -> x1, blocking collectives: none -> 23.2 us  [body(): got = lax.all_to_all(parts, BOTH, 0, 0, tiled=True, axis_index_groups=sides)]
    all_to_all x1 -> x0, waiting for transfers between devices: 19.3 us -> none  [body(): got = lax.all_to_all(parts, BOTH, 0, 0, tiled=True, axis_index_groups=sides)]
    all_to_all x1 -> x0, starting transfers between devices: 4.65 us -> none  [body(): got = lax.all_to_all(parts, BOTH, 0, 0, tiled=True, axis_index_groups=sides)]
    pallas_call x2 -> x4, Pallas kernels: 6.75 us -> 4.93 us  [the longest x3 4.19 us: term_call(): pl.pallas_call(kernel, out_shape=out_shape, in_specs=[SMEM, VMEM, VMEM],...]
    ppermute x1 -> x2, waiting for transfers between devices: 2.39 us -> 1.81 us  [the longest x1 1.5 us: body(): one = lax.ppermute(one, 'narrow', swap)]
where the time goes in v5:
time: 92.6 us; the launch traced here: 92.5 us
  blocking collectives  78.4 us (85%)
  Pallas kernels  10.7 us (12%)
  waiting for transfers between devices  1.81 us (2%)
    all_to_all x1, blocking collectives, body(): coef = lax.all_to_all(parts, BOTH, 0, 0, tiled=True)  37.9 us
    all_to_all x1, blocking collectives, body(): got = lax.all_to_all(parts, BOTH, 0, 0, tiled=True, axis_index_groups=sides)  23.2 us
    all_to_all x1, blocking collectives, body(): lax.all_to_all(copies_of(orbitals, n_narrow), 'narrow', 0, 0, tiled=True)  17.2 us
    pallas_call x3, Pallas kernels, term_call(): pl.pallas_call(kernel, out_shape=out_shape, in_specs=[SMEM, VMEM, VMEM],...  4.19 us
    pallas_call x1, Pallas kernels, coeffs_of(): pl.pallas_call(functools.partial(coeffs_kernel, step), out_shape=jax.Shap...  3.85 us
  transfers between devices with their start and end apart: 2, of which 2 were waited for; matrix products, arithmetic and copies ran while one was open for 0% of the time, Pallas kernels for 2%

profile of v5, /device:TPU:0, one launch (start us, length us, event | category | flops | bytes accessed | tf_op | source)
XLA Modules:
  0.0 92.5 jit_solution(4796624805367041705)
XLA Ops:
  0.0 0.0 slice-start
  0.0 0.0 copy-start.2
  0.0 0.9 copy-done.2
  0.9 0.0 slice-start.1
  0.9 0.0 copy-start.1
  0.9 0.8 copies.1
  1.8 17.2 %all_to_all.15 = bf16[16,64,256]{2,1,0:T(8,128)(2,1)S(1)} all-to-all(bf16[16,64,256]{2,1,0:T(8,128)(2,1)S(1)} %copies.1), channel_id=1, replica_groups=mesh['wide'=8,'narrow'=16] {'narrow'}, dimensions={0} | all-to-all | bytes 1048576 | tf_op jit(solution)/shard_map/all_to_all | solution.py:245
  19.0 0.0 slice-done
  19.0 0.0 slice-done.1
  19.0 0.0 copy-done.1
  19.0 3.9 %coeffs.1 = bf16[128,64,128]{2,1,0:T(8,128)(2,1)S(1)} custom-call(s32[16]{0:T(128)S(1)} %bitcast.9, bf16[1024,256]{1,0:T(8,128)(2,1)S(1)} %bitcast.7, bf16[64,64,1024]{2,1,0:T(8,128)(2,1)S(1)} %bitcast.6), custom_call_target="tpu_custom_call" | custom-call | flops 2147483648 | bytes 8388608 | tf_op jit(solution)/shard_map/coeffs/pallas_call | solution.py:73
  22.9 0.0 copy-start
  22.9 37.9 %all_to_all.16 = bf16[128,64,128]{2,1,0:T(8,128)(2,1)S(1)} all-to-all(bf16[128,64,128]{2,1,0:T(8,128)(2,1)S(1)} %coeffs.1), channel_id=1, replica_groups=mesh['wide'=8,'narrow'=16] {'wide','narrow'}, dimensions={0} | all-to-all | bytes 4194304 | tf_op jit(solution)/shard_map/all_to_all | solution.py:248
  60.8 0.0 copy-done
  60.8 1.3 %first.1 = (bf16[1024,1024]{1,0:T(8,128)(2,1)S(1)}, f32[256,1024]{1,0:T(8,128)S(1)}) custom-call(s32[1]{0:T(128)} %bitcast.1.core_ref, bf16[8,16,2,32,128]{4,3,2,1,0:T(8,128)(2,1)S(1)} %bitcast.8, bf16[512,512]{1,0:T(8,128)(2,1)S(1)} %copy-done), custom_call_target="tpu_custom_call" | custom-call | flops 805306368 | bytes 6291456 | tf_op jit(solution)/shard_map/first/pallas_call | solution.py:139
  62.2 1.0 %second.1 = f32[256,1024]{1,0:T(8,128)S(1)} custom-call(s32[1]{0:T(128)} %bitcast.1.core_ref, bf16[1024,1024]{1,0:T(8,128)(2,1)S(1)} %get-tuple-element.13.packed_ref, bf16[512,512]{1,0:T(8,128)(2,1)S(1)} %copy-done), custom_call_target="tpu_custom_call" | custom-call | flops 805306368 | bytes 6291456 | tf_op jit(solution)/shard_map/second/pallas_call | solution.py:139
  63.2 0.1 collective-permute-start.1
  63.3 0.5 collective-permute-start
  63.8 1.8 %own.1.sum_ref = f32[512,1024]{1,0:T(8,128)S(1)} custom-call(s32[1]{0:T(128)} %bitcast.1.core_ref, bf16[1024,1024]{1,0:T(8,128)(2,1)S(1)} %get-tuple-element.13.packed_ref, bf16[512,512]{1,0:T(8,128)(2,1)S(1)} %copy-done), custom_call_target="tpu_custom_call" | custom-call | flops 1610612736 | bytes 6291456 | tf_op jit(solution)/shard_map/own/pallas_call | solution.py:139
  65.6 0.3 collective-permute-done.1.two_ref
  65.9 1.5 %collective-permute-done.one_ref = f32[256,1024]{1,0:T(8,128)S(1)} collective-permute-done((f32[256,1024]{1,0:T(8,128)S(1)}, f32[256,1024]{1,0:T(8,128)S(1)}, u32[]{:S(2)}, u32[]{:S(2)}) %collective-permute-start) | collective-permute-done | bytes 1048608 | tf_op jit(solution)/shard_map/ppermute | solution.py:254
  67.4 0.7 code.1
  68.2 23.2 %all_to_all.17.got_ref = s16[64,8,1024]{2,1,0:T(8,128)(2,1)S(1)} all-to-all(s16[64,8,1024]{2,1,0:T(8,128)(2,1)S(1)} %code.1), channel_id=1, replica_groups={{0,2,4,6,8,10,12,14,16,18,20,22,24,26,28,30,32,34,36,38,40,42,44,46,48,..., dimensions={0} | all-to-all | bytes 2097152 | tf_op jit(solution)/shard_map/all_to_all | solution.py:261
  91.4 1.1 %finish.1 = f32[8,1024]{1,0:T(8,128)} custom-call(s32[1]{0:T(128)} %bitcast.me_ref, s16[64,8,1024]{2,1,0:T(8,128)(2,1)S(1)} %all_to_all.17.got_ref), custom_call_target="tpu_custom_call" | custom-call | tf_op jit(solution)/shard_map/finish/pallas_call | solution.py:227
  (1 shorter events, 0.0 us)
Async XLA Ops:
  0.0 19.0 %slice-start = ((s8[8388608]{0:T(1024)(128)(4,1)}), s8[4194304]{0:T(1024)(128)(4,1)S(1)}, s32[]{:S(2)}) async-start(s8[8388608]{0:T(1024)(128)(4,1)} %bitcast.5), calls=%async_computation.3 | async-start | bytes 8388608
  0.0 0.9 copy-start.2
  0.9 18.1 %slice-start.1 = ((s8[8388608]{0:T(1024)(128)(4,1)}), s8[4194304]{0:T(1024)(128)(4,1)S(1)}, s32[]{:S(2)}) async-start(s8[8388608]{0:T(1024)(128)(4,1)} %bitcast.5), calls=%async_computation.4 | async-start | bytes 8388608
  0.9 18.1 %copy-start.1 = (s32[1,1,16]{2,1,0:T(1,128)S(1)}, s32[1,1,16]{2,1,0:T(1,128)}, u32[]{:S(2)}) copy-start(s32[1,1,16]{2,1,0:T(1,128)} %param.5) | copy-start | bytes 196
  22.9 38.0 %copy-start = (bf16[512,512]{1,0:T(8,128)(2,1)S(1)}, bf16[512,512]{1,0:T(8,128)(2,1)}, u32[]{:S(2)}) copy-start(bf16[512,512]{1,0:T(8,128)(2,1)} %metric_ref.5) | copy-start | bytes 1572868
  63.2 2.7 %collective-permute-start.1 = (f32[256,1024]{1,0:T(8,128)S(1)}, f32[256,1024]{1,0:T(8,128)S(1)}, u32[]{:S(2)}, u32[]{:S(2)}) collective-permute-start(f32[256,1024]{1,0:T(8,128)S(1)} %second.1), channel_id=1, source_target_pairs={{0,1},{1,0},{2,3},{3,2},{4,5},{5,4},{6,7},{7,6},{8,9},{9,8},{10,11... | collective-permute-start | bytes 3145736 | tf_op jit(solution)/shard_map/ppermute | solution.py:256
  63.3 4.1 %collective-permute-start = (f32[256,1024]{1,0:T(8,128)S(1)}, f32[256,1024]{1,0:T(8,128)S(1)}, u32[]{:S(2)}, u32[]{:S(2)}) collective-permute-start(f32[256,1024]{1,0:T(8,128)S(1)} %get-tuple-element.14), channel_id=1, source_target_pairs={{0,1},{1,0},{2,3},{3,2},{4,5},{5,4},{6,7},{7,6},{8,9},{9,8},{10,11... | collective-permute-start | bytes 3145736 | tf_op jit(solution)/shard_map/ppermute | solution.py:254

commit v6 on v5

--- a/solution.py
+++ b/solution.py
@@ -116,26 +116,22 @@
     return lax.dot_general(fit, packed_ref[...], NT, preferred_element_type=F32)
 
 
-def first_kernel(core_ref, coef_ref, metric_ref, packed_ref, out_ref):
+def partner_kernel(core_ref, coef_ref, metric_ref, packed_ref, *out_refs):
     pack(coef_ref, packed_ref)
-    count = packed_ref.shape[0] // 2
-    out_ref[...] = term_of(1 - core_ref[0], 0, count, packed_ref, metric_ref)
-
-
-def second_kernel(core_ref, packed_ref, metric_ref, out_ref):
-    count = packed_ref.shape[0] // 2
-    out_ref[...] = term_of(1 - core_ref[0], count, count, packed_ref, metric_ref)
+    term = term_of(1 - core_ref[0], 0, packed_ref.shape[0], packed_ref, metric_ref)
+    rows = out_refs[0].shape[0]
+    for k, out_ref in enumerate(out_refs):
+        out_ref[...] = term[k * rows : (k + 1) * rows]
 
 
 def own_kernel(core_ref, packed_ref, metric_ref, out_ref):
     out_ref[...] = term_of(core_ref[0], 0, packed_ref.shape[0], packed_ref, metric_ref)
 
 
-def term_call(kernel, name, out_shape, core, *operands):
-    rows = jax.tree.leaves(out_shape)[-1].shape[0]
-    coef, metric = operands
+def term_call(kernel, name, out_shape, core, coef, metric):
     width = metric.shape[0]
-    flops = 4 * rows * width * (width + coef.size // (2 * width))
+    columns = coef.size // (2 * width)
+    flops = 2 * columns * width * (width + columns)
     return pl.pallas_call(
         kernel,
         out_shape=out_shape,
@@ -147,9 +143,10 @@
     )(core, coef, metric)
 
 
-def code_kernel(core_ref, sum_ref, one_ref, two_ref, out_ref, held, sems):
+def code_kernel(core_ref, sum_ref, *refs):
+    *part_refs, out_ref, held, sems = refs
     copies = [
-        pltpu.make_async_copy(ref, held.at[k], sems.at[k]) for k, ref in enumerate((one_ref, two_ref))
+        pltpu.make_async_copy(ref, held.at[k], sems.at[k]) for k, ref in enumerate(part_refs)
     ]
     for copy in copies:
         copy.start()
@@ -165,7 +162,7 @@
     second = (column == 1) & (row == rows - 1)
     groups = blocks // group
     for g in range(groups):
-        k, at = divmod(g, groups // 2)
+        k, at = divmod(g, groups // len(copies))
         if at == 0:
             copies[k].wait()
         term = sum_ref[g * group * rows : (g + 1) * group * rows, :]
@@ -181,19 +178,22 @@
         out_ref[g * group : (g + 1) * group] = jnp.round(scaled).astype(jnp.int32).astype(jnp.int16)
 
 
-def code_of(core, total, one, two, blocks):
+def code_of(core, total, parts, blocks):
     rows, columns = total.shape
-    anywhere = pl.BlockSpec(memory_space=pl.ANY)
+    count = len(parts)
     return pl.pallas_call(
         code_kernel,
         out_shape=jax.ShapeDtypeStruct((blocks, rows // blocks, columns), jnp.int16),
-        in_specs=[SMEM, VMEM, anywhere, anywhere],
+        in_specs=[SMEM, VMEM] + [pl.BlockSpec(memory_space=pl.ANY)] * count,
         out_specs=VMEM,
-        scratch_shapes=[pltpu.VMEM((2, *one.shape), F32), pltpu.SemaphoreType.DMA((2,))],
+        scratch_shapes=[
+            pltpu.VMEM((count, *parts[0].shape), F32),
+            pltpu.SemaphoreType.DMA((count,)),
+        ],
         compiler_params=params(16),
         cost_estimate=pl.CostEstimate(flops=0, bytes_accessed=6 << 20, transcendentals=0),
         name="code",
-    )(core, total, one, two)
+    )(core, total, *parts)
 
 
 def finish_kernel(me_ref, got_ref, out_ref):
@@ -248,15 +248,13 @@
     coef = lax.all_to_all(parts, BOTH, 0, 0, tiled=True)
     coef = coef.reshape(n_wide, n_narrow, 2, mu_local // 2, 2 * ri_local)
     mu = n_narrow * mu_local
-    quarter = jax.ShapeDtypeStruct((mu // 4, mu), F32)
     packed = jax.ShapeDtypeStruct((mu, 2 * metric.shape[0]), BF16)
-    packed, one = term_call(first_kernel, "first", (packed, quarter), core, coef, metric)
-    one = lax.ppermute(one, "narrow", swap)
-    two = term_call(second_kernel, "second", quarter, core, packed, metric)
-    two = lax.ppermute(two, "narrow", swap)
+    part = jax.ShapeDtypeStruct((mu // 8, mu), F32)
+    packed, *parts = term_call(partner_kernel, "partner", (packed,) + (part,) * 4, core, coef, metric)
+    parts = [lax.ppermute(part, "narrow", swap) for part in parts]
     total = jax.ShapeDtypeStruct((mu // 2, mu), F32)
     total = term_call(own_kernel, "own", total, core, packed, metric)
-    parts = code_of(core, total, one, two, devices // 2)
+    parts = code_of(core, total, parts, devices // 2)
     sides = [[j for j in range(devices) if j % 2 == c] for c in (0, 1)]
     got = lax.all_to_all(parts, BOTH, 0, 0, tiled=True, axis_index_groups=sides)
     return finish(me, got)

time: 92.6 us -> 92.6 us (level)
    pallas_call x3 -> x2, Pallas kernels: 4.19 us -> 3.99 us  [term_call(): pl.pallas_call(kernel, out_shape=out_shape, in_specs=[SMEM, VMEM, VMEM],...]
  transfers between devices with their start and end apart: 2 -> 4, of which waited for: 2 -> 2; matrix products, arithmetic and copies ran while one was open for 0% -> 0% of each run, Pallas kernels for 2% -> 2%
where the time goes in v6:
time: 92.6 us; the launch traced here: 92.5 us
  blocking collectives  78.4 us (85%)
  Pallas kernels  10.7 us (12%)
  waiting for transfers between devices  1.28 us (1%)
  starting transfers between devices  1.09 us (1%)
    all_to_all x1, blocking collectives, body(): coef = lax.all_to_all(parts, BOTH, 0, 0, tiled=True)  37.9 us
    all_to_all x1, blocking collectives, body(): got = lax.all_to_all(parts, BOTH, 0, 0, tiled=True, axis_index_groups=sides)  23.2 us
    all_to_all x1, blocking collectives, body(): lax.all_to_all(copies_of(orbitals, n_narrow), 'narrow', 0, 0, tiled=True)  17.2 us
    pallas_call x2, Pallas kernels, term_call(): pl.pallas_call(kernel, out_shape=out_shape, in_specs=[SMEM, VMEM, VMEM],...  3.99 us
    pallas_call x1, Pallas kernels, coeffs_of(): pl.pallas_call(functools.partial(coeffs_kernel, step), out_shape=jax.Shap...  3.85 us
  transfers between devices with their start and end apart: 4, of which 2 were waited for; matrix products, arithmetic and copies ran while one was open for 0% of the time, Pallas kernels for 2%

profile of v6, /device:TPU:0, one launch (start us, length us, event | category | flops | bytes accessed | tf_op | source)
XLA Modules:
  0.0 92.5 jit_solution(7640964350277393214)
XLA Ops:
  0.0 0.0 slice-start
  0.0 0.0 copy-start.2
  0.0 0.9 copy-done.2
  0.9 0.0 slice-start.1
  0.9 0.0 copy-start
  0.9 0.8 copies.1
  1.8 17.2 %all_to_all.15 = bf16[16,64,256]{2,1,0:T(8,128)(2,1)S(1)} all-to-all(bf16[16,64,256]{2,1,0:T(8,128)(2,1)S(1)} %copies.1), channel_id=1, replica_groups=mesh['wide'=8,'narrow'=16] {'narrow'}, dimensions={0} | all-to-all | bytes 1048576 | tf_op jit(solution)/shard_map/all_to_all | solution.py:245
  19.0 0.0 slice-done
  19.0 0.0 slice-done.1
  19.0 0.0 copy-done
  19.0 3.9 %coeffs.1 = bf16[128,64,128]{2,1,0:T(8,128)(2,1)S(1)} custom-call(s32[16]{0:T(128)S(1)} %bitcast.9, bf16[1024,256]{1,0:T(8,128)(2,1)S(1)} %bitcast.7, bf16[64,64,1024]{2,1,0:T(8,128)(2,1)S(1)} %bitcast.6), custom_call_target="tpu_custom_call" | custom-call | flops 2147483648 | bytes 8388608 | tf_op jit(solution)/shard_map/coeffs/pallas_call | solution.py:73
  22.9 0.0 copy-start.1
  22.9 37.9 %all_to_all.16 = bf16[128,64,128]{2,1,0:T(8,128)(2,1)S(1)} all-to-all(bf16[128,64,128]{2,1,0:T(8,128)(2,1)S(1)} %coeffs.1), channel_id=1, replica_groups=mesh['wide'=8,'narrow'=16] {'wide','narrow'}, dimensions={0} | all-to-all | bytes 4194304 | tf_op jit(solution)/shard_map/all_to_all | solution.py:248
  60.8 0.0 copy-done.1
  60.8 2.2 %partner.1 = (bf16[1024,1024]{1,0:T(8,128)(2,1)S(1)}, f32[128,1024]{1,0:T(8,128)S(1)}, f32[128,1024]{1,0:T(8,128)S(1)}, f32[128,1024]{1,0:T(8,128)S(1)}, f32[128,1024]{1,0:T(8,128)S(1)}) custom-call(s32[1]{0:T(128)} %bitcast.1.core_ref, bf16[8,16,2,32,128]{4,3,2,1,0:T(8,128)(2,1)S(1)} %bitcast.8, bf16[512,512]{1,0:T(8,128)(2,1)S(1)} %copy-done.1), custom_call_target="tpu_custom_call" | custom-call | flops 1610612736 | bytes 6291456 | tf_op jit(solution)/shard_map/partner/pallas_call | solution.py:135
  63.0 0.1 collective-permute-start
  63.1 0.5 collective-permute-start.1
  63.6 0.1 collective-permute-start.2
  63.7 0.4 collective-permute-start.3
  64.1 1.8 %own.1.sum_ref = f32[512,1024]{1,0:T(8,128)S(1)} custom-call(s32[1]{0:T(128)} %bitcast.1.core_ref, bf16[1024,1024]{1,0:T(8,128)(2,1)S(1)} %get-tuple-element.16.packed_ref, bf16[512,512]{1,0:T(8,128)(2,1)S(1)} %copy-done.1), custom_call_target="tpu_custom_call" | custom-call | flops 1610612736 | bytes 6291456 | tf_op jit(solution)/shard_map/own/pallas_call | solution.py:135
  65.9 0.0 collective-permute-done.refs_0_
  65.9 0.0 collective-permute-done.1.refs_1_
  65.9 0.5 collective-permute-done.2.refs_2_
  66.5 0.7 collective-permute-done.3.refs_3_
  67.2 1.0 %code.1 = s16[64,8,1024]{2,1,0:T(8,128)(2,1)S(1)} custom-call(s32[1]{0:T(128)} %bitcast.1.core_ref, f32[512,1024]{1,0:T(8,128)S(1)} %own.1.sum_ref, f32[128,1024]{1,0:T(8,128)S(1)} %collective-permute-done.refs_0_, f32[128,1024]{1,0:T(8,128)S(1)} %collective-permute-done.1.refs_1_, f32[128,1024]{1,0:T(8,128)S(1)} %collective-permute-done.2.refs_2_, ...), custom_call_target="tpu_custom_call" | custom-call | bytes 6291456 | tf_op jit(solution)/shard_map/code/pallas_call | solution.py:184
  68.2 23.2 %all_to_all.17.got_ref = s16[64,8,1024]{2,1,0:T(8,128)(2,1)S(1)} all-to-all(s16[64,8,1024]{2,1,0:T(8,128)(2,1)S(1)} %code.1), channel_id=1, replica_groups={{0,2,4,6,8,10,12,14,16,18,20,22,24,26,28,30,32,34,36,38,40,42,44,46,48,..., dimensions={0} | all-to-all | bytes 2097152 | tf_op jit(solution)/shard_map/all_to_all | solution.py:259
  91.4 1.1 %finish.1 = f32[8,1024]{1,0:T(8,128)} custom-call(s32[1]{0:T(128)} %bitcast.me_ref, s16[64,8,1024]{2,1,0:T(8,128)(2,1)S(1)} %all_to_all.17.got_ref), custom_call_target="tpu_custom_call" | custom-call | tf_op jit(solution)/shard_map/finish/pallas_call | solution.py:227
  (1 shorter events, 0.0 us)
Async XLA Ops:
  0.0 19.0 %slice-start = ((s8[8388608]{0:T(1024)(128)(4,1)}), s8[4194304]{0:T(1024)(128)(4,1)S(1)}, s32[]{:S(2)}) async-start(s8[8388608]{0:T(1024)(128)(4,1)} %bitcast.5), calls=%async_computation.3 | async-start | bytes 8388608
  0.0 0.9 copy-start.2
  0.9 18.1 %slice-start.1 = ((s8[8388608]{0:T(1024)(128)(4,1)}), s8[4194304]{0:T(1024)(128)(4,1)S(1)}, s32[]{:S(2)}) async-start(s8[8388608]{0:T(1024)(128)(4,1)} %bitcast.5), calls=%async_computation.4 | async-start | bytes 8388608
  0.9 18.1 %copy-start = (s32[1,1,16]{2,1,0:T(1,128)S(1)}, s32[1,1,16]{2,1,0:T(1,128)}, u32[]{:S(2)}) copy-start(s32[1,1,16]{2,1,0:T(1,128)} %param.5) | copy-start | bytes 196
  22.9 38.0 %copy-start.1 = (bf16[512,512]{1,0:T(8,128)(2,1)S(1)}, bf16[512,512]{1,0:T(8,128)(2,1)}, u32[]{:S(2)}) copy-start(bf16[512,512]{1,0:T(8,128)(2,1)} %metric_ref.3) | copy-start | bytes 1572868
  63.0 2.9 %collective-permute-start = (f32[128,1024]{1,0:T(8,128)S(1)}, f32[128,1024]{1,0:T(8,128)S(1)}, u32[]{:S(2)}, u32[]{:S(2)}) collective-permute-start(f32[128,1024]{1,0:T(8,128)S(1)} %get-tuple-element.17), channel_id=1, source_target_pairs={{0,1},{1,0},{2,3},{3,2},{4,5},{5,4},{6,7},{7,6},{8,9},{9,8},{10,11... | collective-permute-start | bytes 1572872 | tf_op jit(solution)/shard_map/ppermute | solution.py:254
  63.1 2.9 %collective-permute-start.1 = (f32[128,1024]{1,0:T(8,128)S(1)}, f32[128,1024]{1,0:T(8,128)S(1)}, u32[]{:S(2)}, u32[]{:S(2)}) collective-permute-start(f32[128,1024]{1,0:T(8,128)S(1)} %get-tuple-element.18), channel_id=1, source_target_pairs={{0,1},{1,0},{2,3},{3,2},{4,5},{5,4},{6,7},{7,6},{8,9},{9,8},{10,11... | collective-permute-start | bytes 1572872 | tf_op jit(solution)/shard_map/ppermute | solution.py:254
  63.6 2.9 %collective-permute-start.2 = (f32[128,1024]{1,0:T(8,128)S(1)}, f32[128,1024]{1,0:T(8,128)S(1)}, u32[]{:S(2)}, u32[]{:S(2)}) collective-permute-start(f32[128,1024]{1,0:T(8,128)S(1)} %get-tuple-element.19), channel_id=1, source_target_pairs={{0,1},{1,0},{2,3},{3,2},{4,5},{5,4},{6,7},{7,6},{8,9},{9,8},{10,11... | collective-permute-start | bytes 1572872 | tf_op jit(solution)/shard_map/ppermute | solution.py:254
  63.7 3.6 %collective-permute-start.3 = (f32[128,1024]{1,0:T(8,128)S(1)}, f32[128,1024]{1,0:T(8,128)S(1)}, u32[]{:S(2)}, u32[]{:S(2)}) collective-permute-start(f32[128,1024]{1,0:T(8,128)S(1)} %get-tuple-element.20), channel_id=1, source_target_pairs={{0,1},{1,0},{2,3},{3,2},{4,5},{5,4},{6,7},{7,6},{8,9},{9,8},{10,11... | collective-permute-start | bytes 1572872 | tf_op jit(solution)/shard_map/ppermute | solution.py:254

commit v7 on v6

--- a/solution.py
+++ b/solution.py
@@ -41,7 +41,7 @@
         compiler_params=params(8),
         cost_estimate=pl.CostEstimate(flops=10**10, bytes_accessed=40 << 20, transcendentals=0),
         name="copies",
-    )(orbitals)
+    )(pltpu.with_memory_space_constraint(orbitals, pltpu.HBM))
 
 
 def coeffs_kernel(step, pattern_ref, orbs_ref, tensor_ref, out_ref, masked):
@@ -58,9 +58,10 @@
             value = jnp.dot(
                 block.reshape(ri * step, basis), masked[...], preferred_element_type=F32
             )
-            halves.append(pltpu.einshape("pmi->mpi", value.reshape(ri, step, occupied)))
+            value = value.astype(BF16).reshape(ri, step, occupied)
+            halves.append(pltpu.einshape("pmi->mpi", value))
         value = jnp.concatenate(halves, axis=1)
-        turned = jnp.stack([value[m].T for m in range(step)]).astype(BF16)
+        turned = jnp.stack([value[m].T for m in range(step)])
         turned = pltpu.einshape("mjl->jml", turned)
         for i in range(2):
             first = i * height + s
@@ -169,7 +170,7 @@
         term += held[k, at * group * rows : (at + 1) * group * rows, :]
         term = term.reshape(group, rows, columns)
         largest = jnp.max(jnp.abs(term), axis=2, keepdims=True)
-        code = jnp.ceil(jnp.log2(jnp.maximum(largest, 1e-30)) * 256.0)
+        code = jnp.ceil(jnp.log2(jnp.maximum(largest, 1e-33)) * 256.0)
         scaled = term * (jnp.exp2(code * (-1.0 / 256.0)) * TOP)
         part = scaled[:, :, g * lanes : (g + 1) * lanes]
         part = jnp.where(first, code, jnp.where(second, code[:, 0:1], part))
@@ -249,8 +250,8 @@
     coef = coef.reshape(n_wide, n_narrow, 2, mu_local // 2, 2 * ri_local)
     mu = n_narrow * mu_local
     packed = jax.ShapeDtypeStruct((mu, 2 * metric.shape[0]), BF16)
-    part = jax.ShapeDtypeStruct((mu // 8, mu), F32)
-    packed, *parts = term_call(partner_kernel, "partner", (packed,) + (part,) * 4, core, coef, metric)
+    part = jax.ShapeDtypeStruct((mu // 4, mu), F32)
+    packed, *parts = term_call(partner_kernel, "partner", (packed, part, part), core, coef, metric)
     parts = [lax.ppermute(part, "narrow", swap) for part in parts]
     total = jax.ShapeDtypeStruct((mu // 2, mu), F32)
     total = term_call(own_kernel, "own", total, core, packed, metric)

time: 92.6 us -> 92.2 us (level)
  transfers between devices with their start and end apart: 4 -> 2, of which waited for: 2 -> 2; matrix products, arithmetic and copies ran while one was open for 0% -> 0% of each run, Pallas kernels for 2% -> 2%
where the time goes in v7:
time: 92.2 us; the launch traced here: 92 us
  blocking collectives  78.5 us (85%)
  Pallas kernels  11 us (12%)
  waiting for transfers between devices  1.81 us (2%)
    all_to_all x1, blocking collectives, body(): coef = lax.all_to_all(parts, BOTH, 0, 0, tiled=True)  37.9 us
    all_to_all x1, blocking collectives, body(): got = lax.all_to_all(parts, BOTH, 0, 0, tiled=True, axis_index_groups=sides)  23.2 us
    all_to_all x1, blocking collectives, body(): lax.all_to_all(copies_of(orbitals, n_narrow), 'narrow', 0, 0, tiled=True)  17.4 us
    pallas_call x2, Pallas kernels, term_call(): pl.pallas_call(kernel, out_shape=out_shape, in_specs=[SMEM, VMEM, VMEM],...  3.98 us
    pallas_call x1, Pallas kernels, coeffs_of(): pl.pallas_call(functools.partial(coeffs_kernel, step), out_shape=jax.Shap...  3.73 us
  transfers between devices with their start and end apart: 2, of which 2 were waited for; matrix products, arithmetic and copies ran while one was open for 0% of the time, Pallas kernels for 2%

profile of v7, /device:TPU:0, one launch (start us, length us, event | category | flops | bytes accessed | tf_op | source)
XLA Modules:
  0.0 92.0 jit_solution(688715685980249809)
XLA Ops:
  0.0 0.0 slice-start
  0.0 0.0 slice-start.1
  0.0 0.0 copy-start
  0.0 1.5 %copies.1 = bf16[16,64,256]{2,1,0:T(8,128)(2,1)S(1)} custom-call(bf16[64,256]{1,0:T(8,128)(2,1)} %orbitals_ref), custom_call_target="tpu_custom_call" | custom-call | flops 10000000000 | bytes 41943040 | tf_op jit(solution)/shard_map/copies/pallas_call | solution.py:35
  1.5 17.4 %all_to_all.15 = bf16[16,64,256]{2,1,0:T(8,128)(2,1)S(1)} all-to-all(bf16[16,64,256]{2,1,0:T(8,128)(2,1)S(1)} %copies.1), channel_id=1, replica_groups=mesh['wide'=8,'narrow'=16] {'narrow'}, dimensions={0} | all-to-all | bytes 1048576 | tf_op jit(solution)/shard_map/all_to_all | solution.py:246
  18.9 0.0 slice-done
  18.9 0.0 slice-done.1
  18.9 0.0 copy-done
  18.9 3.7 %coeffs.1 = bf16[128,64,128]{2,1,0:T(8,128)(2,1)S(1)} custom-call(s32[16]{0:T(128)S(1)} %bitcast.9, bf16[1024,256]{1,0:T(8,128)(2,1)S(1)} %bitcast.7, bf16[64,64,1024]{2,1,0:T(8,128)(2,1)S(1)} %bitcast.6), custom_call_target="tpu_custom_call" | custom-call | flops 2147483648 | bytes 8388608 | tf_op jit(solution)/shard_map/coeffs/pallas_call | solution.py:74
  22.6 0.0 copy-start.1
  22.6 37.9 %all_to_all.16 = bf16[128,64,128]{2,1,0:T(8,128)(2,1)S(1)} all-to-all(bf16[128,64,128]{2,1,0:T(8,128)(2,1)S(1)} %coeffs.1), channel_id=1, replica_groups=mesh['wide'=8,'narrow'=16] {'wide','narrow'}, dimensions={0} | all-to-all | bytes 4194304 | tf_op jit(solution)/shard_map/all_to_all | solution.py:249
  60.6 0.0 copy-done.1
  60.6 2.1 %partner.1 = (bf16[1024,1024]{1,0:T(8,128)(2,1)S(1)}, f32[256,1024]{1,0:T(8,128)S(1)}, f32[256,1024]{1,0:T(8,128)S(1)}) custom-call(s32[1]{0:T(128)} %bitcast.1.core_ref, bf16[8,16,2,32,128]{4,3,2,1,0:T(8,128)(2,1)S(1)} %bitcast.8, bf16[512,512]{1,0:T(8,128)(2,1)S(1)} %copy-done.1), custom_call_target="tpu_custom_call" | custom-call | flops 1610612736 | bytes 6291456 | tf_op jit(solution)/shard_map/partner/pallas_call | solution.py:136
  62.7 0.1 collective-permute-start
  62.8 0.5 collective-permute-start.1
  63.3 1.8 %own.1.sum_ref = f32[512,1024]{1,0:T(8,128)S(1)} custom-call(s32[1]{0:T(128)} %bitcast.1.core_ref, bf16[1024,1024]{1,0:T(8,128)(2,1)S(1)} %get-tuple-element.14.packed_ref, bf16[512,512]{1,0:T(8,128)(2,1)S(1)} %copy-done.1), custom_call_target="tpu_custom_call" | custom-call | flops 1610612736 | bytes 6291456 | tf_op jit(solution)/shard_map/own/pallas_call | solution.py:136
  65.1 0.3 collective-permute-done.refs_0_
  65.5 1.5 %collective-permute-done.1.refs_1_ = f32[256,1024]{1,0:T(8,128)S(1)} collective-permute-done((f32[256,1024]{1,0:T(8,128)S(1)}, f32[256,1024]{1,0:T(8,128)S(1)}, u32[]{:S(2)}, u32[]{:S(2)}) %collective-permute-start.1) | collective-permute-done | bytes 1048608 | tf_op jit(solution)/shard_map/ppermute | solution.py:255
  67.0 0.7 code.1
  67.7 23.2 %all_to_all.17.got_ref = s16[64,8,1024]{2,1,0:T(8,128)(2,1)S(1)} all-to-all(s16[64,8,1024]{2,1,0:T(8,128)(2,1)S(1)} %code.1), channel_id=1, replica_groups={{0,2,4,6,8,10,12,14,16,18,20,22,24,26,28,30,32,34,36,38,40,42,44,46,48,..., dimensions={0} | all-to-all | bytes 2097152 | tf_op jit(solution)/shard_map/all_to_all | solution.py:260
  90.9 1.1 %finish.1 = f32[8,1024]{1,0:T(8,128)} custom-call(s32[1]{0:T(128)} %bitcast.me_ref, s16[64,8,1024]{2,1,0:T(8,128)(2,1)S(1)} %all_to_all.17.got_ref), custom_call_target="tpu_custom_call" | custom-call | tf_op jit(solution)/shard_map/finish/pallas_call | solution.py:228
  (1 shorter events, 0.0 us)
Async XLA Ops:
  0.0 18.9 %slice-start = ((s8[8388608]{0:T(1024)(128)(4,1)}), s8[4194304]{0:T(1024)(128)(4,1)S(1)}, s32[]{:S(2)}) async-start(s8[8388608]{0:T(1024)(128)(4,1)} %bitcast.5), calls=%async_computation.3 | async-start | bytes 8388608
  0.0 18.9 %slice-start.1 = ((s8[8388608]{0:T(1024)(128)(4,1)}), s8[4194304]{0:T(1024)(128)(4,1)S(1)}, s32[]{:S(2)}) async-start(s8[8388608]{0:T(1024)(128)(4,1)} %bitcast.5), calls=%async_computation.4 | async-start | bytes 8388608
  0.0 18.9 %copy-start = (s32[1,1,16]{2,1,0:T(1,128)S(1)}, s32[1,1,16]{2,1,0:T(1,128)}, u32[]{:S(2)}) copy-start(s32[1,1,16]{2,1,0:T(1,128)} %param.5) | copy-start | bytes 196
  22.6 38.0 %copy-start.1 = (bf16[512,512]{1,0:T(8,128)(2,1)S(1)}, bf16[512,512]{1,0:T(8,128)(2,1)}, u32[]{:S(2)}) copy-start(bf16[512,512]{1,0:T(8,128)(2,1)} %metric_ref.3) | copy-start | bytes 1572868
  62.7 2.7 %collective-permute-start = (f32[256,1024]{1,0:T(8,128)S(1)}, f32[256,1024]{1,0:T(8,128)S(1)}, u32[]{:S(2)}, u32[]{:S(2)}) collective-permute-start(f32[256,1024]{1,0:T(8,128)S(1)} %get-tuple-element.15), channel_id=1, source_target_pairs={{0,1},{1,0},{2,3},{3,2},{4,5},{5,4},{6,7},{7,6},{8,9},{9,8},{10,11... | collective-permute-start | bytes 3145736 | tf_op jit(solution)/shard_map/ppermute | solution.py:255
  62.8 4.1 %collective-permute-start.1 = (f32[256,1024]{1,0:T(8,128)S(1)}, f32[256,1024]{1,0:T(8,128)S(1)}, u32[]{:S(2)}, u32[]{:S(2)}) collective-permute-start(f32[256,1024]{1,0:T(8,128)S(1)} %get-tuple-element.16), channel_id=1, source_target_pairs={{0,1},{1,0},{2,3},{3,2},{4,5},{5,4},{6,7},{7,6},{8,9},{9,8},{10,11... | collective-permute-start | bytes 3145736 | tf_op jit(solution)/shard_map/ppermute | solution.py:255

commit v8 on v7

--- a/solution.py
+++ b/solution.py
@@ -86,13 +86,13 @@
 
 
 def pack(coef_ref, out_ref):
-    wide, blocks, orbitals, half, lanes = coef_ref.shape
+    blocks, wide, orbitals, half, lanes = coef_ref.shape
     height, width = blocks * half, wide * lanes // 2
     low = lax.broadcasted_iota(jnp.int32, (height, lanes), 1) < lanes // 2
     for i in range(orbitals):
         for g in range(wide // 2):
-            x = coef_ref[2 * g, :, i].reshape(height, lanes)
-            y = coef_ref[2 * g + 1, :, i].reshape(height, lanes)
+            x = coef_ref[:, 2 * g, i].reshape(height, lanes)
+            y = coef_ref[:, 2 * g + 1, i].reshape(height, lanes)
             one = jnp.where(low, x, pltpu.roll(y, lanes // 2, 1)).reshape(blocks, 1, half, lanes)
             two = jnp.where(low, pltpu.roll(x, lanes // 2, 1), y).reshape(blocks, 1, half, lanes)
             at = i * width + g * lanes
@@ -246,8 +246,8 @@
     orbs = lax.all_to_all(copies_of(orbitals, n_narrow), "narrow", 0, 0, tiled=True)
     orbs = orbs.reshape(basis, orbitals.shape[1])
     parts = coeffs_of(pattern.reshape(-1), orbs, tensor3, devices)
-    coef = lax.all_to_all(parts, BOTH, 0, 0, tiled=True)
-    coef = coef.reshape(n_wide, n_narrow, 2, mu_local // 2, 2 * ri_local)
+    coef = lax.all_to_all(parts, ("narrow", "wide"), 0, 0, tiled=True)
+    coef = coef.reshape(n_narrow, n_wide, 2, mu_local // 2, 2 * ri_local)
     mu = n_narrow * mu_local
     packed = jax.ShapeDtypeStruct((mu, 2 * metric.shape[0]), BF16)
     part = jax.ShapeDtypeStruct((mu // 4, mu), F32)

time: 92.2 us -> 92.2 us (level)
    all_to_all x1, blocking collectives: 23.2 us -> 24.2 us  [body(): got = lax.all_to_all(parts, BOTH, 0, 0, tiled=True, axis_index_groups=sides)]
    all_to_all x1, blocking collectives: 37.9 us -> 37 us  [body(): coef = lax.all_to_all(parts, ('narrow', 'wide'), 0, 0, tiled=True)]
where the time goes in v8:
time: 92.2 us; the launch traced here: 92 us
  blocking collectives  78.5 us (85%)
  Pallas kernels  11 us (12%)
  waiting for transfers between devices  1.81 us (2%)
    all_to_all x1, blocking collectives, body(): coef = lax.all_to_all(parts, ('narrow', 'wide'), 0, 0, tiled=True)  37 us
    all_to_all x1, blocking collectives, body(): got = lax.all_to_all(parts, BOTH, 0, 0, tiled=True, axis_index_groups=sides)  24.2 us
    all_to_all x1, blocking collectives, body(): lax.all_to_all(copies_of(orbitals, n_narrow), 'narrow', 0, 0, tiled=True)  17.4 us
    pallas_call x2, Pallas kernels, term_call(): pl.pallas_call(kernel, out_shape=out_shape, in_specs=[SMEM, VMEM, VMEM],...  4 us
    pallas_call x1, Pallas kernels, coeffs_of(): pl.pallas_call(functools.partial(coeffs_kernel, step), out_shape=jax.Shap...  3.73 us
  transfers between devices with their start and end apart: 2, of which 2 were waited for; matrix products, arithmetic and copies ran while one was open for 0% of the time, Pallas kernels for 2%

profile of v8, /device:TPU:0, one launch (start us, length us, event | category | flops | bytes accessed | tf_op | source)
XLA Modules:
  0.0 92.0 jit_solution(5574762860463569788)
XLA Ops:
  0.0 0.0 slice-start
  0.0 0.0 slice-start.1
  0.0 0.0 copy-start
  0.0 1.5 %copies.1 = bf16[16,64,256]{2,1,0:T(8,128)(2,1)S(1)} custom-call(bf16[64,256]{1,0:T(8,128)(2,1)} %orbitals_ref), custom_call_target="tpu_custom_call" | custom-call | flops 10000000000 | bytes 41943040 | tf_op jit(solution)/shard_map/copies/pallas_call | solution.py:35
  1.5 17.4 %all_to_all.15 = bf16[16,64,256]{2,1,0:T(8,128)(2,1)S(1)} all-to-all(bf16[16,64,256]{2,1,0:T(8,128)(2,1)S(1)} %copies.1), channel_id=1, replica_groups=mesh['wide'=8,'narrow'=16] {'narrow'}, dimensions={0} | all-to-all | bytes 1048576 | tf_op jit(solution)/shard_map/all_to_all | solution.py:246
  18.9 0.0 slice-done
  18.9 0.0 slice-done.1
  18.9 0.0 copy-done
  18.9 3.7 %coeffs.1 = bf16[128,64,128]{2,1,0:T(8,128)(2,1)S(1)} custom-call(s32[16]{0:T(128)S(1)} %bitcast.9, bf16[1024,256]{1,0:T(8,128)(2,1)S(1)} %bitcast.7, bf16[64,64,1024]{2,1,0:T(8,128)(2,1)S(1)} %bitcast.6), custom_call_target="tpu_custom_call" | custom-call | flops 2147483648 | bytes 8388608 | tf_op jit(solution)/shard_map/coeffs/pallas_call | solution.py:74
  22.6 0.0 copy-start.1
  22.6 37.0 %all_to_all.16 = bf16[128,64,128]{2,1,0:T(8,128)(2,1)S(1)} all-to-all(bf16[128,64,128]{2,1,0:T(8,128)(2,1)S(1)} %coeffs.1), channel_id=1, replica_groups=mesh['wide'=8,'narrow'=16] {'narrow','wide'}, dimensions={0} | all-to-all | bytes 4194304 | tf_op jit(solution)/shard_map/all_to_all | solution.py:249
  59.6 0.0 copy-done.1
  59.6 2.2 %partner.1 = (bf16[1024,1024]{1,0:T(8,128)(2,1)S(1)}, f32[256,1024]{1,0:T(8,128)S(1)}, f32[256,1024]{1,0:T(8,128)S(1)}) custom-call(s32[1]{0:T(128)} %bitcast.1.core_ref, bf16[16,8,2,32,128]{4,3,2,1,0:T(8,128)(2,1)S(1)} %bitcast.8, bf16[512,512]{1,0:T(8,128)(2,1)S(1)} %copy-done.1), custom_call_target="tpu_custom_call" | custom-call | flops 1610612736 | bytes 6291456 | tf_op jit(solution)/shard_map/partner/pallas_call | solution.py:136
  61.7 0.1 collective-permute-start
  61.8 0.5 collective-permute-start.1
  62.3 1.8 %own.1.sum_ref = f32[512,1024]{1,0:T(8,128)S(1)} custom-call(s32[1]{0:T(128)} %bitcast.1.core_ref, bf16[1024,1024]{1,0:T(8,128)(2,1)S(1)} %get-tuple-element.14.packed_ref, bf16[512,512]{1,0:T(8,128)(2,1)S(1)} %copy-done.1), custom_call_target="tpu_custom_call" | custom-call | flops 1610612736 | bytes 6291456 | tf_op jit(solution)/shard_map/own/pallas_call | solution.py:136
  64.2 0.3 collective-permute-done.refs_0_
  64.5 1.5 %collective-permute-done.1.refs_1_ = f32[256,1024]{1,0:T(8,128)S(1)} collective-permute-done((f32[256,1024]{1,0:T(8,128)S(1)}, f32[256,1024]{1,0:T(8,128)S(1)}, u32[]{:S(2)}, u32[]{:S(2)}) %collective-permute-start.1) | collective-permute-done | bytes 1048608 | tf_op jit(solution)/shard_map/ppermute | solution.py:255
  66.0 0.7 code.1
  66.7 24.2 %all_to_all.17.got_ref = s16[64,8,1024]{2,1,0:T(8,128)(2,1)S(1)} all-to-all(s16[64,8,1024]{2,1,0:T(8,128)(2,1)S(1)} %code.1), channel_id=1, replica_groups={{0,2,4,6,8,10,12,14,16,18,20,22,24,26,28,30,32,34,36,38,40,42,44,46,48,..., dimensions={0} | all-to-all | bytes 2097152 | tf_op jit(solution)/shard_map/all_to_all | solution.py:260
  90.9 1.1 %finish.1 = f32[8,1024]{1,0:T(8,128)} custom-call(s32[1]{0:T(128)} %bitcast.me_ref, s16[64,8,1024]{2,1,0:T(8,128)(2,1)S(1)} %all_to_all.17.got_ref), custom_call_target="tpu_custom_call" | custom-call | tf_op jit(solution)/shard_map/finish/pallas_call | solution.py:228
  (1 shorter events, 0.0 us)
Async XLA Ops:
  0.0 18.9 %slice-start = ((s8[8388608]{0:T(1024)(128)(4,1)}), s8[4194304]{0:T(1024)(128)(4,1)S(1)}, s32[]{:S(2)}) async-start(s8[8388608]{0:T(1024)(128)(4,1)} %bitcast.5), calls=%async_computation.3 | async-start | bytes 8388608
  0.0 18.9 %slice-start.1 = ((s8[8388608]{0:T(1024)(128)(4,1)}), s8[4194304]{0:T(1024)(128)(4,1)S(1)}, s32[]{:S(2)}) async-start(s8[8388608]{0:T(1024)(128)(4,1)} %bitcast.5), calls=%async_computation.4 | async-start | bytes 8388608
  0.0 18.9 %copy-start = (s32[1,1,16]{2,1,0:T(1,128)S(1)}, s32[1,1,16]{2,1,0:T(1,128)}, u32[]{:S(2)}) copy-start(s32[1,1,16]{2,1,0:T(1,128)} %param.5) | copy-start | bytes 196
  22.6 37.0 %copy-start.1 = (bf16[512,512]{1,0:T(8,128)(2,1)S(1)}, bf16[512,512]{1,0:T(8,128)(2,1)}, u32[]{:S(2)}) copy-start(bf16[512,512]{1,0:T(8,128)(2,1)} %metric_ref.3) | copy-start | bytes 1572868
  61.7 2.7 %collective-permute-start = (f32[256,1024]{1,0:T(8,128)S(1)}, f32[256,1024]{1,0:T(8,128)S(1)}, u32[]{:S(2)}, u32[]{:S(2)}) collective-permute-start(f32[256,1024]{1,0:T(8,128)S(1)} %get-tuple-element.15), channel_id=1, source_target_pairs={{0,1},{1,0},{2,3},{3,2},{4,5},{5,4},{6,7},{7,6},{8,9},{9,8},{10,11... | collective-permute-start | bytes 3145736 | tf_op jit(solution)/shard_map/ppermute | solution.py:255
  61.8 4.1 %collective-permute-start.1 = (f32[256,1024]{1,0:T(8,128)S(1)}, f32[256,1024]{1,0:T(8,128)S(1)}, u32[]{:S(2)}, u32[]{:S(2)}) collective-permute-start(f32[256,1024]{1,0:T(8,128)S(1)} %get-tuple-element.16), channel_id=1, source_target_pairs={{0,1},{1,0},{2,3},{3,2},{4,5},{5,4},{6,7},{7,6},{8,9},{9,8},{10,11... | collective-permute-start | bytes 3145736 | tf_op jit(solution)/shard_map/ppermute | solution.py:255

commit v9 on v7

--- a/solution.py
+++ b/solution.py
@@ -44,13 +44,15 @@
     )(pltpu.with_memory_space_constraint(orbitals, pltpu.HBM))
 
 
-def coeffs_kernel(step, pattern_ref, orbs_ref, tensor_ref, out_ref, masked):
+def coeffs_kernel(step, core_ref, pattern_ref, mine_ref, other_ref, tensor_ref, out_ref, masked):
     owners, height, lanes = out_ref.shape
     height, ri = height // 2, lanes // 2
-    basis, occupied = orbs_ref.shape
-    for b in range(basis // BLK):
-        rows = pl.ds(b * BLK, BLK)
-        masked[rows, :] = (orbs_ref[rows, :].astype(F32) * pattern_ref[b].astype(F32)).astype(BF16)
+    basis, occupied = masked.shape
+    for b in range(mine_ref.shape[0]):
+        for orbs_ref, core in ((mine_ref, core_ref[0]), (other_ref, 1 - core_ref[0])):
+            rows = pl.ds(pl.multiple_of((2 * b + core) * BLK, BLK), BLK)
+            keep = pattern_ref[2 * b + core].astype(F32)
+            masked[rows, :] = (orbs_ref[b].astype(F32) * keep).astype(BF16)
     for s in range(0, height, step):
         halves = []
         for h in range(2):
@@ -68,13 +70,13 @@
             out_ref[:, first : first + step, :] = turned[i * owners : (i + 1) * owners]
 
 
-def coeffs_of(pattern, orbs, tensor3, owners, step=8):
-    basis, occupied = orbs.shape
-    ri, mu, _ = tensor3.shape
+def coeffs_of(core, pattern, mine, other, tensor3, owners, step=8):
+    occupied = mine.shape[2]
+    ri, mu, basis = tensor3.shape
     return pl.pallas_call(
         functools.partial(coeffs_kernel, step),
         out_shape=jax.ShapeDtypeStruct((owners, mu, 2 * ri), BF16),
-        in_specs=[SMEM, VMEM, VMEM],
+        in_specs=[SMEM, SMEM, VMEM, VMEM, VMEM],
         out_specs=VMEM,
         scratch_shapes=[pltpu.VMEM((basis, occupied), BF16)],
         compiler_params=params(20),
@@ -82,7 +84,7 @@
             flops=2 * tensor3.size * occupied, bytes_accessed=2 * tensor3.size, transcendentals=0
         ),
         name="coeffs",
-    )(pattern, orbs, tensor3)
+    )(core, pattern, mine, other, tensor3)
 
 
 def pack(coef_ref, out_ref):
@@ -243,9 +245,11 @@
     core = (lax.axis_index("narrow") & 1).astype(jnp.int32).reshape(1)
     me, core, orbitals = lax.optimization_barrier((me.reshape(1), core, orbitals))
     swap = [(i, i ^ 1) for i in range(n_narrow)]
-    orbs = lax.all_to_all(copies_of(orbitals, n_narrow), "narrow", 0, 0, tiled=True)
-    orbs = orbs.reshape(basis, orbitals.shape[1])
-    parts = coeffs_of(pattern.reshape(-1), orbs, tensor3, devices)
+    sides = [[i for i in range(n_narrow) if i % 2 == c] for c in (0, 1)]
+    copies = copies_of(orbitals, n_narrow // 2)
+    mine = lax.all_to_all(copies, "narrow", 0, 0, tiled=True, axis_index_groups=sides)
+    other = lax.ppermute(mine, "narrow", swap)
+    parts = coeffs_of(core, pattern.reshape(-1), mine, other, tensor3, devices)
     coef = lax.all_to_all(parts, BOTH, 0, 0, tiled=True)
     coef = coef.reshape(n_wide, n_narrow, 2, mu_local // 2, 2 * ri_local)
     mu = n_narrow * mu_local

time: 92.2 us -> 89.7 us (0.973)
  blocking collectives: 78.5 us -> 74.7 us
  waiting for transfers between devices: 1.81 us -> 3.33 us
    all_to_all x1, blocking collectives: 17.4 us -> 13.6 us  [body(): lax.all_to_all(copies, 'narrow', 0, 0, tiled=True, axis_index_groups=sides)]
    ppermute x0 -> x1, waiting for transfers between devices: none -> 1.53 us  [body(): other = lax.ppermute(mine, 'narrow', swap)]
  transfers between devices with their start and end apart: 2 -> 3, of which waited for: 2 -> 3; matrix products, arithmetic and copies ran while one was open for 0% -> 0% of each run, Pallas kernels for 2% -> 2%
where the time goes in v9:
time: 89.7 us; the launch traced here: 89.5 us
  blocking collectives  74.7 us (83%)
  Pallas kernels  10.8 us (12%)
  waiting for transfers between devices  3.33 us (4%)
    all_to_all x1, blocking collectives, body(): coef = lax.all_to_all(parts, BOTH, 0, 0, tiled=True)  37.9 us
    all_to_all x1, blocking collectives, body(): got = lax.all_to_all(parts, BOTH, 0, 0, tiled=True, axis_index_groups=sides)  23.2 us
    all_to_all x1, blocking collectives, body(): lax.all_to_all(copies, 'narrow', 0, 0, tiled=True, axis_index_groups=sides)  13.6 us
    pallas_call x2, Pallas kernels, term_call(): pl.pallas_call(kernel, out_shape=out_shape, in_specs=[SMEM, VMEM, VMEM],...  4.05 us
    pallas_call x1, Pallas kernels, coeffs_of(): pl.pallas_call(functools.partial(coeffs_kernel, step), out_shape=jax.Shap...  3.83 us
    ppermute x2, waiting for transfers between devices, body(): parts = [lax.ppermute(part, 'narrow', swap) for part in parts]  1.8 us
  transfers between devices with their start and end apart: 3, of which 3 were waited for; matrix products, arithmetic and copies ran while one was open for 0% of the time, Pallas kernels for 2%

profile of v9, /device:TPU:0, one launch (start us, length us, event | category | flops | bytes accessed | tf_op | source)
XLA Modules:
  0.0 89.5 jit_solution(5573194625514143085)
XLA Ops:
  0.0 0.0 slice-start
  0.0 0.0 slice-start.1
  0.0 0.0 copy-start
  0.0 1.1 %copies.1 = bf16[8,64,256]{2,1,0:T(8,128)(2,1)S(1)} custom-call(bf16[64,256]{1,0:T(8,128)(2,1)} %orbitals_ref), custom_call_target="tpu_custom_call" | custom-call | flops 10000000000 | bytes 41943040 | tf_op jit(solution)/shard_map/copies/pallas_call | solution.py:35
  1.1 13.6 %all_to_all.15.mine_ref = bf16[8,64,256]{2,1,0:T(8,128)(2,1)S(1)} all-to-all(bf16[8,64,256]{2,1,0:T(8,128)(2,1)S(1)} %copies.1), channel_id=1, replica_groups={{0,2,4,6,8,10,12,14},{1,3,5,7,9,11,13,15},{16,18,20,22,24,26,28,30},{17..., dimensions={0} | all-to-all | bytes 524288 | tf_op jit(solution)/shard_map/all_to_all | solution.py:250
  14.7 0.0 collective-permute-start
  14.7 1.5 %collective-permute-done.other_ref = bf16[8,64,256]{2,1,0:T(8,128)(2,1)S(1)} collective-permute-done((bf16[8,64,256]{2,1,0:T(8,128)(2,1)S(1)}, bf16[8,64,256]{2,1,0:T(8,128)(2,1)S(1)}, u32[]{:S(2)}, u32[]{:S(2)}) %collective-permute-start) | collective-permute-done | bytes 262176 | tf_op jit(solution)/shard_map/ppermute | solution.py:251
  16.3 0.0 slice-done
  16.3 0.0 slice-done.1
  16.3 0.0 copy-done
  16.3 3.8 %coeffs.1 = bf16[128,64,128]{2,1,0:T(8,128)(2,1)S(1)} custom-call(s32[1]{0:T(128)} %bitcast.1.core_ref, s32[16]{0:T(128)S(1)} %bitcast.7, bf16[8,64,256]{2,1,0:T(8,128)(2,1)S(1)} %all_to_all.15.mine_ref, bf16[8,64,256]{2,1,0:T(8,128)(2,1)S(1)} %collective-permute-done.other_ref, bf16[64,64,1024]{2,1,0:T(8,128)(2,1)S(1)} %bitcast.5), custom_call_target="tpu_custom_call" | custom-call | flops 2147483648 | bytes 8388608 | tf_op jit(solution)/shard_map/coeffs/pallas_call | solution.py:76
  20.1 0.0 copy-start.1
  20.2 37.9 %all_to_all.16 = bf16[128,64,128]{2,1,0:T(8,128)(2,1)S(1)} all-to-all(bf16[128,64,128]{2,1,0:T(8,128)(2,1)S(1)} %coeffs.1), channel_id=1, replica_groups=mesh['wide'=8,'narrow'=16] {'wide','narrow'}, dimensions={0} | all-to-all | bytes 4194304 | tf_op jit(solution)/shard_map/all_to_all | solution.py:253
  58.0 0.0 copy-done.1
  58.0 2.2 %partner.1 = (bf16[1024,1024]{1,0:T(8,128)(2,1)S(1)}, f32[256,1024]{1,0:T(8,128)S(1)}, f32[256,1024]{1,0:T(8,128)S(1)}) custom-call(s32[1]{0:T(128)} %bitcast.1.core_ref, bf16[8,16,2,32,128]{4,3,2,1,0:T(8,128)(2,1)S(1)} %bitcast.6, bf16[512,512]{1,0:T(8,128)(2,1)S(1)} %copy-done.1), custom_call_target="tpu_custom_call" | custom-call | flops 1610612736 | bytes 6291456 | tf_op jit(solution)/shard_map/partner/pallas_call | solution.py:138
  60.3 0.1 collective-permute-start.1
  60.3 0.5 collective-permute-start.2
  60.8 1.8 %own.1.sum_ref = f32[512,1024]{1,0:T(8,128)S(1)} custom-call(s32[1]{0:T(128)} %bitcast.1.core_ref, bf16[1024,1024]{1,0:T(8,128)(2,1)S(1)} %get-tuple-element.14.packed_ref, bf16[512,512]{1,0:T(8,128)(2,1)S(1)} %copy-done.1), custom_call_target="tpu_custom_call" | custom-call | flops 1610612736 | bytes 6291456 | tf_op jit(solution)/shard_map/own/pallas_call | solution.py:138
  62.7 0.3 collective-permute-done.1.refs_0_
  63.0 1.5 %collective-permute-done.2.refs_1_ = f32[256,1024]{1,0:T(8,128)S(1)} collective-permute-done((f32[256,1024]{1,0:T(8,128)S(1)}, f32[256,1024]{1,0:T(8,128)S(1)}, u32[]{:S(2)}, u32[]{:S(2)}) %collective-permute-start.2) | collective-permute-done | bytes 1048608 | tf_op jit(solution)/shard_map/ppermute | solution.py:259
  64.5 0.7 code.1
  65.2 23.2 %all_to_all.17.got_ref = s16[64,8,1024]{2,1,0:T(8,128)(2,1)S(1)} all-to-all(s16[64,8,1024]{2,1,0:T(8,128)(2,1)S(1)} %code.1), channel_id=1, replica_groups={{0,2,4,6,8,10,12,14,16,18,20,22,24,26,28,30,32,34,36,38,40,42,44,46,48,..., dimensions={0} | all-to-all | bytes 2097152 | tf_op jit(solution)/shard_map/all_to_all | solution.py:264
  88.4 1.1 %finish.1 = f32[8,1024]{1,0:T(8,128)} custom-call(s32[1]{0:T(128)} %bitcast.me_ref, s16[64,8,1024]{2,1,0:T(8,128)(2,1)S(1)} %all_to_all.17.got_ref), custom_call_target="tpu_custom_call" | custom-call | tf_op jit(solution)/shard_map/finish/pallas_call | solution.py:230
  (1 shorter events, 0.0 us)
Async XLA Ops:
  0.0 16.3 %slice-start = ((s8[8388608]{0:T(1024)(128)(4,1)}), s8[4194304]{0:T(1024)(128)(4,1)S(1)}, s32[]{:S(2)}) async-start(s8[8388608]{0:T(1024)(128)(4,1)} %bitcast.4), calls=%async_computation.3 | async-start | bytes 8388608
  0.0 16.3 %slice-start.1 = ((s8[8388608]{0:T(1024)(128)(4,1)}), s8[4194304]{0:T(1024)(128)(4,1)S(1)}, s32[]{:S(2)}) async-start(s8[8388608]{0:T(1024)(128)(4,1)} %bitcast.4), calls=%async_computation.4 | async-start | bytes 8388608
  0.0 16.3 %copy-start = (s32[1,1,16]{2,1,0:T(1,128)S(1)}, s32[1,1,16]{2,1,0:T(1,128)}, u32[]{:S(2)}) copy-start(s32[1,1,16]{2,1,0:T(1,128)} %param.5) | copy-start | bytes 196
  14.7 1.5 %collective-permute-start = (bf16[8,64,256]{2,1,0:T(8,128)(2,1)S(1)}, bf16[8,64,256]{2,1,0:T(8,128)(2,1)S(1)}, u32[]{:S(2)}, u32[]{:S(2)}) collective-permute-start(bf16[8,64,256]{2,1,0:T(8,128)(2,1)S(1)} %all_to_all.15.mine_ref), channel_id=1, source_target_pairs={{0,1},{1,0},{2,3},{3,2},{4,5},{5,4},{6,7},{7,6},{8,9},{9,8},{10,11... | collective-permute-start | bytes 786440 | tf_op jit(solution)/shard_map/ppermute | solution.py:251
  20.1 37.9 %copy-start.1 = (bf16[512,512]{1,0:T(8,128)(2,1)S(1)}, bf16[512,512]{1,0:T(8,128)(2,1)}, u32[]{:S(2)}) copy-start(bf16[512,512]{1,0:T(8,128)(2,1)} %metric_ref.3) | copy-start | bytes 1572868
  60.3 2.7 %collective-permute-start.1 = (f32[256,1024]{1,0:T(8,128)S(1)}, f32[256,1024]{1,0:T(8,128)S(1)}, u32[]{:S(2)}, u32[]{:S(2)}) collective-permute-start(f32[256,1024]{1,0:T(8,128)S(1)} %get-tuple-element.15), channel_id=1, source_target_pairs={{0,1},{1,0},{2,3},{3,2},{4,5},{5,4},{6,7},{7,6},{8,9},{9,8},{10,11... | collective-permute-start | bytes 3145736 | tf_op jit(solution)/shard_map/ppermute | solution.py:259
  60.3 4.1 %collective-permute-start.2 = (f32[256,1024]{1,0:T(8,128)S(1)}, f32[256,1024]{1,0:T(8,128)S(1)}, u32[]{:S(2)}, u32[]{:S(2)}) collective-permute-start(f32[256,1024]{1,0:T(8,128)S(1)} %get-tuple-element.16), channel_id=1, source_target_pairs={{0,1},{1,0},{2,3},{3,2},{4,5},{5,4},{6,7},{7,6},{8,9},{9,8},{10,11... | collective-permute-start | bytes 3145736 | tf_op jit(solution)/shard_map/ppermute | solution.py:259

commit v10 on v9

--- a/solution.py
+++ b/solution.py
@@ -102,6 +102,12 @@
             out_ref[:, at : at + lanes] = both
 
 
+def coded(term, axis):
+    largest = jnp.max(jnp.abs(term), axis=axis, keepdims=True)
+    code = jnp.ceil(jnp.log2(jnp.maximum(largest, 1e-33)) * 256.0)
+    return code, term * (jnp.exp2(code * (-1.0 / 256.0)) * TOP)
+
+
 def term_of(core, first, count, packed_ref, metric_ref):
     width = metric_ref.shape[0]
     orbitals = packed_ref.shape[1] // width
@@ -119,12 +125,14 @@
     return lax.dot_general(fit, packed_ref[...], NT, preferred_element_type=F32)
 
 
-def partner_kernel(core_ref, coef_ref, metric_ref, packed_ref, *out_refs):
+def partner_kernel(core_ref, coef_ref, metric_ref, packed_ref, out_ref):
     pack(coef_ref, packed_ref)
     term = term_of(1 - core_ref[0], 0, packed_ref.shape[0], packed_ref, metric_ref)
-    rows = out_refs[0].shape[0]
-    for k, out_ref in enumerate(out_refs):
-        out_ref[...] = term[k * rows : (k + 1) * rows]
+    columns = term.shape[1]
+    code, scaled = coded(term, 1)
+    out_ref[:, :columns] = jnp.round(scaled).astype(jnp.int32).astype(jnp.int16)
+    tail = (term.shape[0], out_ref.shape[1] - columns)
+    out_ref[:, columns:] = jnp.broadcast_to(code.astype(jnp.int32), tail).astype(jnp.int16)
 
 
 def own_kernel(core_ref, packed_ref, metric_ref, out_ref):
@@ -146,13 +154,9 @@
     )(core, coef, metric)
 
 
-def code_kernel(core_ref, sum_ref, *refs):
-    *part_refs, out_ref, held, sems = refs
-    copies = [
-        pltpu.make_async_copy(ref, held.at[k], sems.at[k]) for k, ref in enumerate(part_refs)
-    ]
-    for copy in copies:
-        copy.start()
+def code_kernel(core_ref, sum_ref, other_ref, out_ref, held, sem):
+    copy = pltpu.make_async_copy(other_ref, held, sem)
+    copy.start()
     core = core_ref[0]
     blocks, rows, columns = out_ref.shape
     lanes = 128
@@ -163,17 +167,14 @@
     column = lax.broadcasted_iota(jnp.int32, shape, 2) - rows * (2 * block + core)
     first = (column == 0) & (row > 0)
     second = (column == 1) & (row == rows - 1)
-    groups = blocks // group
-    for g in range(groups):
-        k, at = divmod(g, groups // len(copies))
-        if at == 0:
-            copies[k].wait()
-        term = sum_ref[g * group * rows : (g + 1) * group * rows, :]
-        term += held[k, at * group * rows : (at + 1) * group * rows, :]
+    copy.wait()
+    for g in range(blocks // group):
+        some = slice(g * group * rows, (g + 1) * group * rows)
+        other = held[some, :columns].astype(jnp.int32).astype(F32)
+        power = held[some, columns : columns + 1].astype(jnp.int32).astype(F32)
+        term = sum_ref[some, :] + other * (jnp.exp2(power * (1.0 / 256.0)) * (1.0 / TOP))
         term = term.reshape(group, rows, columns)
-        largest = jnp.max(jnp.abs(term), axis=2, keepdims=True)
-        code = jnp.ceil(jnp.log2(jnp.maximum(largest, 1e-33)) * 256.0)
-        scaled = term * (jnp.exp2(code * (-1.0 / 256.0)) * TOP)
+        code, scaled = coded(term, 2)
         part = scaled[:, :, g * lanes : (g + 1) * lanes]
         part = jnp.where(first, code, jnp.where(second, code[:, 0:1], part))
         scaled = [scaled[:, :, : g * lanes], part, scaled[:, :, (g + 1) * lanes :]]
@@ -181,22 +182,18 @@
         out_ref[g * group : (g + 1) * group] = jnp.round(scaled).astype(jnp.int32).astype(jnp.int16)
 
 
-def code_of(core, total, parts, blocks):
+def code_of(core, total, other, blocks):
     rows, columns = total.shape
-    count = len(parts)
     return pl.pallas_call(
         code_kernel,
         out_shape=jax.ShapeDtypeStruct((blocks, rows // blocks, columns), jnp.int16),
-        in_specs=[SMEM, VMEM] + [pl.BlockSpec(memory_space=pl.ANY)] * count,
+        in_specs=[SMEM, VMEM, pl.BlockSpec(memory_space=pl.ANY)],
         out_specs=VMEM,
-        scratch_shapes=[
-            pltpu.VMEM((count, *parts[0].shape), F32),
-            pltpu.SemaphoreType.DMA((count,)),
-        ],
+        scratch_shapes=[pltpu.VMEM(other.shape, jnp.int16), pltpu.SemaphoreType.DMA],
         compiler_params=params(16),
         cost_estimate=pl.CostEstimate(flops=0, bytes_accessed=6 << 20, transcendentals=0),
         name="code",
-    )(core, total, *parts)
+    )(core, total, other)
 
 
 def finish_kernel(me_ref, got_ref, out_ref):
@@ -254,12 +251,12 @@
     coef = coef.reshape(n_wide, n_narrow, 2, mu_local // 2, 2 * ri_local)
     mu = n_narrow * mu_local
     packed = jax.ShapeDtypeStruct((mu, 2 * metric.shape[0]), BF16)
-    part = jax.ShapeDtypeStruct((mu // 4, mu), F32)
-    packed, *parts = term_call(partner_kernel, "partner", (packed, part, part), core, coef, metric)
-    parts = [lax.ppermute(part, "narrow", swap) for part in parts]
+    part = jax.ShapeDtypeStruct((mu // 2, mu + 128), jnp.int16)
+    packed, other = term_call(partner_kernel, "partner", (packed, part), core, coef, metric)
+    other = lax.ppermute(other, "narrow", swap)
     total = jax.ShapeDtypeStruct((mu // 2, mu), F32)
     total = term_call(own_kernel, "own", total, core, packed, metric)
-    parts = code_of(core, total, parts, devices // 2)
+    parts = code_of(core, total, other, devices // 2)
     sides = [[j for j in range(devices) if j % 2 == c] for c in (0, 1)]
     got = lax.all_to_all(parts, BOTH, 0, 0, tiled=True, axis_index_groups=sides)
     return finish(me, got)

time: 89.7 us -> 89.1 us (level)
    ppermute x2 -> x1, waiting for transfers between devices: 1.8 us -> 0.99 us  [body(): other = lax.ppermute(other, 'narrow', swap)]
  transfers between devices with their start and end apart: 3 -> 2, of which waited for: 3 -> 2; matrix products, arithmetic and copies ran while one was open for 0% -> 0% of each run, Pallas kernels for 2% -> 2%
where the time goes in v10:
time: 89.1 us; the launch traced here: 88.9 us
  blocking collectives  74.7 us (84%)
  Pallas kernels  11.5 us (13%)
  waiting for transfers between devices  2.52 us (3%)
    all_to_all x1, blocking collectives, body(): coef = lax.all_to_all(parts, BOTH, 0, 0, tiled=True)  37.9 us
    all_to_all x1, blocking collectives, body(): got = lax.all_to_all(parts, BOTH, 0, 0, tiled=True, axis_index_groups=sides)  23.2 us
    all_to_all x1, blocking collectives, body(): lax.all_to_all(copies, 'narrow', 0, 0, tiled=True, axis_index_groups=sides)  13.6 us
    pallas_call x2, Pallas kernels, term_call(): pl.pallas_call(kernel, out_shape=out_shape, in_specs=[SMEM, VMEM, VMEM],...  4.25 us
    pallas_call x1, Pallas kernels, coeffs_of(): pl.pallas_call(functools.partial(coeffs_kernel, step), out_shape=jax.Shap...  3.83 us
  transfers between devices with their start and end apart: 2, of which 2 were waited for; matrix products, arithmetic and copies ran while one was open for 0% of the time, Pallas kernels for 2%

profile of v10, /device:TPU:0, one launch (start us, length us, event | category | flops | bytes accessed | tf_op | source)
XLA Modules:
  0.0 88.9 jit_solution(7857231643914306800)
XLA Ops:
  0.0 0.0 slice-start
  0.0 0.0 slice-start.1
  0.0 0.0 copy-start
  0.0 1.1 %copies.1 = bf16[8,64,256]{2,1,0:T(8,128)(2,1)S(1)} custom-call(bf16[64,256]{1,0:T(8,128)(2,1)} %orbitals_ref), custom_call_target="tpu_custom_call" | custom-call | flops 10000000000 | bytes 41943040 | tf_op jit(solution)/shard_map/copies/pallas_call | solution.py:35
  1.1 13.6 %all_to_all.15.mine_ref = bf16[8,64,256]{2,1,0:T(8,128)(2,1)S(1)} all-to-all(bf16[8,64,256]{2,1,0:T(8,128)(2,1)S(1)} %copies.1), channel_id=1, replica_groups={{0,2,4,6,8,10,12,14},{1,3,5,7,9,11,13,15},{16,18,20,22,24,26,28,30},{17..., dimensions={0} | all-to-all | bytes 524288 | tf_op jit(solution)/shard_map/all_to_all | solution.py:247
  14.7 0.0 collective-permute-start
  14.7 1.5 %collective-permute-done.other_ref = bf16[8,64,256]{2,1,0:T(8,128)(2,1)S(1)} collective-permute-done((bf16[8,64,256]{2,1,0:T(8,128)(2,1)S(1)}, bf16[8,64,256]{2,1,0:T(8,128)(2,1)S(1)}, u32[]{:S(2)}, u32[]{:S(2)}) %collective-permute-start) | collective-permute-done | bytes 262176 | tf_op jit(solution)/shard_map/ppermute | solution.py:248
  16.3 0.0 slice-done
  16.3 0.0 slice-done.1
  16.3 0.0 copy-done
  16.3 3.8 %coeffs.1 = bf16[128,64,128]{2,1,0:T(8,128)(2,1)S(1)} custom-call(s32[1]{0:T(128)} %bitcast.1.core_ref, s32[16]{0:T(128)S(1)} %bitcast.7, bf16[8,64,256]{2,1,0:T(8,128)(2,1)S(1)} %all_to_all.15.mine_ref, bf16[8,64,256]{2,1,0:T(8,128)(2,1)S(1)} %collective-permute-done.other_ref, bf16[64,64,1024]{2,1,0:T(8,128)(2,1)S(1)} %bitcast.5), custom_call_target="tpu_custom_call" | custom-call | flops 2147483648 | bytes 8388608 | tf_op jit(solution)/shard_map/coeffs/pallas_call | solution.py:76
  20.1 0.0 copy-start.1
  20.2 37.9 %all_to_all.16 = bf16[128,64,128]{2,1,0:T(8,128)(2,1)S(1)} all-to-all(bf16[128,64,128]{2,1,0:T(8,128)(2,1)S(1)} %coeffs.1), channel_id=1, replica_groups=mesh['wide'=8,'narrow'=16] {'wide','narrow'}, dimensions={0} | all-to-all | bytes 4194304 | tf_op jit(solution)/shard_map/all_to_all | solution.py:250
  58.0 0.0 copy-done.1
  58.0 2.4 %partner.1 = (bf16[1024,1024]{1,0:T(8,128)(2,1)S(1)}, s16[512,1152]{1,0:T(8,128)(2,1)S(1)}) custom-call(s32[1]{0:T(128)} %bitcast.1.core_ref, bf16[8,16,2,32,128]{4,3,2,1,0:T(8,128)(2,1)S(1)} %bitcast.6, bf16[512,512]{1,0:T(8,128)(2,1)S(1)} %copy-done.1), custom_call_target="tpu_custom_call" | custom-call | flops 1610612736 | bytes 6291456 | tf_op jit(solution)/shard_map/partner/pallas_call | solution.py:146
  60.5 0.1 collective-permute-start.1
  60.6 1.8 %own.1.sum_ref = f32[512,1024]{1,0:T(8,128)S(1)} custom-call(s32[1]{0:T(128)} %bitcast.1.core_ref, bf16[1024,1024]{1,0:T(8,128)(2,1)S(1)} %get-tuple-element.13.packed_ref, bf16[512,512]{1,0:T(8,128)(2,1)S(1)} %copy-done.1), custom_call_target="tpu_custom_call" | custom-call | flops 1610612736 | bytes 6291456 | tf_op jit(solution)/shard_map/own/pallas_call | solution.py:146
  62.4 1.0 %collective-permute-done.1.other_ref = s16[512,1152]{1,0:T(8,128)(2,1)S(1)} collective-permute-done((s16[512,1152]{1,0:T(8,128)(2,1)S(1)}, s16[512,1152]{1,0:T(8,128)(2,1)S(1)}, u32[]{:S(2)}, u32[]{:S(2)}) %collective-permute-start.1) | collective-permute-done | bytes 1179680 | tf_op jit(solution)/shard_map/ppermute | solution.py:256
  63.4 1.2 %code.1 = s16[64,8,1024]{2,1,0:T(8,128)(2,1)S(1)} custom-call(s32[1]{0:T(128)} %bitcast.1.core_ref, f32[512,1024]{1,0:T(8,128)S(1)} %own.1.sum_ref, s16[512,1152]{1,0:T(8,128)(2,1)S(1)} %collective-permute-done.1.other_ref), custom_call_target="tpu_custom_call" | custom-call | bytes 6291456 | tf_op jit(solution)/shard_map/code/pallas_call | solution.py:187
  64.6 23.2 %all_to_all.17.got_ref = s16[64,8,1024]{2,1,0:T(8,128)(2,1)S(1)} all-to-all(s16[64,8,1024]{2,1,0:T(8,128)(2,1)S(1)} %code.1), channel_id=1, replica_groups={{0,2,4,6,8,10,12,14,16,18,20,22,24,26,28,30,32,34,36,38,40,42,44,46,48,..., dimensions={0} | all-to-all | bytes 2097152 | tf_op jit(solution)/shard_map/all_to_all | solution.py:261
  87.8 1.1 %finish.1 = f32[8,1024]{1,0:T(8,128)} custom-call(s32[1]{0:T(128)} %bitcast.me_ref, s16[64,8,1024]{2,1,0:T(8,128)(2,1)S(1)} %all_to_all.17.got_ref), custom_call_target="tpu_custom_call" | custom-call | tf_op jit(solution)/shard_map/finish/pallas_call | solution.py:227
  (1 shorter events, 0.0 us)
Async XLA Ops:
  0.0 16.3 %slice-start = ((s8[8388608]{0:T(1024)(128)(4,1)}), s8[4194304]{0:T(1024)(128)(4,1)S(1)}, s32[]{:S(2)}) async-start(s8[8388608]{0:T(1024)(128)(4,1)} %bitcast.4), calls=%async_computation.3 | async-start | bytes 8388608
  0.0 16.3 %slice-start.1 = ((s8[8388608]{0:T(1024)(128)(4,1)}), s8[4194304]{0:T(1024)(128)(4,1)S(1)}, s32[]{:S(2)}) async-start(s8[8388608]{0:T(1024)(128)(4,1)} %bitcast.4), calls=%async_computation.4 | async-start | bytes 8388608
  0.0 16.3 %copy-start = (s32[1,1,16]{2,1,0:T(1,128)S(1)}, s32[1,1,16]{2,1,0:T(1,128)}, u32[]{:S(2)}) copy-start(s32[1,1,16]{2,1,0:T(1,128)} %param.5) | copy-start | bytes 196
  14.7 1.5 %collective-permute-start = (bf16[8,64,256]{2,1,0:T(8,128)(2,1)S(1)}, bf16[8,64,256]{2,1,0:T(8,128)(2,1)S(1)}, u32[]{:S(2)}, u32[]{:S(2)}) collective-permute-start(bf16[8,64,256]{2,1,0:T(8,128)(2,1)S(1)} %all_to_all.15.mine_ref), channel_id=1, source_target_pairs={{0,1},{1,0},{2,3},{3,2},{4,5},{5,4},{6,7},{7,6},{8,9},{9,8},{10,11... | collective-permute-start | bytes 786440 | tf_op jit(solution)/shard_map/ppermute | solution.py:248
  20.1 37.9 %copy-start.1 = (bf16[512,512]{1,0:T(8,128)(2,1)S(1)}, bf16[512,512]{1,0:T(8,128)(2,1)}, u32[]{:S(2)}) copy-start(bf16[512,512]{1,0:T(8,128)(2,1)} %metric_ref.3) | copy-start | bytes 1572868
  60.5 2.9 %collective-permute-start.1 = (s16[512,1152]{1,0:T(8,128)(2,1)S(1)}, s16[512,1152]{1,0:T(8,128)(2,1)S(1)}, u32[]{:S(2)}, u32[]{:S(2)}) collective-permute-start(s16[512,1152]{1,0:T(8,128)(2,1)S(1)} %get-tuple-element.14), channel_id=1, source_target_pairs={{0,1},{1,0},{2,3},{3,2},{4,5},{5,4},{6,7},{7,6},{8,9},{9,8},{10,11... | collective-permute-start | bytes 3538952 | tf_op jit(solution)/shard_map/ppermute | solution.py:256

commit v11 on v10

--- a/solution.py
+++ b/solution.py
@@ -154,9 +154,7 @@
     )(core, coef, metric)
 
 
-def code_kernel(core_ref, sum_ref, other_ref, out_ref, held, sem):
-    copy = pltpu.make_async_copy(other_ref, held, sem)
-    copy.start()
+def code_kernel(core_ref, sum_ref, held, out_ref):
     core = core_ref[0]
     blocks, rows, columns = out_ref.shape
     lanes = 128
@@ -167,7 +165,6 @@
     column = lax.broadcasted_iota(jnp.int32, shape, 2) - rows * (2 * block + core)
     first = (column == 0) & (row > 0)
     second = (column == 1) & (row == rows - 1)
-    copy.wait()
     for g in range(blocks // group):
         some = slice(g * group * rows, (g + 1) * group * rows)
         other = held[some, :columns].astype(jnp.int32).astype(F32)
@@ -187,9 +184,8 @@
     return pl.pallas_call(
         code_kernel,
         out_shape=jax.ShapeDtypeStruct((blocks, rows // blocks, columns), jnp.int16),
-        in_specs=[SMEM, VMEM, pl.BlockSpec(memory_space=pl.ANY)],
+        in_specs=[SMEM, VMEM, VMEM],
         out_specs=VMEM,
-        scratch_shapes=[pltpu.VMEM(other.shape, jnp.int16), pltpu.SemaphoreType.DMA],
         compiler_params=params(16),
         cost_estimate=pl.CostEstimate(flops=0, bytes_accessed=6 << 20, transcendentals=0),
         name="code",

time: 89.1 us -> 88.8 us (level)
  no operation moved by 1% of the time
where the time goes in v11:
time: 88.8 us; the launch traced here: 88.6 us
  blocking collectives  74.7 us (84%)
  Pallas kernels  11.2 us (13%)
  waiting for transfers between devices  2.52 us (3%)
    all_to_all x1, blocking collectives, body(): coef = lax.all_to_all(parts, BOTH, 0, 0, tiled=True)  37.9 us
    all_to_all x1, blocking collectives, body(): got = lax.all_to_all(parts, BOTH, 0, 0, tiled=True, axis_index_groups=sides)  23.2 us
    all_to_all x1, blocking collectives, body(): lax.all_to_all(copies, 'narrow', 0, 0, tiled=True, axis_index_groups=sides)  13.6 us
    pallas_call x2, Pallas kernels, term_call(): pl.pallas_call(kernel, out_shape=out_shape, in_specs=[SMEM, VMEM, VMEM],...  4.25 us
    pallas_call x1, Pallas kernels, coeffs_of(): pl.pallas_call(functools.partial(coeffs_kernel, step), out_shape=jax.Shap...  3.83 us
  transfers between devices with their start and end apart: 2, of which 2 were waited for; matrix products, arithmetic and copies ran while one was open for 0% of the time, Pallas kernels for 2%

profile of v11, /device:TPU:0, one launch (start us, length us, event | category | flops | bytes accessed | tf_op | source)
XLA Modules:
  0.0 88.6 jit_solution(7203722412378372680)
XLA Ops:
  0.0 0.0 slice-start
  0.0 0.0 slice-start.1
  0.0 0.0 copy-start
  0.0 1.1 %copies.1 = bf16[8,64,256]{2,1,0:T(8,128)(2,1)S(1)} custom-call(bf16[64,256]{1,0:T(8,128)(2,1)} %orbitals_ref), custom_call_target="tpu_custom_call" | custom-call | flops 10000000000 | bytes 41943040 | tf_op jit(solution)/shard_map/copies/pallas_call | solution.py:35
  1.1 13.6 %all_to_all.15.mine_ref = bf16[8,64,256]{2,1,0:T(8,128)(2,1)S(1)} all-to-all(bf16[8,64,256]{2,1,0:T(8,128)(2,1)S(1)} %copies.1), channel_id=1, replica_groups={{0,2,4,6,8,10,12,14},{1,3,5,7,9,11,13,15},{16,18,20,22,24,26,28,30},{17..., dimensions={0} | all-to-all | bytes 524288 | tf_op jit(solution)/shard_map/all_to_all | solution.py:243
  14.7 0.0 collective-permute-start
  14.7 1.5 %collective-permute-done.other_ref = bf16[8,64,256]{2,1,0:T(8,128)(2,1)S(1)} collective-permute-done((bf16[8,64,256]{2,1,0:T(8,128)(2,1)S(1)}, bf16[8,64,256]{2,1,0:T(8,128)(2,1)S(1)}, u32[]{:S(2)}, u32[]{:S(2)}) %collective-permute-start) | collective-permute-done | bytes 262176 | tf_op jit(solution)/shard_map/ppermute | solution.py:244
  16.3 0.0 slice-done
  16.3 0.0 slice-done.1
  16.3 0.0 copy-done
  16.3 3.8 %coeffs.1 = bf16[128,64,128]{2,1,0:T(8,128)(2,1)S(1)} custom-call(s32[1]{0:T(128)} %bitcast.1.core_ref, s32[16]{0:T(128)S(1)} %bitcast.7, bf16[8,64,256]{2,1,0:T(8,128)(2,1)S(1)} %all_to_all.15.mine_ref, bf16[8,64,256]{2,1,0:T(8,128)(2,1)S(1)} %collective-permute-done.other_ref, bf16[64,64,1024]{2,1,0:T(8,128)(2,1)S(1)} %bitcast.5), custom_call_target="tpu_custom_call" | custom-call | flops 2147483648 | bytes 8388608 | tf_op jit(solution)/shard_map/coeffs/pallas_call | solution.py:76
  20.1 0.0 copy-start.1
  20.2 37.9 %all_to_all.16 = bf16[128,64,128]{2,1,0:T(8,128)(2,1)S(1)} all-to-all(bf16[128,64,128]{2,1,0:T(8,128)(2,1)S(1)} %coeffs.1), channel_id=1, replica_groups=mesh['wide'=8,'narrow'=16] {'wide','narrow'}, dimensions={0} | all-to-all | bytes 4194304 | tf_op jit(solution)/shard_map/all_to_all | solution.py:246
  58.0 0.0 copy-done.1
  58.0 2.4 %partner.1 = (bf16[1024,1024]{1,0:T(8,128)(2,1)S(1)}, s16[512,1152]{1,0:T(8,128)(2,1)S(1)}) custom-call(s32[1]{0:T(128)} %bitcast.1.core_ref, bf16[8,16,2,32,128]{4,3,2,1,0:T(8,128)(2,1)S(1)} %bitcast.6, bf16[512,512]{1,0:T(8,128)(2,1)S(1)} %copy-done.1), custom_call_target="tpu_custom_call" | custom-call | flops 1610612736 | bytes 6291456 | tf_op jit(solution)/shard_map/partner/pallas_call | solution.py:146
  60.5 0.1 collective-permute-start.1
  60.6 1.8 %own.1.sum_ref = f32[512,1024]{1,0:T(8,128)S(1)} custom-call(s32[1]{0:T(128)} %bitcast.1.core_ref, bf16[1024,1024]{1,0:T(8,128)(2,1)S(1)} %get-tuple-element.13.packed_ref, bf16[512,512]{1,0:T(8,128)(2,1)S(1)} %copy-done.1), custom_call_target="tpu_custom_call" | custom-call | flops 1610612736 | bytes 6291456 | tf_op jit(solution)/shard_map/own/pallas_call | solution.py:146
  62.4 1.0 %collective-permute-done.1.held = s16[512,1152]{1,0:T(8,128)(2,1)S(1)} collective-permute-done((s16[512,1152]{1,0:T(8,128)(2,1)S(1)}, s16[512,1152]{1,0:T(8,128)(2,1)S(1)}, u32[]{:S(2)}, u32[]{:S(2)}) %collective-permute-start.1) | collective-permute-done | bytes 1179680 | tf_op jit(solution)/shard_map/ppermute | solution.py:252
  63.4 0.9 %code.1 = s16[64,8,1024]{2,1,0:T(8,128)(2,1)S(1)} custom-call(s32[1]{0:T(128)} %bitcast.1.core_ref, f32[512,1024]{1,0:T(8,128)S(1)} %own.1.sum_ref, s16[512,1152]{1,0:T(8,128)(2,1)S(1)} %collective-permute-done.1.held), custom_call_target="tpu_custom_call" | custom-call | bytes 6291456 | tf_op jit(solution)/shard_map/code/pallas_call | solution.py:184
  64.3 23.2 %all_to_all.17.got_ref = s16[64,8,1024]{2,1,0:T(8,128)(2,1)S(1)} all-to-all(s16[64,8,1024]{2,1,0:T(8,128)(2,1)S(1)} %code.1), channel_id=1, replica_groups={{0,2,4,6,8,10,12,14,16,18,20,22,24,26,28,30,32,34,36,38,40,42,44,46,48,..., dimensions={0} | all-to-all | bytes 2097152 | tf_op jit(solution)/shard_map/all_to_all | solution.py:257
  87.5 1.1 %finish.1 = f32[8,1024]{1,0:T(8,128)} custom-call(s32[1]{0:T(128)} %bitcast.me_ref, s16[64,8,1024]{2,1,0:T(8,128)(2,1)S(1)} %all_to_all.17.got_ref), custom_call_target="tpu_custom_call" | custom-call | tf_op jit(solution)/shard_map/finish/pallas_call | solution.py:223
  (1 shorter events, 0.0 us)
Async XLA Ops:
  0.0 16.3 %slice-start = ((s8[8388608]{0:T(1024)(128)(4,1)}), s8[4194304]{0:T(1024)(128)(4,1)S(1)}, s32[]{:S(2)}) async-start(s8[8388608]{0:T(1024)(128)(4,1)} %bitcast.4), calls=%async_computation.3 | async-start | bytes 8388608
  0.0 16.3 %slice-start.1 = ((s8[8388608]{0:T(1024)(128)(4,1)}), s8[4194304]{0:T(1024)(128)(4,1)S(1)}, s32[]{:S(2)}) async-start(s8[8388608]{0:T(1024)(128)(4,1)} %bitcast.4), calls=%async_computation.4 | async-start | bytes 8388608
  0.0 16.3 %copy-start = (s32[1,1,16]{2,1,0:T(1,128)S(1)}, s32[1,1,16]{2,1,0:T(1,128)}, u32[]{:S(2)}) copy-start(s32[1,1,16]{2,1,0:T(1,128)} %param.5) | copy-start | bytes 196
  14.7 1.5 %collective-permute-start = (bf16[8,64,256]{2,1,0:T(8,128)(2,1)S(1)}, bf16[8,64,256]{2,1,0:T(8,128)(2,1)S(1)}, u32[]{:S(2)}, u32[]{:S(2)}) collective-permute-start(bf16[8,64,256]{2,1,0:T(8,128)(2,1)S(1)} %all_to_all.15.mine_ref), channel_id=1, source_target_pairs={{0,1},{1,0},{2,3},{3,2},{4,5},{5,4},{6,7},{7,6},{8,9},{9,8},{10,11... | collective-permute-start | bytes 786440 | tf_op jit(solution)/shard_map/ppermute | solution.py:244
  20.1 37.9 %copy-start.1 = (bf16[512,512]{1,0:T(8,128)(2,1)S(1)}, bf16[512,512]{1,0:T(8,128)(2,1)}, u32[]{:S(2)}) copy-start(bf16[512,512]{1,0:T(8,128)(2,1)} %metric_ref.3) | copy-start | bytes 1572868
  60.5 2.9 %collective-permute-start.1 = (s16[512,1152]{1,0:T(8,128)(2,1)S(1)}, s16[512,1152]{1,0:T(8,128)(2,1)S(1)}, u32[]{:S(2)}, u32[]{:S(2)}) collective-permute-start(s16[512,1152]{1,0:T(8,128)(2,1)S(1)} %get-tuple-element.14), channel_id=1, source_target_pairs={{0,1},{1,0},{2,3},{3,2},{4,5},{5,4},{6,7},{7,6},{8,9},{9,8},{10,11... | collective-permute-start | bytes 3538952 | tf_op jit(solution)/shard_map/ppermute | solution.py:252

commit v12 on v11

--- a/solution.py
+++ b/solution.py
@@ -125,14 +125,17 @@
     return lax.dot_general(fit, packed_ref[...], NT, preferred_element_type=F32)
 
 
-def partner_kernel(core_ref, coef_ref, metric_ref, packed_ref, out_ref):
+def partner_kernel(core_ref, coef_ref, metric_ref, packed_ref, *out_refs):
     pack(coef_ref, packed_ref)
     term = term_of(1 - core_ref[0], 0, packed_ref.shape[0], packed_ref, metric_ref)
     columns = term.shape[1]
     code, scaled = coded(term, 1)
-    out_ref[:, :columns] = jnp.round(scaled).astype(jnp.int32).astype(jnp.int16)
-    tail = (term.shape[0], out_ref.shape[1] - columns)
-    out_ref[:, columns:] = jnp.broadcast_to(code.astype(jnp.int32), tail).astype(jnp.int16)
+    tail = (term.shape[0], out_refs[0].shape[1] - columns)
+    scaled = jnp.concatenate([jnp.round(scaled), jnp.broadcast_to(code, tail)], axis=1)
+    scaled = scaled.astype(jnp.int32).astype(jnp.int16)
+    rows = out_refs[0].shape[0]
+    for k, out_ref in enumerate(out_refs):
+        out_ref[...] = scaled[k * rows : (k + 1) * rows]
 
 
 def own_kernel(core_ref, packed_ref, metric_ref, out_ref):
@@ -154,7 +157,7 @@
     )(core, coef, metric)
 
 
-def code_kernel(core_ref, sum_ref, held, out_ref):
+def code_kernel(core_ref, sum_ref, one_ref, two_ref, out_ref):
     core = core_ref[0]
     blocks, rows, columns = out_ref.shape
     lanes = 128
@@ -167,8 +170,11 @@
     second = (column == 1) & (row == rows - 1)
     for g in range(blocks // group):
         some = slice(g * group * rows, (g + 1) * group * rows)
-        other = held[some, :columns].astype(jnp.int32).astype(F32)
-        power = held[some, columns : columns + 1].astype(jnp.int32).astype(F32)
+        held = (one_ref, two_ref)[some.start // one_ref.shape[0]]
+        first_row = some.start % one_ref.shape[0]
+        there = slice(first_row, first_row + group * rows)
+        other = held[there, :columns].astype(jnp.int32).astype(F32)
+        power = held[there, columns : columns + 1].astype(jnp.int32).astype(F32)
         term = sum_ref[some, :] + other * (jnp.exp2(power * (1.0 / 256.0)) * (1.0 / TOP))
         term = term.reshape(group, rows, columns)
         code, scaled = coded(term, 2)
@@ -179,17 +185,17 @@
         out_ref[g * group : (g + 1) * group] = jnp.round(scaled).astype(jnp.int32).astype(jnp.int16)
 
 
-def code_of(core, total, other, blocks):
+def code_of(core, total, others, blocks):
     rows, columns = total.shape
     return pl.pallas_call(
         code_kernel,
         out_shape=jax.ShapeDtypeStruct((blocks, rows // blocks, columns), jnp.int16),
-        in_specs=[SMEM, VMEM, VMEM],
+        in_specs=[SMEM, VMEM, VMEM, VMEM],
         out_specs=VMEM,
         compiler_params=params(16),
         cost_estimate=pl.CostEstimate(flops=0, bytes_accessed=6 << 20, transcendentals=0),
         name="code",
-    )(core, total, other)
+    )(core, total, *others)
 
 
 def finish_kernel(me_ref, got_ref, out_ref):
@@ -247,12 +253,12 @@
     coef = coef.reshape(n_wide, n_narrow, 2, mu_local // 2, 2 * ri_local)
     mu = n_narrow * mu_local
     packed = jax.ShapeDtypeStruct((mu, 2 * metric.shape[0]), BF16)
-    part = jax.ShapeDtypeStruct((mu // 2, mu + 128), jnp.int16)
-    packed, other = term_call(partner_kernel, "partner", (packed, part), core, coef, metric)
-    other = lax.ppermute(other, "narrow", swap)
+    part = jax.ShapeDtypeStruct((mu // 4, mu + 128), jnp.int16)
+    packed, *others = term_call(partner_kernel, "partner", (packed, part, part), core, coef, metric)
+    others = [lax.ppermute(part, "narrow", swap) for part in others]
     total = jax.ShapeDtypeStruct((mu // 2, mu), F32)
     total = term_call(own_kernel, "own", total, core, packed, metric)
-    parts = code_of(core, total, other, devices // 2)
+    parts = code_of(core, total, others, devices // 2)
     sides = [[j for j in range(devices) if j % 2 == c] for c in (0, 1)]
     got = lax.all_to_all(parts, BOTH, 0, 0, tiled=True, axis_index_groups=sides)
     return finish(me, got)

time: 88.8 us -> 88.8 us (level)
  transfers between devices with their start and end apart: 2 -> 3, of which waited for: 2 -> 2; matrix products, arithmetic and copies ran while one was open for 0% -> 0% of each run, Pallas kernels for 2% -> 2%
where the time goes in v12:
time: 88.8 us; the launch traced here: 88.6 us
  blocking collectives  74.7 us (84%)
  Pallas kernels  11.2 us (13%)
  waiting for transfers between devices  2.02 us (2%)
    all_to_all x1, blocking collectives, body(): coef = lax.all_to_all(parts, BOTH, 0, 0, tiled=True)  37.9 us
    all_to_all x1, blocking collectives, body(): got = lax.all_to_all(parts, BOTH, 0, 0, tiled=True, axis_index_groups=sides)  23.2 us
    all_to_all x1, blocking collectives, body(): lax.all_to_all(copies, 'narrow', 0, 0, tiled=True, axis_index_groups=sides)  13.6 us
    pallas_call x2, Pallas kernels, term_call(): pl.pallas_call(kernel, out_shape=out_shape, in_specs=[SMEM, VMEM, VMEM],...  4.23 us
    pallas_call x1, Pallas kernels, coeffs_of(): pl.pallas_call(functools.partial(coeffs_kernel, step), out_shape=jax.Shap...  3.83 us
  transfers between devices with their start and end apart: 3, of which 2 were waited for; matrix products, arithmetic and copies ran while one was open for 0% of the time, Pallas kernels for 2%

profile of v12, /device:TPU:0, one launch (start us, length us, event | category | flops | bytes accessed | tf_op | source)
XLA Modules:
  0.0 88.6 jit_solution(3804944862905508546)
XLA Ops:
  0.0 0.0 slice-start
  0.0 0.0 slice-start.1
  0.0 0.0 copy-start
  0.0 1.1 %copies.1 = bf16[8,64,256]{2,1,0:T(8,128)(2,1)S(1)} custom-call(bf16[64,256]{1,0:T(8,128)(2,1)} %orbitals_ref), custom_call_target="tpu_custom_call" | custom-call | flops 10000000000 | bytes 41943040 | tf_op jit(solution)/shard_map/copies/pallas_call | solution.py:35
  1.1 13.6 %all_to_all.15.mine_ref = bf16[8,64,256]{2,1,0:T(8,128)(2,1)S(1)} all-to-all(bf16[8,64,256]{2,1,0:T(8,128)(2,1)S(1)} %copies.1), channel_id=1, replica_groups={{0,2,4,6,8,10,12,14},{1,3,5,7,9,11,13,15},{16,18,20,22,24,26,28,30},{17..., dimensions={0} | all-to-all | bytes 524288 | tf_op jit(solution)/shard_map/all_to_all | solution.py:249
  14.7 0.0 collective-permute-start
  14.7 1.5 %collective-permute-done.other_ref = bf16[8,64,256]{2,1,0:T(8,128)(2,1)S(1)} collective-permute-done((bf16[8,64,256]{2,1,0:T(8,128)(2,1)S(1)}, bf16[8,64,256]{2,1,0:T(8,128)(2,1)S(1)}, u32[]{:S(2)}, u32[]{:S(2)}) %collective-permute-start) | collective-permute-done | bytes 262176 | tf_op jit(solution)/shard_map/ppermute | solution.py:250
  16.3 0.0 slice-done
  16.3 0.0 slice-done.1
  16.3 0.0 copy-done
  16.3 3.8 %coeffs.1 = bf16[128,64,128]{2,1,0:T(8,128)(2,1)S(1)} custom-call(s32[1]{0:T(128)} %bitcast.1.core_ref, s32[16]{0:T(128)S(1)} %bitcast.7, bf16[8,64,256]{2,1,0:T(8,128)(2,1)S(1)} %all_to_all.15.mine_ref, bf16[8,64,256]{2,1,0:T(8,128)(2,1)S(1)} %collective-permute-done.other_ref, bf16[64,64,1024]{2,1,0:T(8,128)(2,1)S(1)} %bitcast.5), custom_call_target="tpu_custom_call" | custom-call | flops 2147483648 | bytes 8388608 | tf_op jit(solution)/shard_map/coeffs/pallas_call | solution.py:76
  20.1 0.0 copy-start.1
  20.2 37.9 %all_to_all.16 = bf16[128,64,128]{2,1,0:T(8,128)(2,1)S(1)} all-to-all(bf16[128,64,128]{2,1,0:T(8,128)(2,1)S(1)} %coeffs.1), channel_id=1, replica_groups=mesh['wide'=8,'narrow'=16] {'wide','narrow'}, dimensions={0} | all-to-all | bytes 4194304 | tf_op jit(solution)/shard_map/all_to_all | solution.py:252
  58.0 0.0 copy-done.1
  58.0 2.4 %partner.1 = (bf16[1024,1024]{1,0:T(8,128)(2,1)S(1)}, s16[256,1152]{1,0:T(8,128)(2,1)S(1)}, s16[256,1152]{1,0:T(8,128)(2,1)S(1)}) custom-call(s32[1]{0:T(128)} %bitcast.1.core_ref, bf16[8,16,2,32,128]{4,3,2,1,0:T(8,128)(2,1)S(1)} %bitcast.6, bf16[512,512]{1,0:T(8,128)(2,1)S(1)} %copy-done.1), custom_call_target="tpu_custom_call" | custom-call | flops 1610612736 | bytes 6291456 | tf_op jit(solution)/shard_map/partner/pallas_call | solution.py:149
  60.4 0.1 collective-permute-start.1
  60.5 0.5 collective-permute-start.2
  61.0 1.8 %own.1.sum_ref = f32[512,1024]{1,0:T(8,128)S(1)} custom-call(s32[1]{0:T(128)} %bitcast.1.core_ref, bf16[1024,1024]{1,0:T(8,128)(2,1)S(1)} %get-tuple-element.14.packed_ref, bf16[512,512]{1,0:T(8,128)(2,1)S(1)} %copy-done.1), custom_call_target="tpu_custom_call" | custom-call | flops 1610612736 | bytes 6291456 | tf_op jit(solution)/shard_map/own/pallas_call | solution.py:149
  62.9 0.0 collective-permute-done.1.one_ref
  62.9 0.5 collective-permute-done.2.two_ref
  63.4 0.9 %code.1 = s16[64,8,1024]{2,1,0:T(8,128)(2,1)S(1)} custom-call(s32[1]{0:T(128)} %bitcast.1.core_ref, f32[512,1024]{1,0:T(8,128)S(1)} %own.1.sum_ref, s16[256,1152]{1,0:T(8,128)(2,1)S(1)} %collective-permute-done.1.one_ref, s16[256,1152]{1,0:T(8,128)(2,1)S(1)} %collective-permute-done.2.two_ref), custom_call_target="tpu_custom_call" | custom-call | bytes 6291456 | tf_op jit(solution)/shard_map/code/pallas_call | solution.py:190
  64.3 23.2 %all_to_all.17.got_ref = s16[64,8,1024]{2,1,0:T(8,128)(2,1)S(1)} all-to-all(s16[64,8,1024]{2,1,0:T(8,128)(2,1)S(1)} %code.1), channel_id=1, replica_groups={{0,2,4,6,8,10,12,14,16,18,20,22,24,26,28,30,32,34,36,38,40,42,44,46,48,..., dimensions={0} | all-to-all | bytes 2097152 | tf_op jit(solution)/shard_map/all_to_all | solution.py:263
  87.5 1.1 %finish.1 = f32[8,1024]{1,0:T(8,128)} custom-call(s32[1]{0:T(128)} %bitcast.me_ref, s16[64,8,1024]{2,1,0:T(8,128)(2,1)S(1)} %all_to_all.17.got_ref), custom_call_target="tpu_custom_call" | custom-call | tf_op jit(solution)/shard_map/finish/pallas_call | solution.py:229
  (1 shorter events, 0.0 us)
Async XLA Ops:
  0.0 16.3 %slice-start = ((s8[8388608]{0:T(1024)(128)(4,1)}), s8[4194304]{0:T(1024)(128)(4,1)S(1)}, s32[]{:S(2)}) async-start(s8[8388608]{0:T(1024)(128)(4,1)} %bitcast.4), calls=%async_computation.3 | async-start | bytes 8388608
  0.0 16.3 %slice-start.1 = ((s8[8388608]{0:T(1024)(128)(4,1)}), s8[4194304]{0:T(1024)(128)(4,1)S(1)}, s32[]{:S(2)}) async-start(s8[8388608]{0:T(1024)(128)(4,1)} %bitcast.4), calls=%async_computation.4 | async-start | bytes 8388608
  0.0 16.3 %copy-start = (s32[1,1,16]{2,1,0:T(1,128)S(1)}, s32[1,1,16]{2,1,0:T(1,128)}, u32[]{:S(2)}) copy-start(s32[1,1,16]{2,1,0:T(1,128)} %param.5) | copy-start | bytes 196
  14.7 1.5 %collective-permute-start = (bf16[8,64,256]{2,1,0:T(8,128)(2,1)S(1)}, bf16[8,64,256]{2,1,0:T(8,128)(2,1)S(1)}, u32[]{:S(2)}, u32[]{:S(2)}) collective-permute-start(bf16[8,64,256]{2,1,0:T(8,128)(2,1)S(1)} %all_to_all.15.mine_ref), channel_id=1, source_target_pairs={{0,1},{1,0},{2,3},{3,2},{4,5},{5,4},{6,7},{7,6},{8,9},{9,8},{10,11... | collective-permute-start | bytes 786440 | tf_op jit(solution)/shard_map/ppermute | solution.py:250
  20.1 37.9 %copy-start.1 = (bf16[512,512]{1,0:T(8,128)(2,1)S(1)}, bf16[512,512]{1,0:T(8,128)(2,1)}, u32[]{:S(2)}) copy-start(bf16[512,512]{1,0:T(8,128)(2,1)} %metric_ref.3) | copy-start | bytes 1572868
  60.4 2.4 %collective-permute-start.1 = (s16[256,1152]{1,0:T(8,128)(2,1)S(1)}, s16[256,1152]{1,0:T(8,128)(2,1)S(1)}, u32[]{:S(2)}, u32[]{:S(2)}) collective-permute-start(s16[256,1152]{1,0:T(8,128)(2,1)S(1)} %get-tuple-element.15), channel_id=1, source_target_pairs={{0,1},{1,0},{2,3},{3,2},{4,5},{5,4},{6,7},{7,6},{8,9},{9,8},{10,11... | collective-permute-start | bytes 1769480 | tf_op jit(solution)/shard_map/ppermute | solution.py:258
  60.5 2.8 %collective-permute-start.2 = (s16[256,1152]{1,0:T(8,128)(2,1)S(1)}, s16[256,1152]{1,0:T(8,128)(2,1)S(1)}, u32[]{:S(2)}, u32[]{:S(2)}) collective-permute-start(s16[256,1152]{1,0:T(8,128)(2,1)S(1)} %get-tuple-element.16), channel_id=1, source_target_pairs={{0,1},{1,0},{2,3},{3,2},{4,5},{5,4},{6,7},{7,6},{8,9},{9,8},{10,11... | collective-permute-start | bytes 1769480 | tf_op jit(solution)/shard_map/ppermute | solution.py:258

commit v13 on v11

--- a/solution.py
+++ b/solution.py
@@ -20,15 +20,13 @@
     return pltpu.CompilerParams(vmem_limit_bytes=mib << 20)
 
 
-def copies_kernel(orbitals_ref, out_ref, sems):
-    copies = [
-        pltpu.make_async_copy(orbitals_ref, out_ref.at[i], sems.at[i])
-        for i in range(out_ref.shape[0])
-    ]
-    for copy in copies:
-        copy.start()
-    for copy in copies:
-        copy.wait()
+def copies_kernel(orbitals_ref, out_ref, held, sem):
+    copy = pltpu.make_async_copy(orbitals_ref, held, sem)
+    copy.start()
+    copy.wait()
+    value = held[...]
+    for i in range(out_ref.shape[0]):
+        out_ref[i] = value
 
 
 def copies_of(orbitals, count):
@@ -36,8 +34,8 @@
         copies_kernel,
         out_shape=jax.ShapeDtypeStruct((count, *orbitals.shape), BF16),
         in_specs=[pl.BlockSpec(memory_space=pl.ANY)],
-        out_specs=pl.BlockSpec(memory_space=pl.ANY),
-        scratch_shapes=[pltpu.SemaphoreType.DMA((count,))],
+        out_specs=VMEM,
+        scratch_shapes=[pltpu.VMEM(orbitals.shape, BF16), pltpu.SemaphoreType.DMA],
         compiler_params=params(8),
         cost_estimate=pl.CostEstimate(flops=10**10, bytes_accessed=40 << 20, transcendentals=0),
         name="copies",

time: 88.8 us -> 88.6 us (level)
  no operation moved by 1% of the time
where the time goes in v13:
time: 88.6 us; the launch traced here: 88.4 us
  blocking collectives  74.7 us (84%)
  Pallas kernels  11.1 us (13%)
  waiting for transfers between devices  2.52 us (3%)
    all_to_all x1, blocking collectives, body(): coef = lax.all_to_all(parts, BOTH, 0, 0, tiled=True)  37.9 us
    all_to_all x1, blocking collectives, body(): got = lax.all_to_all(parts, BOTH, 0, 0, tiled=True, axis_index_groups=sides)  23.2 us
    all_to_all x1, blocking collectives, body(): lax.all_to_all(copies, 'narrow', 0, 0, tiled=True, axis_index_groups=sides)  13.6 us
    pallas_call x2, Pallas kernels, term_call(): pl.pallas_call(kernel, out_shape=out_shape, in_specs=[SMEM, VMEM, VMEM],...  4.25 us
    pallas_call x1, Pallas kernels, coeffs_of(): pl.pallas_call(functools.partial(coeffs_kernel, step), out_shape=jax.Shap...  3.84 us
  transfers between devices with their start and end apart: 2, of which 2 were waited for; matrix products, arithmetic and copies ran while one was open for 0% of the time, Pallas kernels for 2%

profile of v13, /device:TPU:0, one launch (start us, length us, event | category | flops | bytes accessed | tf_op | source)
XLA Modules:
  0.0 88.4 jit_solution(13190891544488694511)
XLA Ops:
  0.0 0.0 slice-start
  0.0 0.0 slice-start.1
  0.0 0.0 copy-start
  0.0 0.9 %copies.1 = bf16[8,64,256]{2,1,0:T(8,128)(2,1)S(1)} custom-call(bf16[64,256]{1,0:T(8,128)(2,1)} %orbitals_ref), custom_call_target="tpu_custom_call" | custom-call | flops 10000000000 | bytes 41943040 | tf_op jit(solution)/shard_map/copies/pallas_call | solution.py:33
  0.9 13.6 %all_to_all.15.mine_ref = bf16[8,64,256]{2,1,0:T(8,128)(2,1)S(1)} all-to-all(bf16[8,64,256]{2,1,0:T(8,128)(2,1)S(1)} %copies.1), channel_id=1, replica_groups={{0,2,4,6,8,10,12,14},{1,3,5,7,9,11,13,15},{16,18,20,22,24,26,28,30},{17..., dimensions={0} | all-to-all | bytes 524288 | tf_op jit(solution)/shard_map/all_to_all | solution.py:241
  14.6 0.0 collective-permute-start
  14.6 1.5 %collective-permute-done.other_ref = bf16[8,64,256]{2,1,0:T(8,128)(2,1)S(1)} collective-permute-done((bf16[8,64,256]{2,1,0:T(8,128)(2,1)S(1)}, bf16[8,64,256]{2,1,0:T(8,128)(2,1)S(1)}, u32[]{:S(2)}, u32[]{:S(2)}) %collective-permute-start) | collective-permute-done | bytes 262176 | tf_op jit(solution)/shard_map/ppermute | solution.py:242
  16.1 0.0 slice-done
  16.1 0.0 slice-done.1
  16.1 0.0 copy-done
  16.1 3.8 %coeffs.1 = bf16[128,64,128]{2,1,0:T(8,128)(2,1)S(1)} custom-call(s32[1]{0:T(128)} %bitcast.1.core_ref, s32[16]{0:T(128)S(1)} %bitcast.7, bf16[8,64,256]{2,1,0:T(8,128)(2,1)S(1)} %all_to_all.15.mine_ref, bf16[8,64,256]{2,1,0:T(8,128)(2,1)S(1)} %collective-permute-done.other_ref, bf16[64,64,1024]{2,1,0:T(8,128)(2,1)S(1)} %bitcast.5), custom_call_target="tpu_custom_call" | custom-call | flops 2147483648 | bytes 8388608 | tf_op jit(solution)/shard_map/coeffs/pallas_call | solution.py:74
  20.0 0.0 copy-start.1
  20.0 37.9 %all_to_all.16 = bf16[128,64,128]{2,1,0:T(8,128)(2,1)S(1)} all-to-all(bf16[128,64,128]{2,1,0:T(8,128)(2,1)S(1)} %coeffs.1), channel_id=1, replica_groups=mesh['wide'=8,'narrow'=16] {'wide','narrow'}, dimensions={0} | all-to-all | bytes 4194304 | tf_op jit(solution)/shard_map/all_to_all | solution.py:244
  57.9 0.0 copy-done.1
  57.9 2.4 %partner.1 = (bf16[1024,1024]{1,0:T(8,128)(2,1)S(1)}, s16[512,1152]{1,0:T(8,128)(2,1)S(1)}) custom-call(s32[1]{0:T(128)} %bitcast.1.core_ref, bf16[8,16,2,32,128]{4,3,2,1,0:T(8,128)(2,1)S(1)} %bitcast.6, bf16[512,512]{1,0:T(8,128)(2,1)S(1)} %copy-done.1), custom_call_target="tpu_custom_call" | custom-call | flops 1610612736 | bytes 6291456 | tf_op jit(solution)/shard_map/partner/pallas_call | solution.py:144
  60.3 0.1 collective-permute-start.1
  60.4 1.8 %own.1.sum_ref = f32[512,1024]{1,0:T(8,128)S(1)} custom-call(s32[1]{0:T(128)} %bitcast.1.core_ref, bf16[1024,1024]{1,0:T(8,128)(2,1)S(1)} %get-tuple-element.13.packed_ref, bf16[512,512]{1,0:T(8,128)(2,1)S(1)} %copy-done.1), custom_call_target="tpu_custom_call" | custom-call | flops 1610612736 | bytes 6291456 | tf_op jit(solution)/shard_map/own/pallas_call | solution.py:144
  62.2 1.0 %collective-permute-done.1.held = s16[512,1152]{1,0:T(8,128)(2,1)S(1)} collective-permute-done((s16[512,1152]{1,0:T(8,128)(2,1)S(1)}, s16[512,1152]{1,0:T(8,128)(2,1)S(1)}, u32[]{:S(2)}, u32[]{:S(2)}) %collective-permute-start.1) | collective-permute-done | bytes 1179680 | tf_op jit(solution)/shard_map/ppermute | solution.py:250
  63.2 0.9 %code.1 = s16[64,8,1024]{2,1,0:T(8,128)(2,1)S(1)} custom-call(s32[1]{0:T(128)} %bitcast.1.core_ref, f32[512,1024]{1,0:T(8,128)S(1)} %own.1.sum_ref, s16[512,1152]{1,0:T(8,128)(2,1)S(1)} %collective-permute-done.1.held), custom_call_target="tpu_custom_call" | custom-call | bytes 6291456 | tf_op jit(solution)/shard_map/code/pallas_call | solution.py:182
  64.2 23.2 %all_to_all.17.got_ref = s16[64,8,1024]{2,1,0:T(8,128)(2,1)S(1)} all-to-all(s16[64,8,1024]{2,1,0:T(8,128)(2,1)S(1)} %code.1), channel_id=1, replica_groups={{0,2,4,6,8,10,12,14,16,18,20,22,24,26,28,30,32,34,36,38,40,42,44,46,48,..., dimensions={0} | all-to-all | bytes 2097152 | tf_op jit(solution)/shard_map/all_to_all | solution.py:255
  87.3 1.1 %finish.1 = f32[8,1024]{1,0:T(8,128)} custom-call(s32[1]{0:T(128)} %bitcast.me_ref, s16[64,8,1024]{2,1,0:T(8,128)(2,1)S(1)} %all_to_all.17.got_ref), custom_call_target="tpu_custom_call" | custom-call | tf_op jit(solution)/shard_map/finish/pallas_call | solution.py:221
  (1 shorter events, 0.0 us)
Async XLA Ops:
  0.0 16.1 %slice-start = ((s8[8388608]{0:T(1024)(128)(4,1)}), s8[4194304]{0:T(1024)(128)(4,1)S(1)}, s32[]{:S(2)}) async-start(s8[8388608]{0:T(1024)(128)(4,1)} %bitcast.4), calls=%async_computation.3 | async-start | bytes 8388608
  0.0 16.1 %slice-start.1 = ((s8[8388608]{0:T(1024)(128)(4,1)}), s8[4194304]{0:T(1024)(128)(4,1)S(1)}, s32[]{:S(2)}) async-start(s8[8388608]{0:T(1024)(128)(4,1)} %bitcast.4), calls=%async_computation.4 | async-start | bytes 8388608
  0.0 16.1 %copy-start = (s32[1,1,16]{2,1,0:T(1,128)S(1)}, s32[1,1,16]{2,1,0:T(1,128)}, u32[]{:S(2)}) copy-start(s32[1,1,16]{2,1,0:T(1,128)} %param.5) | copy-start | bytes 196
  14.6 1.5 %collective-permute-start = (bf16[8,64,256]{2,1,0:T(8,128)(2,1)S(1)}, bf16[8,64,256]{2,1,0:T(8,128)(2,1)S(1)}, u32[]{:S(2)}, u32[]{:S(2)}) collective-permute-start(bf16[8,64,256]{2,1,0:T(8,128)(2,1)S(1)} %all_to_all.15.mine_ref), channel_id=1, source_target_pairs={{0,1},{1,0},{2,3},{3,2},{4,5},{5,4},{6,7},{7,6},{8,9},{9,8},{10,11... | collective-permute-start | bytes 786440 | tf_op jit(solution)/shard_map/ppermute | solution.py:242
  20.0 37.9 %copy-start.1 = (bf16[512,512]{1,0:T(8,128)(2,1)S(1)}, bf16[512,512]{1,0:T(8,128)(2,1)}, u32[]{:S(2)}) copy-start(bf16[512,512]{1,0:T(8,128)(2,1)} %metric_ref.3) | copy-start | bytes 1572868
  60.3 2.9 %collective-permute-start.1 = (s16[512,1152]{1,0:T(8,128)(2,1)S(1)}, s16[512,1152]{1,0:T(8,128)(2,1)S(1)}, u32[]{:S(2)}, u32[]{:S(2)}) collective-permute-start(s16[512,1152]{1,0:T(8,128)(2,1)S(1)} %get-tuple-element.14), channel_id=1, source_target_pairs={{0,1},{1,0},{2,3},{3,2},{4,5},{5,4},{6,7},{7,6},{8,9},{9,8},{10,11... | collective-permute-start | bytes 3538952 | tf_op jit(solution)/shard_map/ppermute | solution.py:250

commit v14 on v13

--- a/solution.py
+++ b/solution.py
@@ -203,10 +203,10 @@
     other = jnp.sum(jnp.where(lane == at + 1, window, 0.0), axis=2, keepdims=True)
     code = jnp.where(row[:, :, :1] == 0, other[:, rows - 1 :], code)
     factor = jnp.exp2(code * (1.0 / 256.0)) * (-1.0 / TOP)
-    total = jnp.zeros((rows, columns), F32)
+    sums = [jnp.zeros((rows, columns), F32) for _ in range(4)]
     for s in range(blocks):
-        total += got_ref[s].astype(jnp.int32).astype(F32) * factor[s]
-    out_ref[...] = total
+        sums[s % 4] += got_ref[s].astype(jnp.int32).astype(F32) * factor[s]
+    out_ref[...] = (sums[0] + sums[1]) + (sums[2] + sums[3])
     part = out_ref[:, pl.ds(base, lanes)]
     lane = lax.broadcasted_iota(jnp.int32, part.shape, 1) - at
     row = lax.broadcasted_iota(jnp.int32, part.shape, 0)

time: 88.6 us -> 88.6 us (level)
  no operation moved by 1% of the time
where the time goes in v14:
time: 88.6 us; the launch traced here: 88.5 us
  blocking collectives  74.7 us (84%)
  Pallas kernels  11.1 us (13%)
  waiting for transfers between devices  2.52 us (3%)
    all_to_all x1, blocking collectives, body(): coef = lax.all_to_all(parts, BOTH, 0, 0, tiled=True)  37.9 us
    all_to_all x1, blocking collectives, body(): got = lax.all_to_all(parts, BOTH, 0, 0, tiled=True, axis_index_groups=sides)  23.2 us
    all_to_all x1, blocking collectives, body(): lax.all_to_all(copies, 'narrow', 0, 0, tiled=True, axis_index_groups=sides)  13.6 us
    pallas_call x2, Pallas kernels, term_call(): pl.pallas_call(kernel, out_shape=out_shape, in_specs=[SMEM, VMEM, VMEM],...  4.25 us
    pallas_call x1, Pallas kernels, coeffs_of(): pl.pallas_call(functools.partial(coeffs_kernel, step), out_shape=jax.Shap...  3.84 us
  transfers between devices with their start and end apart: 2, of which 2 were waited for; matrix products, arithmetic and copies ran while one was open for 0% of the time, Pallas kernels for 2%

profile of v14, /device:TPU:0, one launch (start us, length us, event | category | flops | bytes accessed | tf_op | source)
XLA Modules:
  0.0 88.5 jit_solution(16172215549200957062)
XLA Ops:
  0.0 0.0 slice-start
  0.0 0.0 slice-start.1
  0.0 0.0 copy-start
  0.0 0.9 %copies.1 = bf16[8,64,256]{2,1,0:T(8,128)(2,1)S(1)} custom-call(bf16[64,256]{1,0:T(8,128)(2,1)} %orbitals_ref), custom_call_target="tpu_custom_call" | custom-call | flops 10000000000 | bytes 41943040 | tf_op jit(solution)/shard_map/copies/pallas_call | solution.py:33
  0.9 13.6 %all_to_all.15.mine_ref = bf16[8,64,256]{2,1,0:T(8,128)(2,1)S(1)} all-to-all(bf16[8,64,256]{2,1,0:T(8,128)(2,1)S(1)} %copies.1), channel_id=1, replica_groups={{0,2,4,6,8,10,12,14},{1,3,5,7,9,11,13,15},{16,18,20,22,24,26,28,30},{17..., dimensions={0} | all-to-all | bytes 524288 | tf_op jit(solution)/shard_map/all_to_all | solution.py:241
  14.6 0.0 collective-permute-start
  14.6 1.5 %collective-permute-done.other_ref = bf16[8,64,256]{2,1,0:T(8,128)(2,1)S(1)} collective-permute-done((bf16[8,64,256]{2,1,0:T(8,128)(2,1)S(1)}, bf16[8,64,256]{2,1,0:T(8,128)(2,1)S(1)}, u32[]{:S(2)}, u32[]{:S(2)}) %collective-permute-start) | collective-permute-done | bytes 262176 | tf_op jit(solution)/shard_map/ppermute | solution.py:242
  16.1 0.0 slice-done
  16.1 0.0 slice-done.1
  16.1 0.0 copy-done
  16.1 3.8 %coeffs.1 = bf16[128,64,128]{2,1,0:T(8,128)(2,1)S(1)} custom-call(s32[1]{0:T(128)} %bitcast.1.core_ref, s32[16]{0:T(128)S(1)} %bitcast.7, bf16[8,64,256]{2,1,0:T(8,128)(2,1)S(1)} %all_to_all.15.mine_ref, bf16[8,64,256]{2,1,0:T(8,128)(2,1)S(1)} %collective-permute-done.other_ref, bf16[64,64,1024]{2,1,0:T(8,128)(2,1)S(1)} %bitcast.5), custom_call_target="tpu_custom_call" | custom-call | flops 2147483648 | bytes 8388608 | tf_op jit(solution)/shard_map/coeffs/pallas_call | solution.py:74
  20.0 0.0 copy-start.1
  20.0 37.9 %all_to_all.16 = bf16[128,64,128]{2,1,0:T(8,128)(2,1)S(1)} all-to-all(bf16[128,64,128]{2,1,0:T(8,128)(2,1)S(1)} %coeffs.1), channel_id=1, replica_groups=mesh['wide'=8,'narrow'=16] {'wide','narrow'}, dimensions={0} | all-to-all | bytes 4194304 | tf_op jit(solution)/shard_map/all_to_all | solution.py:244
  57.9 0.0 copy-done.1
  57.9 2.4 %partner.1 = (bf16[1024,1024]{1,0:T(8,128)(2,1)S(1)}, s16[512,1152]{1,0:T(8,128)(2,1)S(1)}) custom-call(s32[1]{0:T(128)} %bitcast.1.core_ref, bf16[8,16,2,32,128]{4,3,2,1,0:T(8,128)(2,1)S(1)} %bitcast.6, bf16[512,512]{1,0:T(8,128)(2,1)S(1)} %copy-done.1), custom_call_target="tpu_custom_call" | custom-call | flops 1610612736 | bytes 6291456 | tf_op jit(solution)/shard_map/partner/pallas_call | solution.py:144
  60.3 0.1 collective-permute-start.1
  60.4 1.8 %own.1.sum_ref = f32[512,1024]{1,0:T(8,128)S(1)} custom-call(s32[1]{0:T(128)} %bitcast.1.core_ref, bf16[1024,1024]{1,0:T(8,128)(2,1)S(1)} %get-tuple-element.13.packed_ref, bf16[512,512]{1,0:T(8,128)(2,1)S(1)} %copy-done.1), custom_call_target="tpu_custom_call" | custom-call | flops 1610612736 | bytes 6291456 | tf_op jit(solution)/shard_map/own/pallas_call | solution.py:144
  62.2 1.0 %collective-permute-done.1.held = s16[512,1152]{1,0:T(8,128)(2,1)S(1)} collective-permute-done((s16[512,1152]{1,0:T(8,128)(2,1)S(1)}, s16[512,1152]{1,0:T(8,128)(2,1)S(1)}, u32[]{:S(2)}, u32[]{:S(2)}) %collective-permute-start.1) | collective-permute-done | bytes 1179680 | tf_op jit(solution)/shard_map/ppermute | solution.py:250
  63.2 0.9 %code.1 = s16[64,8,1024]{2,1,0:T(8,128)(2,1)S(1)} custom-call(s32[1]{0:T(128)} %bitcast.1.core_ref, f32[512,1024]{1,0:T(8,128)S(1)} %own.1.sum_ref, s16[512,1152]{1,0:T(8,128)(2,1)S(1)} %collective-permute-done.1.held), custom_call_target="tpu_custom_call" | custom-call | bytes 6291456 | tf_op jit(solution)/shard_map/code/pallas_call | solution.py:182
  64.2 23.2 %all_to_all.17.got_ref = s16[64,8,1024]{2,1,0:T(8,128)(2,1)S(1)} all-to-all(s16[64,8,1024]{2,1,0:T(8,128)(2,1)S(1)} %code.1), channel_id=1, replica_groups={{0,2,4,6,8,10,12,14,16,18,20,22,24,26,28,30,32,34,36,38,40,42,44,46,48,..., dimensions={0} | all-to-all | bytes 2097152 | tf_op jit(solution)/shard_map/all_to_all | solution.py:255
  87.3 1.1 %finish.1 = f32[8,1024]{1,0:T(8,128)} custom-call(s32[1]{0:T(128)} %bitcast.me_ref, s16[64,8,1024]{2,1,0:T(8,128)(2,1)S(1)} %all_to_all.17.got_ref), custom_call_target="tpu_custom_call" | custom-call | tf_op jit(solution)/shard_map/finish/pallas_call | solution.py:221
  (1 shorter events, 0.0 us)
Async XLA Ops:
  0.0 16.1 %slice-start = ((s8[8388608]{0:T(1024)(128)(4,1)}), s8[4194304]{0:T(1024)(128)(4,1)S(1)}, s32[]{:S(2)}) async-start(s8[8388608]{0:T(1024)(128)(4,1)} %bitcast.4), calls=%async_computation.3 | async-start | bytes 8388608
  0.0 16.1 %slice-start.1 = ((s8[8388608]{0:T(1024)(128)(4,1)}), s8[4194304]{0:T(1024)(128)(4,1)S(1)}, s32[]{:S(2)}) async-start(s8[8388608]{0:T(1024)(128)(4,1)} %bitcast.4), calls=%async_computation.4 | async-start | bytes 8388608
  0.0 16.1 %copy-start = (s32[1,1,16]{2,1,0:T(1,128)S(1)}, s32[1,1,16]{2,1,0:T(1,128)}, u32[]{:S(2)}) copy-start(s32[1,1,16]{2,1,0:T(1,128)} %param.5) | copy-start | bytes 196
  14.6 1.5 %collective-permute-start = (bf16[8,64,256]{2,1,0:T(8,128)(2,1)S(1)}, bf16[8,64,256]{2,1,0:T(8,128)(2,1)S(1)}, u32[]{:S(2)}, u32[]{:S(2)}) collective-permute-start(bf16[8,64,256]{2,1,0:T(8,128)(2,1)S(1)} %all_to_all.15.mine_ref), channel_id=1, source_target_pairs={{0,1},{1,0},{2,3},{3,2},{4,5},{5,4},{6,7},{7,6},{8,9},{9,8},{10,11... | collective-permute-start | bytes 786440 | tf_op jit(solution)/shard_map/ppermute | solution.py:242
  20.0 37.9 %copy-start.1 = (bf16[512,512]{1,0:T(8,128)(2,1)S(1)}, bf16[512,512]{1,0:T(8,128)(2,1)}, u32[]{:S(2)}) copy-start(bf16[512,512]{1,0:T(8,128)(2,1)} %metric_ref.3) | copy-start | bytes 1572868
  60.3 2.9 %collective-permute-start.1 = (s16[512,1152]{1,0:T(8,128)(2,1)S(1)}, s16[512,1152]{1,0:T(8,128)(2,1)S(1)}, u32[]{:S(2)}, u32[]{:S(2)}) collective-permute-start(s16[512,1152]{1,0:T(8,128)(2,1)S(1)} %get-tuple-element.14), channel_id=1, source_target_pairs={{0,1},{1,0},{2,3},{3,2},{4,5},{5,4},{6,7},{7,6},{8,9},{9,8},{10,11... | collective-permute-start | bytes 3538952 | tf_op jit(solution)/shard_map/ppermute | solution.py:250
